TPU v7x, 32 devices: a whole 2x2x4 slice. The times are simulated.
32 devices in a mesh: groups: 2 (over x), mesh: 16 (over z, y, core).
Axes of the slice: x: 2, y: 2, z: 4, core: 2. Of those that a mesh axis runs over, the one named last changes fastest.
Arguments:
- water_depth: float32 [768, 10, 640], P(('groups', 'mesh')), parts along dimension 0, may hold values from 1 to 3
- momentum: float32 [768, 2, 10, 640], P(('groups', 'mesh')), parts along dimension 0, may hold values from -3 to 3
- metric: float32 [768, 4, 64], P(('groups', 'mesh')), parts along dimension 0, may hold values from -2 to 2
- face_scale: float32 [768, 192], P(('groups', 'mesh')), parts along dimension 0, may hold values from 0.5 to 2
- face_angle: float32 [768, 192], P(('groups', 'mesh')), parts along dimension 0, may hold values from -3.140625 to 3.140625
- face_map: int32 [768, 192], P(('groups', 'mesh')), parts along dimension 0, may hold values from 0 to 4735, as said below
- rim_faces: int32 [32, 128], P(('groups', 'mesh')), parts along dimension 0, may hold values from 0 to 4607, as said below
- wet_blocks: int32 [768], P(('groups', 'mesh')), parts along dimension 0, may hold values from 0 to 1, as said below
- breach: int32 [768, 10], P(('groups', 'mesh')), parts along dimension 0, may hold values from 0 to 3
- block_plan: int32 [768], P('groups'), parts along dimension 0, may hold values from 0 to 383, as said below
Outputs:
- depth_out: float32 [768, 10, 640], P(('groups', 'mesh')), parts along dimension 0
- momentum_out: float32 [768, 2, 10, 640], P(('groups', 'mesh')), parts along dimension 0
There are 2 independent parts, one for each index of `groups`. A program takes and returns all parts, laid end to end along the dimension named above; each array names one. Nothing has to cross between parts.
Inputs may be any that keep to these rules, and one draw needn't show every extreme that they name: `face_map`: The rim entries pair in order: entry i of index d's second half of rim_faces with entry i of index d + 1's first half. No face of the first index names a previous index, none of the last a next one. `rim_faces`: each row holds 128 distinct local face numbers. `wet_blocks`: every block of mesh index 0 is 1; the chance of a 1 falls along the mesh axis. `block_plan`: A permutation of the block slots. Each mesh index hands exactly 8 of its blocks to other indices, each to a different index, and receives exactly 8, each from a different index, into the slots it vacates; the other blocks stay.
All inputs are finite; a program needn't handle non-finite values.
Results may differ from a plain program's by a relative error of at most 0.000059.
Values sent between devices are 32-bit elements; how exact they have to be, the bound alone decides.
No kernel may reach another device: no remote copies, remote signals or barrier semaphores. Data moves between devices by JAX's collectives and lax.ppermute only.
A program may use at most 192 MiB of HBM per device.

v0:
```python
import functools
import math

import jax
import jax.numpy as jnp
import numpy as np
from jax import lax
from jax.experimental import pallas as pl
from jax.experimental.pallas import tpu as pltpu
from jax.sharding import PartitionSpec as P

time_step = 0.01
gravity = 1.0
breach_rate = 5.0
LANES = 128


def gauss_solve(matrix, right):
    dimension = matrix.shape[0]
    augmented = np.concatenate([np.array(matrix) * 1.0, np.array(right) * 1.0], axis=1)
    for pivot_col in range(dimension):
        largest = pivot_col + int(np.argmax(np.abs(augmented[pivot_col:, pivot_col])))
        swapped = augmented[[largest, pivot_col]]
        augmented[[pivot_col, largest]] = swapped
        augmented[pivot_col] = augmented[pivot_col] / augmented[pivot_col, pivot_col]
        for row_id in range(dimension):
            if row_id != pivot_col:
                augmented[row_id] = (
                    augmented[row_id] - augmented[row_id, pivot_col] * augmented[pivot_col]
                )
    return augmented[:, dimension:]


def node_tables():
    points = np.array(
        [(across / 3.0, upward / 3.0) for upward in range(4) for across in range(4 - upward)]
    )
    powers = [(power_r, power_s) for power_r in range(4) for power_s in range(4 - power_r)]
    vander = np.zeros((10, 10))
    grad_r = np.zeros((10, 10))
    grad_s = np.zeros((10, 10))
    mono_mass = np.zeros((10, 10))
    for column, (power_r, power_s) in enumerate(powers):
        vander[:, column] = points[:, 0] ** power_r * points[:, 1] ** power_s
        if power_r > 0:
            grad_r[:, column] = power_r * points[:, 0] ** (power_r - 1) * points[:, 1] ** power_s
        if power_s > 0:
            grad_s[:, column] = power_s * points[:, 0] ** power_r * points[:, 1] ** (power_s - 1)
        for second_column, (other_r, other_s) in enumerate(powers):
            mono_mass[column, second_column] = (
                math.factorial(power_r + other_r)
                * math.factorial(power_s + other_s)
                / math.factorial(power_r + other_r + power_s + other_s + 2)
            )
    inverse = gauss_solve(vander, np.eye(10))
    mass_matrix = inverse.T @ mono_mass @ inverse
    line_points = np.arange(4) / 3.0
    line_vander = line_points[:, None] ** np.arange(4)[None, :]
    hilbert = 1.0 / (np.arange(4)[:, None] + np.arange(4)[None, :] + 1.0)
    line_inverse = gauss_solve(line_vander, np.eye(4))
    edge_mass = line_inverse.T @ hilbert @ line_inverse
    face_nodes = np.array([[0, 1, 2, 3], [3, 6, 8, 9], [9, 7, 4, 0]])
    edge_embed = np.zeros((10, 12))
    for face_id in range(3):
        for node_id in range(4):
            edge_embed[face_nodes[face_id, node_id], 4 * face_id : 4 * face_id + 4] += edge_mass[
                node_id
            ]
    lifting = gauss_solve(mass_matrix, edge_embed).reshape(10, 3, 4)
    return (
        np.asarray(grad_r @ inverse, np.float32),
        np.asarray(grad_s @ inverse, np.float32),
        np.asarray(lifting, np.float32),
        face_nodes.reshape(-1),
    )


def round_up(value, step):
    return (value + step - 1) // step * step


def static_tables(members, elements):
    deriv_r, deriv_s, lifting, face_order = node_tables()
    nodes = deriv_r.shape[0]
    pairs = nodes // 2
    used = members * pairs
    comp = round_up(used, 8)
    face_nodes = face_order.reshape(3, 4)
    wide = members * 4

    def lane_of(s, n):
        return (n % 2) * comp + s * pairs + n // 2

    own = np.zeros((LANES, LANES), np.float32)
    back = np.zeros((LANES, LANES), np.float32)
    lift = np.zeros((2 * comp, LANES), np.float32)
    along = np.zeros((2, 2 * comp, LANES), np.float32)
    for s in range(members):
        for f in range(3):
            for k in range(4):
                n = int(face_nodes[f, k])
                own[lane_of(s, n), f * wide + s * 4 + k] = 1.0
                back[lane_of(s, n), f * wide + s * 4 + 3 - k] = 1.0
        for n in range(nodes):
            for f in range(3):
                for k in range(4):
                    lift[lane_of(s, n), f * wide + s * 4 + k] = lifting[n, f, k]
            for m in range(nodes):
                along[0, lane_of(s, n), lane_of(s, m)] = -deriv_r[n, m]
                along[1, lane_of(s, n), lane_of(s, m)] = -deriv_s[n, m]
            along[0, lane_of(s, n), 2 * comp + s] = breach_rate
    spread = np.zeros((16, 8 * LANES), np.float32)
    for q in range(4):
        for f in range(3):
            spread[3 * q + f, q * LANES + f * wide : q * LANES + (f + 1) * wide] = 1.0
        spread[12 + q, (4 + q) * LANES : (5 + q) * LANES] = 1.0
    return dict(
        own=own, back=back, lift=lift, along=along, spread=spread,
        comp=comp, pairs=pairs, used=used, wide=wide, nodes=nodes, members=members,
    )


def high_low(matrix):
    high = matrix.astype(jnp.bfloat16)
    low = (matrix - high.astype(np.float32)).astype(jnp.bfloat16)
    return high, low


def mm(a, b, dims=((1,), (0,))):
    return lax.dot_general(a, b, (dims, ((), ())), preferred_element_type=jnp.float32)


def split(x):
    high = x.astype(jnp.bfloat16)
    return high, (x - high.astype(jnp.float32)).astype(jnp.bfloat16)


def swap_halves(x):
    return pltpu.roll(x, LANES // 2, 1)


def turn_pair(fields, first, second, turned, halves, comp):
    lower = lax.broadcasted_iota(jnp.int32, (comp, LANES), 1) < LANES // 2
    for c in range(3):
        a = fields[first, c * comp : (c + 1) * comp]
        b = fields[second, c * comp : (c + 1) * comp]
        even = jnp.where(lower, a, swap_halves(b))
        odd = jnp.where(lower, swap_halves(a), b)
        fill = jnp.full((LANES - 2 * comp, LANES), 1.0 if c == 0 else 0.0, jnp.float32)
        flat = jnp.concatenate([even, odd, fill], axis=0).T
        if turned is not None:
            turned[c] = flat
        high, low = split(flat)
        halves[c * LANES : (c + 1) * LANES, :LANES] = high
        halves[c * LANES : (c + 1) * LANES, LANES:] = low


def place_face(pieces, c, wide, lane):
    moved = [pltpu.roll(p, ((i - c) * wide) % LANES, 1) if i != c else p for i, p in enumerate(pieces)]
    return jnp.where(lane < wide, moved[0], jnp.where(lane < 2 * wide, moved[1], moved[2]))


def start_all(copies):
    for copy in copies:
        copy.start()
    return copies


def wait_all(copies):
    for copy in copies:
        copy.wait()


def prepare_kernel(
    rim, depth_in, flow_in, back_in, fields_out, pool_out, head, tail,
    depth, flow, back, fields, pool, halves, sems, *, t, blocks, elements,
):
    comp, pairs, members, wide = t["comp"], t["pairs"], t["members"], t["wide"]
    tiles = blocks // 8
    group = 8 * 3 * elements
    first = start_all(
        [pltpu.make_async_copy(depth_in, depth, sems.at[0]), pltpu.make_async_copy(back_in, back, sems.at[1])]
    )
    flows = start_all(
        [
            pltpu.make_async_copy(flow_in.at[pl.ds(8 * i, 8)], flow.at[pl.ds(8 * i, 8)], sems.at[2 + i])
            for i in range(tiles)
        ]
    )
    wait_all(first)
    outs = []
    filled = members * pairs
    for tile in range(tiles):
        flows[tile].wait()

        def rows_of(sub, carry):
            b = tile * 8 + sub
            for c in range(3):
                end = comp * (c + 1)
                fields[b, end - 8 : end] = jnp.full((8, LANES), 1.0 if c == 0 else 0.0, jnp.float32)
            for s in range(members):
                start = (s * tiles + tile) * pairs * 8 + sub
                fields[b, s * pairs : (s + 1) * pairs] = depth[pl.ds(start, pairs, stride=8), :]
                for j in range(pairs):
                    two = flow[b, s, :, j * LANES : (j + 1) * LANES]
                    row = s * pairs + j
                    fields[b, comp + row : comp + row + 1] = two[0:1]
                    fields[b, 2 * comp + row : 2 * comp + row + 1] = two[1:2]
            return carry

        lax.fori_loop(0, 8, rows_of, 0)

        def faces_of(i, carry):
            b = tile * 8 + 2 * i
            turn_pair(fields, b, b + 1, None, halves, comp)
            rows = mm(halves[...], back[...])
            lane = lax.broadcasted_iota(jnp.int32, (LANES, LANES), 1)
            pieces = [rows[c * LANES : (c + 1) * LANES] for c in range(3)]
            for f in range(3):
                face = place_face(pieces, f, wide, lane)
                for u in range(2):
                    pool[pl.ds(((b + u) * 3 + f) * elements, elements), :] = face[u * elements : (u + 1) * elements]
            return carry

        lax.fori_loop(0, 4, faces_of, 0)
        outs += start_all(
            [
                pltpu.make_async_copy(
                    fields.at[pl.ds(8 * tile, 8)], fields_out.at[pl.ds(8 * tile, 8)], sems.at[2 + tiles + 2 * tile]
                ),
                pltpu.make_async_copy(
                    pool.at[pl.ds(group * tile, group)], pool_out.at[pl.ds(group * tile, group)],
                    sems.at[3 + tiles + 2 * tile],
                ),
            ]
        )
    width = head.shape[0]

    def pick(i, carry):
        for u in range(16):
            r = i * 16 + u
            head[pl.ds(r, 1), :] = pool[pl.ds(rim[r], 1), :]
            tail[pl.ds(r, 1), :] = pool[pl.ds(rim[width + r], 1), :]
        return carry

    lax.fori_loop(0, width // 16, pick, 0)
    wait_all(outs)


def finish_kernel(
    order, place, count, links, wet,
    fields_in, pool_in, before_in, after_in, coefs_in, inflow_in, own_in, spread_in, matrix_in, low_in,
    *rest, t, blocks, elements, leaving,
):
    outs, scratch = (rest[:1], rest[1:]) if leaving else (rest[:2], rest[2:])
    fields, pool, coefs, inflow, own, spread, matrix, low, turned, halves, traces, factors, outer, pieces, *scratch = scratch
    staged, sems = scratch[0], scratch[-1]
    comp, pairs, members, wide, used = t["comp"], t["pairs"], t["members"], t["wide"], t["used"]
    faces = blocks * 3 * elements
    width = before_in.shape[0]
    loads = [
        (fields_in, fields), (pool_in, pool.at[pl.ds(0, faces)]), (before_in, pool.at[pl.ds(faces, width)]),
        (after_in, pool.at[pl.ds(faces + width, width)]), (coefs_in, coefs), (inflow_in, inflow), (own_in, own),
        (spread_in, spread), (matrix_in, matrix), (low_in, low),
    ]
    wait_all(start_all([pltpu.make_async_copy(a, b, sems.at[i]) for i, (a, b) in enumerate(loads)]))
    n_loads = len(loads)
    begin = 0 if leaving else count[0]
    end = count[0] if leaving else blocks
    step = 32
    chunks = [slice(i * step, (i + 1) * step) for i in range(LANES // step)]

    def one(i, carry):
        at = (begin + 2 * i, jnp.minimum(begin + 2 * i + 1, end - 1))
        both = (order[at[0]], order[at[1]])

        for u in range(2):
            base = both[u] * (3 * elements)
            for f in range(3):

                def pick(r, carry):
                    for w in range(32):
                        e = r * 32 + w
                        v = links[base + f * elements + e]
                        outer[pl.ds(f * LANES + u * elements + e, 1), :] = pool[pl.ds(v, 1), :]
                    return carry

                lax.fori_loop(0, elements // 32, pick, 0)

        turn_pair(fields, both[0], both[1], turned, halves, comp)
        inner = mm(halves[...], own[...])
        for c in range(3):
            traces[c] = inner[c * LANES : (c + 1) * LANES]
        lower = lax.broadcasted_iota(jnp.int32, (16, LANES), 1) < elements
        values = jnp.where(lower, coefs[both[0]], coefs[both[1]])
        rough = values.astype(jnp.bfloat16).astype(jnp.float32)
        stacked = jnp.concatenate([rough, values - rough], axis=0).T.astype(jnp.bfloat16)
        factors[...] = mm(stacked, spread[...])

        lane = lax.broadcasted_iota(jnp.int32, (step, LANES), 1)
        for rows in chunks:
            n_x, n_y, scale, wall, rx, sx, ry, sy = (
                factors[rows, q * LANES : (q + 1) * LANES] for q in range(8)
            )
            height, flow_x, flow_y = (turned[c, rows] for c in range(3))
            pressure = 0.5 * gravity * height * height
            inverse = 1.0 / height
            speed_x = flow_x * inverse
            speed_y = flow_y * inverse
            cross = flow_y * speed_x
            flux_f = (flow_x, flow_x * speed_x + pressure, cross)
            flux_g = (flow_y, cross, flow_y * speed_y + pressure)
            add = inflow[pl.ds(both[0] if rows.start < elements else both[1], 1), :]
            for c in range(3):
                along_r = rx * flux_f[c] + ry * flux_g[c]
                along_s = sx * flux_f[c] + sy * flux_g[c]
                along_r = jnp.where(lane < 2 * comp, along_r, add if c == 0 else 0.0)
                pieces[c, rows, 0:LANES], pieces[c, rows, LANES : 2 * LANES] = split(along_r)
                pieces[c, rows, 2 * LANES : 3 * LANES], pieces[c, rows, 3 * LANES : 4 * LANES] = split(along_s)

            live = lane < 3 * wide
            theirs = [outer[f * LANES + rows.start : f * LANES + rows.stop] for f in range(3)]
            height = jnp.where(live, traces[0, rows], 1.0)
            flow_x, flow_y = traces[1, rows], traces[2, rows]
            is_wall = wall > 0.5
            through = flow_x * n_x + flow_y * n_y
            height_o = jnp.where(live, jnp.where(is_wall, height, place_face(theirs, 0, wide, lane)), 1.0)
            flow_xo = jnp.where(is_wall, flow_x - 2.0 * through * n_x, place_face(theirs, 1, wide, lane))
            flow_yo = jnp.where(is_wall, flow_y - 2.0 * through * n_y, place_face(theirs, 2, wide, lane))
            through_o = flow_xo * n_x + flow_yo * n_y
            speed = through / height
            speed_o = through_o / height_o
            fast = jnp.maximum(
                jnp.abs(speed) + jnp.sqrt(gravity * height), jnp.abs(speed_o) + jnp.sqrt(gravity * height_o)
            )
            push = 0.5 * gravity * (height * height - height_o * height_o)
            half = 0.5 * scale
            jumps = (
                half * (through - through_o + fast * (height_o - height)),
                half * (flow_x * speed - flow_xo * speed_o + push * n_x + fast * (flow_xo - flow_x)),
                half * (flow_y * speed - flow_yo * speed_o + push * n_y + fast * (flow_yo - flow_y)),
            )
            for c in range(3):
                jump = jnp.where(live, jumps[c], 0.0)
                pieces[c, rows, 4 * LANES : 5 * LANES], pieces[c, rows, 5 * LANES : 6 * LANES] = split(jump)

        rates = [time_step * wet[b].astype(jnp.float32) for b in both]
        last = ((1,), (1,))
        narrow = lax.broadcasted_iota(jnp.int32, (comp, LANES), 1) < elements
        for c in range(3):
            tall = mm(matrix[...], pieces[c], last) + mm(low[...], pieces[c, :, 4 * LANES : 5 * LANES], last)
            even, odd = tall[:comp], tall[comp:]
            gains = (jnp.where(narrow, even, swap_halves(odd)), jnp.where(narrow, swap_halves(even), odd))
            for u in range(2):
                done = fields[both[u], c * comp : (c + 1) * comp] + rates[u] * gains[u]
                if leaving:
                    staged[at[u], c * used : (c + 1) * used] = done[:used]
                else:
                    staged[u, c * comp : (c + 1) * comp] = done

        if leaving:
            for u in range(2):

                @pl.when(begin + 2 * i + u < end)
                def _():
                    pltpu.make_async_copy(
                        staged.at[at[u]], outs[0].at[place[both[u]]], sems.at[n_loads + at[u]]
                    ).start()
        else:
            for u in range(2):
                write_block(both[u], staged.at[u], comp, scratch[1], scratch[2], t, blocks)
        return carry

    lax.fori_loop(0, (end - begin + 1) // 2, one, 0)
    if leaving:

        def finish(i, carry):
            pltpu.make_async_copy(staged.at[i], outs[0].at[place[order[i]]], sems.at[n_loads + i]).wait()
            return carry

        lax.fori_loop(0, end, finish, 0)
    else:
        wait_all(
            start_all([pltpu.make_async_copy(scratch[1 + i], outs[i], sems.at[n_loads + i]) for i in range(2)])
        )


def write_block(b, rows, step, depth, flow, t, blocks):
    pairs, members = t["pairs"], t["members"]
    tile, sub = b // 8, b % 8
    for s in range(members):
        start = (s * (blocks // 8) + tile) * pairs * 8 + sub
        depth[pl.ds(start, pairs, stride=8), :] = rows[s * pairs : (s + 1) * pairs]
        for j in range(pairs):
            row = s * pairs + j
            flow[b, s, 0:1, j * LANES : (j + 1) * LANES] = rows[step + row : step + row + 1]
            flow[b, s, 1:2, j * LANES : (j + 1) * LANES] = rows[2 * step + row : 2 * step + row + 1]


def merge_kernel(source, arrives, got, depth_in, flow_in, depth_out, flow_out, depth, flow, came, sems, *, t, blocks):
    def arrival(b):
        return pltpu.make_async_copy(got.at[source[b]], came.at[b], sems.at[b])

    def leave(b):
        return pltpu.make_async_copy(flow.at[b], flow_out.at[b], sems.at[blocks + b])

    whole = pltpu.make_async_copy(depth_in, depth, sems.at[2 * blocks])
    whole.start()

    def each(act):
        def one(b, carry):
            @pl.when(arrives[b] == 1)
            def _():
                act(b)

            return carry

        lax.fori_loop(0, blocks, one, 0)

    each(lambda b: arrival(b).start())
    whole.wait()

    def put(b):
        arrival(b).wait()
        write_block(b, came.at[b], t["used"], depth, flow, t, blocks)
        leave(b).start()

    each(put)
    back = pltpu.make_async_copy(depth, depth_out, sems.at[2 * blocks])
    back.start()
    each(lambda b: leave(b).wait())
    back.wait()


SMEM = pl.BlockSpec(memory_space=pltpu.SMEM)
ANY = pl.BlockSpec(memory_space=pl.ANY)
VMEM = pl.BlockSpec(memory_space=pltpu.VMEM)


def call(kernel, out_shape, n_smem, n_args, scratch, out_specs, **keys):
    return pl.pallas_call(
        kernel,
        out_shape=out_shape,
        in_specs=[SMEM] * n_smem + [ANY] * n_args,
        out_specs=out_specs,
        scratch_shapes=scratch,
        compiler_params=pltpu.CompilerParams(vmem_limit_bytes=48 << 20),
        **keys,
    )


def body(
    water_depth, momentum, metric, face_scale, face_angle, face_map, rim_faces, wet_blocks, breach, block_plan
):
    blocks, members, node_cells = water_depth.shape
    elements = metric.shape[2]
    t = static_tables(members, elements)
    comp, pairs, used = t["comp"], t["pairs"], t["used"]
    f32, bf16 = jnp.float32, jnp.bfloat16
    tiles = blocks // 8
    depth_rows = water_depth.reshape(tiles, 8, members, pairs, LANES).transpose(2, 0, 3, 1, 4).reshape(-1, LANES)
    flow_rows = momentum.transpose(0, 2, 1, 3)
    links = face_map.reshape(-1)
    faces = links.shape[0]
    rim_list = rim_faces.reshape(-1)
    width = rim_list.shape[0] // 2
    dma = pltpu.SemaphoreType.DMA

    back = jnp.asarray(np.tile(t["back"], (2, 1)), bf16)
    fields, pool, head, tail = call(
        functools.partial(prepare_kernel, t=t, blocks=blocks, elements=elements),
        (
            jax.ShapeDtypeStruct((blocks, 3 * comp, LANES), f32),
            jax.ShapeDtypeStruct((faces, LANES), f32),
            jax.ShapeDtypeStruct((width, LANES), f32),
            jax.ShapeDtypeStruct((width, LANES), f32),
        ),
        1, 3,
        [
            pltpu.VMEM(depth_rows.shape, f32), pltpu.VMEM(flow_rows.shape, f32), pltpu.VMEM(back.shape, bf16),
            pltpu.VMEM((blocks, 3 * comp, LANES), f32), pltpu.VMEM((faces, LANES), f32),
            pltpu.VMEM((3 * LANES, 2 * LANES), bf16), dma((2 + 3 * tiles,)),
        ],
        (ANY, ANY, VMEM, VMEM),
    )(rim_list, depth_rows, flow_rows, back)

    count = lax.axis_size("mesh")
    before = lax.ppermute(tail, "mesh", [(i, i + 1) for i in range(count - 1)])
    after = lax.ppermute(head, "mesh", [(i + 1, i) for i in range(count - 1)])

    own_index = lax.axis_index("mesh")
    all_slots = block_plan.shape[0]
    local_ids = jnp.arange(blocks, dtype=jnp.int32)
    slot_ids = own_index * blocks + local_ids
    targets = lax.dynamic_slice_in_dim(block_plan, own_index * blocks, blocks)
    target_dev = targets // blocks
    leaves = (target_dev != own_index).astype(jnp.int32)
    every_slot = jnp.arange(all_slots, dtype=jnp.int32)
    source = jnp.sum(jnp.where(block_plan[None, :] == slot_ids[:, None], every_slot[None, :], 0), axis=1)
    source_dev = source // blocks
    arrives = (source_dev != own_index).astype(jnp.int32)
    n_leaving = jnp.sum(leaves)
    earlier = local_ids[None, :] < local_ids[:, None]
    rank_leave = jnp.sum(jnp.where(earlier, leaves[None, :], 0), axis=1)
    rank = jnp.where(leaves == 1, rank_leave, n_leaving + local_ids - rank_leave)
    order = jnp.sum(jnp.where(rank[None, :] == local_ids[:, None], local_ids[None, :], 0), axis=1)

    walls = (links == jnp.arange(faces, dtype=jnp.int32)).astype(f32).reshape(blocks, 3, elements)
    angles = face_angle.reshape(blocks, 3, elements)
    coefs = jnp.concatenate(
        [jnp.cos(angles), jnp.sin(angles), face_scale.reshape(blocks, 3, elements), walls, metric], axis=1
    )
    coefs = jnp.concatenate([coefs, coefs], axis=2)
    inflow = jnp.pad(breach.astype(f32), ((0, 0), (2 * comp, LANES - 2 * comp - members)))
    lift_h, lift_l = high_low(t["lift"])
    matrix = np.concatenate(
        [t["along"][0], t["along"][0], t["along"][1], t["along"][1], lift_h.astype(np.float32), lift_h.astype(np.float32)],
        axis=1,
    )
    mats = [
        jnp.asarray(np.tile(t["own"], (2, 1)), bf16), jnp.asarray(np.tile(t["spread"], (2, 1)), bf16),
        jnp.asarray(matrix, bf16), jnp.asarray(lift_l),
    ]
    packed = round_up(3 * used, 8)

    def finish(leaving, out_shape, extra, n_sems):
        return call(
            functools.partial(finish_kernel, t=t, blocks=blocks, elements=elements, leaving=leaving),
            out_shape,
            5, 10,
            [
                pltpu.VMEM((blocks, 3 * comp, LANES), f32), pltpu.VMEM((faces + 2 * width, LANES), f32),
                pltpu.VMEM(coefs.shape, f32), pltpu.VMEM(inflow.shape, f32),
                *[pltpu.VMEM(m.shape, bf16) for m in mats],
                pltpu.VMEM((3, LANES, LANES), f32), pltpu.VMEM((3 * LANES, 2 * LANES), bf16),
                pltpu.VMEM((3, LANES, LANES), f32), pltpu.VMEM((LANES, 8 * LANES), f32),
                pltpu.VMEM((3 * LANES, LANES), f32), pltpu.VMEM((3, LANES, 6 * LANES), bf16),
                *extra, dma((10 + n_sems,)),
            ],
            jax.tree.map(lambda _: ANY, out_shape),
        )(order, target_dev, n_leaving.reshape(1), links, wet_blocks, fields, pool, before, after, coefs, inflow, *mats)

    sent = finish(
        True, jax.ShapeDtypeStruct((count, packed, LANES), f32), [pltpu.VMEM((blocks, packed, LANES), f32)], blocks
    )
    got = lax.all_to_all(sent, "mesh", split_axis=0, concat_axis=0, tiled=True)
    final = (jax.ShapeDtypeStruct(depth_rows.shape, f32), jax.ShapeDtypeStruct(flow_rows.shape, f32))
    whole = [pltpu.VMEM(depth_rows.shape, f32), pltpu.VMEM(flow_rows.shape, f32)]
    kept = finish(False, final, [pltpu.VMEM((2, 3 * comp, LANES), f32), *whole], 2)
    depth_new, flow_new = call(
        functools.partial(merge_kernel, t=t, blocks=blocks),
        final,
        2, 3,
        [*whole, pltpu.VMEM((blocks, packed, LANES), f32), dma((2 * blocks + 1,))],
        (ANY, ANY),
        input_output_aliases={3: 0, 4: 1},
    )(source_dev, arrives, got, *kept)
    depth_out = depth_new.reshape(members, tiles, pairs, 8, LANES).transpose(1, 3, 0, 2, 4).reshape(water_depth.shape)
    return depth_out, flow_new.transpose(0, 2, 1, 3)


def solution(mesh):
    in_specs = (
        P(("groups", "mesh"), None, None),
        P(("groups", "mesh"), None, None, None),
        P(("groups", "mesh"), None, None),
        P(("groups", "mesh"), None),
        P(("groups", "mesh"), None),
        P(("groups", "mesh"), None),
        P(("groups", "mesh"), None),
        P(("groups", "mesh")),
        P(("groups", "mesh"), None),
        P("groups"),
    )
    out_specs = (P(("groups", "mesh"), None, None), P(("groups", "mesh"), None, None, None))
    return jax.shard_map(body, mesh=mesh, in_specs=in_specs, out_specs=out_specs, check_vma=False)
```

profile of v0, /device:TPU:15, one launch (start us, length us, event | category | flops | bytes accessed | tf_op | source)
XLA Modules:
  0.0 75.7 jit_solution(17698736521648415892)
XLA Ops:
  0.6 0.0 copy-start.18
  0.6 0.0 copy-start.4
  0.7 1.3 %copy-done.4 = f32[24,2,10,640]{3,1,2,0:T(2,128)S(1)} copy-done((f32[24,2,10,640]{3,1,2,0:T(2,128)S(1)}, f32[24,2,10,640]{3,1,2,0:T(2,128)}, u32[]{:S(2)}) %copy-start.4) | copy-done | bytes 1228824
  1.9 1.1 %copy-done.6 = f32[24,10,640]{2,0,1:T(8,128)S(1)} copy-done((f32[24,10,640]{2,0,1:T(8,128)S(1)}, f32[24,10,640]{2,0,1:T(8,128)}, u32[]{:S(2)}) %copy-start.6) | copy-done | bytes 614424
  3.0 0.8 %copy-done.10 = bf16[256,128]{1,0:T(8,128)(2,1)S(1)} copy-done((bf16[256,128]{1,0:T(8,128)(2,1)S(1)}, bf16[256,128]{1,0:T(8,128)(2,1)}, u32[]{:S(2)}) %copy-start.10) | copy-done | bytes 65560
  3.9 0.7 copy-done.12
  4.5 0.0 copy-start.17
  4.5 0.0 copy-start.5
  4.5 0.0 copy-start.7
  4.6 0.0 copy-start.8
  4.6 0.0 copy-start.9
  4.6 0.0 copy-start.11
  4.6 9.8 %shard_map.158 = (f32[24,168,128]{2,1,0:T(8,128)S(1)}, f32[4608,128]{1,0:T(8,128)}, f32[64,128]{1,0:T(8,128)S(1)}, f32[64,128]{1,0:T(8,128)S(1)}) custom-call(s32[128]{0:T(128)S(1)} %bitcast.16, f32[1200,128]{1,0:T(8,128)S(1)} %bitcast.15, f32[24,10,2,640]{3,2,1,0:T(2,128)S(1)} %bitcast.14, bf16[256,128]{1,0:T(8,128)(2,1)S(1)} %copy-done.10), custom_call_target="tpu_custom_call" | custom-call | tf_op jit(solution)/shard_map/pallas_call | solution.py:470
  14.4 3.7 %collective-permute-start = (f32[64,128]{1,0:T(8,128)S(1)}, f32[64,128]{1,0:T(8,128)S(1)}, u32[]{:S(2)}, u32[]{:S(2)}) collective-permute-start(f32[64,128]{1,0:T(8,128)S(1)} %get-tuple-element.12), channel_id=1, source_target_pairs={{0,1},{1,2},{2,3},{3,4},{4,5},{5,6},{6,7},{7,8},{8,9},{9,10},{10,1... | collective-permute-start | bytes 98312 | tf_op jit(solution)/shard_map/ppermute | solution.py:488
  18.1 1.9 %collective-permute-start.1 = (f32[64,128]{1,0:T(8,128)S(1)}, f32[64,128]{1,0:T(8,128)S(1)}, u32[]{:S(2)}, u32[]{:S(2)}) collective-permute-start(f32[64,128]{1,0:T(8,128)S(1)} %get-tuple-element.13), channel_id=1, source_target_pairs={{1,0},{2,1},{3,2},{4,3},{5,4},{6,5},{7,6},{8,7},{9,8},{10,9},{11,1... | collective-permute-start | bytes 98312 | tf_op jit(solution)/shard_map/ppermute | solution.py:489
  20.1 0.0 copy-done.18
  20.1 0.7 fusion.1
  20.8 0.1 select_reduce_fusion.2
  20.9 0.0 copy-done.15
  20.9 0.1 fusion.2
  21.0 0.1 cos.7
  21.1 0.1 sin.7
  21.2 0.0 copy-done.13
  21.2 0.1 reshape.50
  21.3 0.0 copy-done.16
  21.3 0.1 reshape.49
  21.4 0.0 copy-done.14
  21.4 0.3 concatenate.6
  21.7 0.1 pad_maximum_fusion.coefs_in
  21.8 0.6 compare_select_fusion
  22.4 0.1 select_reduce_fusion.1.order
  22.5 0.1 reshape.45.links
  22.6 0.0 copy-done.17
  22.6 0.1 copy.22
  22.7 0.1 pad.4.inflow_in
  22.7 0.0 collective-permute-done.before_in
  22.7 1.5 %collective-permute-done.1.after_in = f32[64,128]{1,0:T(8,128)S(1)} collective-permute-done((f32[64,128]{1,0:T(8,128)S(1)}, f32[64,128]{1,0:T(8,128)S(1)}, u32[]{:S(2)}, u32[]{:S(2)}) %collective-permute-start.1) | collective-permute-done | bytes 32800 | tf_op jit(solution)/shard_map/ppermute | solution.py:489
  24.3 0.0 copy-done.5
  24.3 0.0 copy-done.7
  24.3 11.2 %shard_map.159 = f32[16,152,128]{2,1,0:T(8,128)S(1)} custom-call(s32[24]{0:T(128)S(1)} %select_reduce_fusion.1.order, s32[24]{0:T(128)S(1)} %get-tuple-element.20.place, s32[1]{0:T(128)} %bitcast.count, s32[4608]{0:T(1024)S(1)} %reshape.45.links, s32[24]{0:T(128)S(1)} %copy-done.11, f32[24,168,128]{2,1,0:T(8,128)S(1)} %get-tuple-element.10.fields_in, ...), custom_call_target="tpu_custom_call" | custom-call | tf_op jit(solution)/shard_map/pallas_call | solution.py:527
  35.5 1.3 %copy-done.1 = f32[24,168,128]{2,1,0:T(8,128)} copy-done((f32[24,168,128]{2,1,0:T(8,128)}, f32[24,168,128]{2,1,0:T(8,128)S(1)}, u32[]{:S(2)}) %copy-start.1) | copy-done | bytes 2064408
  36.8 1.1 %copy-done.3 = f32[16,152,128]{2,1,0:T(8,128)} copy-done((f32[16,152,128]{2,1,0:T(8,128)}, f32[16,152,128]{2,1,0:T(8,128)S(1)}, u32[]{:S(2)}) %copy-start.3) | copy-done | bytes 1245208
  37.8 5.1 %all-to-all-start = ((f32[16,152,128]{2,1,0:T(8,128)}), f32[16,152,128]{2,1,0:T(8,128)}, u32[]{:S(2)}, u32[]{:S(2)}) async-start(f32[16,152,128]{2,1,0:T(8,128)} %copy-done.3), calls=%async_computation | async-start | bytes 2490368 | tf_op jit(solution)/shard_map/all_to_all | solution.py:546
  42.9 0.2 select_reduce_fusion
  43.2 1.6 %copy-done.2 = f32[24,168,128]{2,1,0:T(8,128)S(1)} copy-done((f32[24,168,128]{2,1,0:T(8,128)S(1)}, f32[24,168,128]{2,1,0:T(8,128)}, u32[]{:S(2)}) %copy-start.2) | copy-done | bytes 2064408
  44.7 17.5 %shard_map.160 = (f32[1200,128]{1,0:T(8,128)}, f32[24,10,2,640]{3,2,1,0:T(2,128)}) custom-call(s32[24]{0:T(128)S(1)} %select_reduce_fusion.1.order, s32[24]{0:T(128)S(1)} %get-tuple-element.20.place, s32[1]{0:T(128)} %bitcast.count, s32[4608]{0:T(1024)S(1)} %reshape.45.links, s32[24]{0:T(128)S(1)} %copy-done.11, f32[24,168,128]{2,1,0:T(8,128)S(1)} %copy-done.2, ...), custom_call_target="tpu_custom_call" | custom-call | tf_op jit(solution)/shard_map/pallas_call | solution.py:527
  62.2 10.0 %all-to-all-done.got = f32[16,152,128]{2,1,0:T(8,128)} async-done(((f32[16,152,128]{2,1,0:T(8,128)}), f32[16,152,128]{2,1,0:T(8,128)}, u32[]{:S(2)}, u32[]{:S(2)}) %all-to-all-start) | async-done | bytes 1245216 | tf_op jit(solution)/shard_map/all_to_all | solution.py:546
  72.2 3.5 %shard_map.161 = (f32[1200,128]{1,0:T(8,128)}, f32[24,10,2,640]{3,2,1,0:T(2,128)}) custom-call(s32[24]{0:T(128)S(1)} %get-tuple-element.22.source, s32[24]{0:T(128)S(1)} %get-tuple-element.21.arrives, f32[16,152,128]{2,1,0:T(8,128)} %all-to-all-done.got, f32[1200,128]{1,0:T(8,128)} %get-tuple-element.14.depth_in, ...), custom_call_target="tpu_custom_call", output_to_operand_aliasing={{0}: (3, {}), {1}: (4, {})} | custom-call | tf_op jit(solution)/shard_map/pallas_call | solution.py:550
  (19 shorter events, 0.1 us)
Async XLA Ops:
  0.6 19.4 %copy-start.18 = (s32[384]{0:T(512)S(1)}, s32[384]{0:T(512)}, u32[]{:S(2)}) copy-start(s32[384]{0:T(512)} %param.24) | copy-start | bytes 4612
  0.6 1.3 %copy-start.4 = (f32[24,2,10,640]{3,1,2,0:T(2,128)S(1)}, f32[24,2,10,640]{3,1,2,0:T(2,128)}, u32[]{:S(2)}) copy-start(f32[24,2,10,640]{3,1,2,0:T(2,128)} %param.16) | copy-start | bytes 3686404
  1.9 1.1 %copy-start.6 = (f32[24,10,640]{2,0,1:T(8,128)S(1)}, f32[24,10,640]{2,0,1:T(8,128)}, u32[]{:S(2)}) copy-start(f32[24,10,640]{2,0,1:T(8,128)} %param.15) | copy-start | bytes 1843204
  3.0 0.8 %copy-start.10 = (bf16[256,128]{1,0:T(8,128)(2,1)S(1)}, bf16[256,128]{1,0:T(8,128)(2,1)}, u32[]{:S(2)}) copy-start(bf16[256,128]{1,0:T(8,128)(2,1)} %constant.38.clone.back_in) | copy-start | bytes 196612
  3.9 0.7 copy-start.12
  4.5 16.4 %copy-start.15 = (f32[24,192]{1,0:T(8,128)S(1)}, f32[24,192]{1,0:T(8,128)}, u32[]{:S(2)}) copy-start(f32[24,192]{1,0:T(8,128)} %param.19) | copy-start | bytes 55300
  4.5 16.6 %copy-start.13 = (s32[24,192]{1,0:T(8,128)S(1)}, s32[24,192]{1,0:T(8,128)}, u32[]{:S(2)}) copy-start(s32[24,192]{1,0:T(8,128)} %param.20) | copy-start | bytes 55300
  4.5 16.8 %copy-start.16 = (f32[24,192]{1,0:T(8,128)S(1)}, f32[24,192]{1,0:T(8,128)}, u32[]{:S(2)}) copy-start(f32[24,192]{1,0:T(8,128)} %param.18) | copy-start | bytes 55300
  4.5 16.9 %copy-start.14 = (f32[24,4,64]{2,1,0:T(4,128)S(1)}, f32[24,4,64]{2,1,0:T(4,128)}, u32[]{:S(2)}) copy-start(f32[24,4,64]{2,1,0:T(4,128)} %param.17) | copy-start | bytes 73732
  4.5 18.0 %copy-start.17 = (s32[24,10]{0,1:T(8,128)S(1)}, s32[24,10]{0,1:T(8,128)}, u32[]{:S(2)}) copy-start(s32[24,10]{0,1:T(8,128)} %param.23) | copy-start | bytes 2884
  4.5 19.7 %copy-start.5 = (bf16[112,768]{1,0:T(8,128)(2,1)S(1)}, bf16[112,768]{1,0:T(8,128)(2,1)}, u32[]{:S(2)}) copy-start(bf16[112,768]{1,0:T(8,128)(2,1)} %constant.41.clone.matrix_in) | copy-start | bytes 516100
  4.5 19.7 %copy-start.7 = (bf16[256,128]{1,0:T(8,128)(2,1)S(1)}, bf16[256,128]{1,0:T(8,128)(2,1)}, u32[]{:S(2)}) copy-start(bf16[256,128]{1,0:T(8,128)(2,1)} %constant.39.clone.own_in) | copy-start | bytes 196612
  4.6 19.7 %copy-start.8 = (bf16[32,1024]{1,0:T(8,128)(2,1)S(1)}, bf16[32,1024]{1,0:T(8,128)(2,1)}, u32[]{:S(2)}) copy-start(bf16[32,1024]{1,0:T(8,128)(2,1)} %constant.40.clone.spread_in) | copy-start | bytes 196612
  4.6 19.7 %copy-start.9 = (bf16[112,128]{1,0:T(8,128)(2,1)S(1)}, bf16[112,128]{1,0:T(8,128)(2,1)}, u32[]{:S(2)}) copy-start(bf16[112,128]{1,0:T(8,128)(2,1)} %constant.42.clone.low_in) | copy-start | bytes 86020
  4.6 19.7 %copy-start.11 = (s32[24]{0:T(128)S(1)}, s32[24]{0:T(128)}, u32[]{:S(2)}) copy-start(s32[24]{0:T(128)} %wet.3) | copy-start | bytes 292
  14.4 8.3 %collective-permute-start = (f32[64,128]{1,0:T(8,128)S(1)}, f32[64,128]{1,0:T(8,128)S(1)}, u32[]{:S(2)}, u32[]{:S(2)}) collective-permute-start(f32[64,128]{1,0:T(8,128)S(1)} %get-tuple-element.12), channel_id=1, source_target_pairs={{0,1},{1,2},{2,3},{3,4},{4,5},{5,6},{6,7},{7,8},{8,9},{9,10},{10,1... | collective-permute-start | bytes 98312 | tf_op jit(solution)/shard_map/ppermute | solution.py:488
  18.1 6.1 %collective-permute-start.1 = (f32[64,128]{1,0:T(8,128)S(1)}, f32[64,128]{1,0:T(8,128)S(1)}, u32[]{:S(2)}, u32[]{:S(2)}) collective-permute-start(f32[64,128]{1,0:T(8,128)S(1)} %get-tuple-element.13), channel_id=1, source_target_pairs={{1,0},{2,1},{3,2},{4,3},{5,4},{6,5},{7,6},{8,7},{9,8},{10,9},{11,1... | collective-permute-start | bytes 98312 | tf_op jit(solution)/shard_map/ppermute | solution.py:489
  35.5 1.3 %copy-start.1 = (f32[24,168,128]{2,1,0:T(8,128)}, f32[24,168,128]{2,1,0:T(8,128)S(1)}, u32[]{:S(2)}) copy-start(f32[24,168,128]{2,1,0:T(8,128)S(1)} %get-tuple-element.10.fields_in) | copy-start | bytes 6193156
  36.8 1.1 %copy-start.3 = (f32[16,152,128]{2,1,0:T(8,128)}, f32[16,152,128]{2,1,0:T(8,128)S(1)}, u32[]{:S(2)}) copy-start(f32[16,152,128]{2,1,0:T(8,128)S(1)} %shard_map.159) | copy-start | bytes 3735556
  37.8 5.3 %copy-start = (f32[4608,128]{1,0:T(8,128)S(1)}, f32[4608,128]{1,0:T(8,128)}, u32[]{:S(2)}) copy-start(f32[4608,128]{1,0:T(8,128)} %get-tuple-element.11.pool_in) | copy-start | bytes 7077892
  37.8 34.4 %all-to-all-start = ((f32[16,152,128]{2,1,0:T(8,128)}), f32[16,152,128]{2,1,0:T(8,128)}, u32[]{:S(2)}, u32[]{:S(2)}) async-start(f32[16,152,128]{2,1,0:T(8,128)} %copy-done.3), calls=%async_computation | async-start | bytes 2490368 | tf_op jit(solution)/shard_map/all_to_all | solution.py:546
  43.1 1.6 %copy-start.2 = (f32[24,168,128]{2,1,0:T(8,128)S(1)}, f32[24,168,128]{2,1,0:T(8,128)}, u32[]{:S(2)}) copy-start(f32[24,168,128]{2,1,0:T(8,128)} %copy-done.1) | copy-start | bytes 6193156
where the time goes:
time: 76.2 us; the launch traced here: 75.7 us
  Pallas kernels  42 us (55%)
  waiting for transfers between devices  11.5 us (15%)
  starting transfers between devices  10.7 us (14%)
  local copies, waits for them, and re-layouts  8.81 us (12%)
  other arithmetic  1.8 us (2%)
  between operations  0.89 us (1%)
    pallas_call x2, Pallas kernels, finish(): call(functools.partial(finish_kernel, t=t, blocks=blocks, elements=elemen...  28.6 us
    all_to_all x1, waiting for transfers between devices, body(): got = lax.all_to_all(sent, 'mesh', split_axis=0, concat_axis=0, tiled=True)  9.99 us
    pallas_call x1, Pallas kernels, body(): call(functools.partial(prepare_kernel, t=t, blocks=blocks, elements=eleme...  9.81 us
    unnamed x38, local copies, waits for them, and re-layouts  7.84 us
    all_to_all x1, starting transfers between devices, body(): got = lax.all_to_all(sent, 'mesh', split_axis=0, concat_axis=0, tiled=True)  5.1 us
    ppermute x1, starting transfers between devices, body(): before = lax.ppermute(tail, 'mesh', [(i, i + 1) for i in range(count - 1)])  3.71 us
    pallas_call x1, Pallas kernels, body(): call(functools.partial(merge_kernel, t=t, blocks=blocks), final, 2, 3, [*...  3.54 us
    ppermute x1, starting transfers between devices, body(): after = lax.ppermute(head, 'mesh', [(i + 1, i) for i in range(count - 1)])  1.92 us
  transfers between devices with their start and end apart: 3, of which 2 were waited for; matrix products, arithmetic and copies ran while one was open for 4% of the time, Pallas kernels for 23%

commit v1 on v0

--- a/solution.py
+++ b/solution.py
@@ -139,7 +139,11 @@
     return pltpu.roll(x, LANES // 2, 1)
 
 
-def turn_pair(fields, first, second, turned, halves, comp):
+def turn(x, eye):
+    return mm(eye[...], jnp.concatenate(split(x), axis=1), ((1,), (1,)))
+
+
+def turn_pair(fields, first, second, eye, turned, halves, comp):
     lower = lax.broadcasted_iota(jnp.int32, (comp, LANES), 1) < LANES // 2
     for c in range(3):
         a = fields[first, c * comp : (c + 1) * comp]
@@ -147,7 +151,7 @@
         even = jnp.where(lower, a, swap_halves(b))
         odd = jnp.where(lower, swap_halves(a), b)
         fill = jnp.full((LANES - 2 * comp, LANES), 1.0 if c == 0 else 0.0, jnp.float32)
-        flat = jnp.concatenate([even, odd, fill], axis=0).T
+        flat = turn(jnp.concatenate([even, odd, fill], axis=0), eye)
         if turned is not None:
             turned[c] = flat
         high, low = split(flat)
@@ -160,6 +164,10 @@
     return jnp.where(lane < wide, moved[0], jnp.where(lane < 2 * wide, moved[1], moved[2]))
 
 
+def root(x):
+    return x * lax.rsqrt(x)
+
+
 def start_all(copies):
     for copy in copies:
         copy.start()
@@ -172,29 +180,38 @@
 
 
 def prepare_kernel(
-    rim, depth_in, flow_in, back_in, fields_out, pool_out, head, tail,
-    depth, flow, back, fields, pool, halves, sems, *, t, blocks, elements,
+    rim, depth_in, flow_in, back_in, eye_in, fields_out, pool_out, head, tail,
+    depth, flow, back, eye, fields, pool, halves, sems, *, t, blocks, elements,
 ):
     comp, pairs, members, wide = t["comp"], t["pairs"], t["members"], t["wide"]
     tiles = blocks // 8
-    group = 8 * 3 * elements
+    steps = blocks // 2
+    group = 2 * 3 * elements
     first = start_all(
-        [pltpu.make_async_copy(depth_in, depth, sems.at[0]), pltpu.make_async_copy(back_in, back, sems.at[1])]
-    )
-    flows = start_all(
         [
-            pltpu.make_async_copy(flow_in.at[pl.ds(8 * i, 8)], flow.at[pl.ds(8 * i, 8)], sems.at[2 + i])
-            for i in range(tiles)
+            pltpu.make_async_copy(depth_in, depth, sems.at[0]), pltpu.make_async_copy(back_in, back, sems.at[1]),
+            pltpu.make_async_copy(eye_in, eye, sems.at[2]),
         ]
     )
+
+    def part(tile):
+        rows = pl.ds(8 * tile, 8)
+        return pltpu.make_async_copy(flow_in.at[rows], flow.at[rows], sems.at[3 + tile])
+
+    def outward(i):
+        rows, lines = pl.ds(2 * i, 2), pl.ds(group * i, group)
+        return [
+            pltpu.make_async_copy(fields.at[rows], fields_out.at[rows], sems.at[3 + tiles + i]),
+            pltpu.make_async_copy(pool.at[lines], pool_out.at[lines], sems.at[3 + tiles + steps + i]),
+        ]
+
+    start_all([part(tile) for tile in range(tiles)])
     wait_all(first)
-    outs = []
-    filled = members * pairs
-    for tile in range(tiles):
-        flows[tile].wait()
-
-        def rows_of(sub, carry):
-            b = tile * 8 + sub
+
+    def build(i):
+        for u in range(2):
+            b = 2 * i + u
+            tile, sub = b // 8, b % 8
             for c in range(3):
                 end = comp * (c + 1)
                 fields[b, end - 8 : end] = jnp.full((8, LANES), 1.0 if c == 0 else 0.0, jnp.float32)
@@ -206,34 +223,34 @@
                     row = s * pairs + j
                     fields[b, comp + row : comp + row + 1] = two[0:1]
                     fields[b, 2 * comp + row : 2 * comp + row + 1] = two[1:2]
-            return carry
-
-        lax.fori_loop(0, 8, rows_of, 0)
-
-        def faces_of(i, carry):
-            b = tile * 8 + 2 * i
-            turn_pair(fields, b, b + 1, None, halves, comp)
-            rows = mm(halves[...], back[...])
-            lane = lax.broadcasted_iota(jnp.int32, (LANES, LANES), 1)
-            pieces = [rows[c * LANES : (c + 1) * LANES] for c in range(3)]
-            for f in range(3):
-                face = place_face(pieces, f, wide, lane)
-                for u in range(2):
-                    pool[pl.ds(((b + u) * 3 + f) * elements, elements), :] = face[u * elements : (u + 1) * elements]
-            return carry
-
-        lax.fori_loop(0, 4, faces_of, 0)
-        outs += start_all(
-            [
-                pltpu.make_async_copy(
-                    fields.at[pl.ds(8 * tile, 8)], fields_out.at[pl.ds(8 * tile, 8)], sems.at[2 + tiles + 2 * tile]
-                ),
-                pltpu.make_async_copy(
-                    pool.at[pl.ds(group * tile, group)], pool_out.at[pl.ds(group * tile, group)],
-                    sems.at[3 + tiles + 2 * tile],
-                ),
-            ]
-        )
+
+    def faces_of(i):
+        turn_pair(fields, 2 * i, 2 * i + 1, eye, None, halves, comp)
+        rows = mm(halves[...], back[...])
+        lane = lax.broadcasted_iota(jnp.int32, (LANES, LANES), 1)
+        pieces = [rows[c * LANES : (c + 1) * LANES] for c in range(3)]
+        for f in range(3):
+            face = place_face(pieces, f, wide, lane)
+            for u in range(2):
+                at = ((2 * i + u) * 3 + f) * elements
+                pool[pl.ds(at, elements), :] = face[u * elements : (u + 1) * elements]
+
+    part(0).wait()
+    build(0)
+
+    def one(i, carry):
+        @pl.when(i % 4 == 0)
+        def _():
+            part(i // 4).wait()
+
+        faces_of(i - 1)
+        build(i)
+        start_all(outward(i - 1))
+        return carry
+
+    lax.fori_loop(1, steps, one, 0)
+    faces_of(steps - 1)
+    start_all(outward(steps - 1))
     width = head.shape[0]
 
     def pick(i, carry):
@@ -244,16 +261,21 @@
         return carry
 
     lax.fori_loop(0, width // 16, pick, 0)
-    wait_all(outs)
+
+    def drain(i, carry):
+        wait_all(outward(i))
+        return carry
+
+    lax.fori_loop(0, steps, drain, 0)
 
 
 def finish_kernel(
-    order, place, count, links, wet,
-    fields_in, pool_in, before_in, after_in, coefs_in, inflow_in, own_in, spread_in, matrix_in, low_in,
+    order, place, count, wet,
+    links, fields_in, pool_in, before_in, after_in, coefs_in, inflow_in, own_in, spread_in, matrix_in, low_in, eye_in,
     *rest, t, blocks, elements, leaving,
 ):
     outs, scratch = (rest[:1], rest[1:]) if leaving else (rest[:2], rest[2:])
-    fields, pool, coefs, inflow, own, spread, matrix, low, turned, halves, traces, factors, outer, pieces, *scratch = scratch
+    fields, pool, coefs, inflow, own, spread, matrix, low, eye, turned, halves, traces, factors, outer, pieces, near, *scratch = scratch
     staged, sems = scratch[0], scratch[-1]
     comp, pairs, members, wide, used = t["comp"], t["pairs"], t["members"], t["wide"], t["used"]
     faces = blocks * 3 * elements
@@ -262,39 +284,53 @@
         (fields_in, fields), (pool_in, pool.at[pl.ds(0, faces)]), (before_in, pool.at[pl.ds(faces, width)]),
         (after_in, pool.at[pl.ds(faces + width, width)]), (coefs_in, coefs), (inflow_in, inflow), (own_in, own),
         (spread_in, spread), (matrix_in, matrix), (low_in, low),
+        (eye_in, eye),
     ]
-    wait_all(start_all([pltpu.make_async_copy(a, b, sems.at[i]) for i, (a, b) in enumerate(loads)]))
-    n_loads = len(loads)
     begin = 0 if leaving else count[0]
     end = count[0] if leaving else blocks
-    step = 32
+    n_loads = len(loads) + 2
+
+    def indices(i):
+        at = (begin + 2 * i, jnp.minimum(begin + 2 * i + 1, end - 1))
+        return [
+            pltpu.make_async_copy(links.at[order[at[u]]], near.at[u], sems.at[len(loads) + u]) for u in range(2)
+        ]
+
+    steps = (end - begin + 1) // 2
+
+    @pl.when(steps > 0)
+    def _():
+        start_all(indices(0))
+
+    wait_all(start_all([pltpu.make_async_copy(a, b, sems.at[i]) for i, (a, b) in enumerate(loads)]))
+    step = 16
     chunks = [slice(i * step, (i + 1) * step) for i in range(LANES // step)]
 
     def one(i, carry):
         at = (begin + 2 * i, jnp.minimum(begin + 2 * i + 1, end - 1))
         both = (order[at[0]], order[at[1]])
 
+        wait_all(indices(i))
         for u in range(2):
-            base = both[u] * (3 * elements)
             for f in range(3):
-
-                def pick(r, carry):
-                    for w in range(32):
-                        e = r * 32 + w
-                        v = links[base + f * elements + e]
-                        outer[pl.ds(f * LANES + u * elements + e, 1), :] = pool[pl.ds(v, 1), :]
-                    return carry
-
-                lax.fori_loop(0, elements // 32, pick, 0)
-
-        turn_pair(fields, both[0], both[1], turned, halves, comp)
+                for e in range(elements):
+                    v = near[u, f * elements + e]
+                    row = f * LANES + u * elements + e
+                    outer[row : row + 1, :] = pool[pl.ds(v, 1), :]
+
+        @pl.when(i + 1 < steps)
+        def _():
+            start_all(indices(i + 1))
+
+        turn_pair(fields, both[0], both[1], eye, turned, halves, comp)
         inner = mm(halves[...], own[...])
         for c in range(3):
             traces[c] = inner[c * LANES : (c + 1) * LANES]
         lower = lax.broadcasted_iota(jnp.int32, (16, LANES), 1) < elements
         values = jnp.where(lower, coefs[both[0]], coefs[both[1]])
         rough = values.astype(jnp.bfloat16).astype(jnp.float32)
-        stacked = jnp.concatenate([rough, values - rough], axis=0).T.astype(jnp.bfloat16)
+        stacked = jnp.concatenate([rough, values - rough], axis=0).astype(jnp.bfloat16)
+        stacked = mm(eye[:, :LANES], stacked, ((1,), (1,))).astype(jnp.bfloat16)
         factors[...] = mm(stacked, spread[...])
 
         lane = lax.broadcasted_iota(jnp.int32, (step, LANES), 1)
@@ -331,7 +367,7 @@
             speed = through / height
             speed_o = through_o / height_o
             fast = jnp.maximum(
-                jnp.abs(speed) + jnp.sqrt(gravity * height), jnp.abs(speed_o) + jnp.sqrt(gravity * height_o)
+                jnp.abs(speed) + root(gravity * height), jnp.abs(speed_o) + root(gravity * height_o)
             )
             push = 0.5 * gravity * (height * height - height_o * height_o)
             half = 0.5 * scale
@@ -371,7 +407,7 @@
                 write_block(both[u], staged.at[u], comp, scratch[1], scratch[2], t, blocks)
         return carry
 
-    lax.fori_loop(0, (end - begin + 1) // 2, one, 0)
+    lax.fori_loop(0, steps, one, 0)
     if leaving:
 
         def finish(i, carry):
@@ -433,7 +469,7 @@
 
 
 SMEM = pl.BlockSpec(memory_space=pltpu.SMEM)
-ANY = pl.BlockSpec(memory_space=pl.ANY)
+HBM = pl.BlockSpec(memory_space=pltpu.HBM)
 VMEM = pl.BlockSpec(memory_space=pltpu.VMEM)
 
 
@@ -441,10 +477,10 @@
     return pl.pallas_call(
         kernel,
         out_shape=out_shape,
-        in_specs=[SMEM] * n_smem + [ANY] * n_args,
+        in_specs=[SMEM] * n_smem + [HBM] * n_args,
         out_specs=out_specs,
         scratch_shapes=scratch,
-        compiler_params=pltpu.CompilerParams(vmem_limit_bytes=48 << 20),
+        compiler_params=pltpu.CompilerParams(vmem_limit_bytes=64 << 20),
         **keys,
     )
 
@@ -467,6 +503,7 @@
     dma = pltpu.SemaphoreType.DMA
 
     back = jnp.asarray(np.tile(t["back"], (2, 1)), bf16)
+    eye = jnp.asarray(np.tile(np.eye(LANES), (1, 2)), bf16)
     fields, pool, head, tail = call(
         functools.partial(prepare_kernel, t=t, blocks=blocks, elements=elements),
         (
@@ -475,14 +512,15 @@
             jax.ShapeDtypeStruct((width, LANES), f32),
             jax.ShapeDtypeStruct((width, LANES), f32),
         ),
-        1, 3,
+        1, 4,
         [
             pltpu.VMEM(depth_rows.shape, f32), pltpu.VMEM(flow_rows.shape, f32), pltpu.VMEM(back.shape, bf16),
+            pltpu.VMEM(eye.shape, bf16),
             pltpu.VMEM((blocks, 3 * comp, LANES), f32), pltpu.VMEM((faces, LANES), f32),
-            pltpu.VMEM((3 * LANES, 2 * LANES), bf16), dma((2 + 3 * tiles,)),
+            pltpu.VMEM((3 * LANES, 2 * LANES), bf16), dma((3 + tiles + blocks,)),
         ],
-        (ANY, ANY, VMEM, VMEM),
-    )(rim_list, depth_rows, flow_rows, back)
+        (HBM, HBM, VMEM, VMEM),
+    )(rim_list, depth_rows, flow_rows, back, eye)
 
     count = lax.axis_size("mesh")
     before = lax.ppermute(tail, "mesh", [(i, i + 1) for i in range(count - 1)])
@@ -519,7 +557,7 @@
     )
     mats = [
         jnp.asarray(np.tile(t["own"], (2, 1)), bf16), jnp.asarray(np.tile(t["spread"], (2, 1)), bf16),
-        jnp.asarray(matrix, bf16), jnp.asarray(lift_l),
+        jnp.asarray(matrix, bf16), jnp.asarray(lift_l), eye,
     ]
     packed = round_up(3 * used, 8)
 
@@ -527,7 +565,7 @@
         return call(
             functools.partial(finish_kernel, t=t, blocks=blocks, elements=elements, leaving=leaving),
             out_shape,
-            5, 10,
+            4, 12,
             [
                 pltpu.VMEM((blocks, 3 * comp, LANES), f32), pltpu.VMEM((faces + 2 * width, LANES), f32),
                 pltpu.VMEM(coefs.shape, f32), pltpu.VMEM(inflow.shape, f32),
@@ -535,10 +573,11 @@
                 pltpu.VMEM((3, LANES, LANES), f32), pltpu.VMEM((3 * LANES, 2 * LANES), bf16),
                 pltpu.VMEM((3, LANES, LANES), f32), pltpu.VMEM((LANES, 8 * LANES), f32),
                 pltpu.VMEM((3 * LANES, LANES), f32), pltpu.VMEM((3, LANES, 6 * LANES), bf16),
-                *extra, dma((10 + n_sems,)),
+                pltpu.SMEM((2, face_map.shape[1]), jnp.int32),
+                *extra, dma((13 + n_sems,)),
             ],
-            jax.tree.map(lambda _: ANY, out_shape),
-        )(order, target_dev, n_leaving.reshape(1), links, wet_blocks, fields, pool, before, after, coefs, inflow, *mats)
+            jax.tree.map(lambda _: HBM, out_shape),
+        )(order, target_dev, n_leaving.reshape(1), wet_blocks, face_map, fields, pool, before, after, coefs, inflow, *mats)
 
     sent = finish(
         True, jax.ShapeDtypeStruct((count, packed, LANES), f32), [pltpu.VMEM((blocks, packed, LANES), f32)], blocks
@@ -552,7 +591,7 @@
         final,
         2, 3,
         [*whole, pltpu.VMEM((blocks, packed, LANES), f32), dma((2 * blocks + 1,))],
-        (ANY, ANY),
+        (HBM, HBM),
         input_output_aliases={3: 0, 4: 1},
     )(source_dev, arrives, got, *kept)
     depth_out = depth_new.reshape(members, tiles, pairs, 8, LANES).transpose(1, 3, 0, 2, 4).reshape(water_depth.shape)

time: 76.2 us -> 78 us (1.024)
  Pallas kernels: 42 us -> 47.2 us
  local copies, waits for them, and re-layouts: 8.81 us -> 4.52 us
  waiting for transfers between devices: 11.5 us -> 7.71 us
  other arithmetic: 1.8 us -> 4.95 us
  starting transfers between devices: 10.7 us -> 12.1 us
    unnamed x38 -> x4, local copies, waits for them, and re-layouts: 7.84 us -> 0.01 us
    pallas_call x2, Pallas kernels: 28.6 us -> 33 us  [finish(): call(functools.partial(finish_kernel, t=t, blocks=blocks, elements=elemen...]
    all_to_all x1, waiting for transfers between devices: 9.99 us -> 7.7 us  [body(): got = lax.all_to_all(sent, 'mesh', split_axis=0, concat_axis=0, tiled=True)]
    ppermute x1, waiting for transfers between devices: 1.53 us -> 0.01 us  [body(): after = lax.ppermute(head, 'mesh', [(i + 1, i) for i in range(count - 1)])]
    all_to_all x1, starting transfers between devices: 5.1 us -> 6.46 us  [body(): got = lax.all_to_all(sent, 'mesh', split_axis=0, concat_axis=0, tiled=True)]
    reduce_sum x1, other arithmetic: 0.69 us -> 1.95 us  [body(): n_leaving = jnp.sum(leaves)]
    concatenate x1, local copies, waits for them, and re-layouts: 0.3 us -> 1.09 us  [body(): jnp.concatenate([jnp.cos(angles), jnp.sin(angles), face_scale.reshape(blo...]
  transfers between devices with their start and end apart: 3 -> 3, of which waited for: 2 -> 1; matrix products, arithmetic and copies ran while one was open for 4% -> 12% of each run, Pallas kernels for 23% -> 27%
where the time goes in v1:
time: 78 us; the launch traced here: 77.2 us
  Pallas kernels  47.2 us (61%)
  starting transfers between devices  12.1 us (16%)
  waiting for transfers between devices  7.71 us (10%)
  other arithmetic  4.95 us (6%)
  local copies, waits for them, and re-layouts  4.52 us (6%)
    pallas_call x2, Pallas kernels, finish(): call(functools.partial(finish_kernel, t=t, blocks=blocks, elements=elemen...  33 us
    pallas_call x1, Pallas kernels, body(): call(functools.partial(prepare_kernel, t=t, blocks=blocks, elements=eleme...  10.5 us
    all_to_all x1, waiting for transfers between devices, body(): got = lax.all_to_all(sent, 'mesh', split_axis=0, concat_axis=0, tiled=True)  7.7 us
    all_to_all x1, starting transfers between devices, body(): got = lax.all_to_all(sent, 'mesh', split_axis=0, concat_axis=0, tiled=True)  6.46 us
    ppermute x1, starting transfers between devices, body(): before = lax.ppermute(tail, 'mesh', [(i, i + 1) for i in range(count - 1)])  3.71 us
    pallas_call x1, Pallas kernels, body(): call(functools.partial(merge_kernel, t=t, blocks=blocks), final, 2, 3, [*...  3.68 us
    reduce_sum x1, other arithmetic, body(): n_leaving = jnp.sum(leaves)  1.95 us
    ppermute x1, starting transfers between devices, body(): after = lax.ppermute(head, 'mesh', [(i + 1, i) for i in range(count - 1)])  1.92 us
  transfers between devices with their start and end apart: 3, of which 1 were waited for; matrix products, arithmetic and copies ran while one was open for 12% of the time, Pallas kernels for 27%

profile of v1, /device:TPU:15, one launch (start us, length us, event | category | flops | bytes accessed | tf_op | source)
XLA Modules:
  0.0 77.2 jit_solution(18074793893749391711)
XLA Ops:
  0.6 10.5 %shard_map.167 = (f32[24,168,128]{2,1,0:T(8,128)}, f32[4608,128]{1,0:T(8,128)}, f32[64,128]{1,0:T(8,128)}, f32[64,128]{1,0:T(8,128)}) custom-call(s32[128]{0:T(128)} %bitcast.18, f32[1200,128]{1,0:T(8,128)} %bitcast.16, f32[24,10,2,640]{3,2,1,0:T(2,128)} %bitcast.14, bf16[256,128]{1,0:T(8,128)(2,1)} %constant.40.clone.back_in, ...), custom_call_target="tpu_custom_call" | custom-call | tf_op jit(solution)/shard_map/pallas_call | solution.py:507
  11.2 0.0 copy-start
  11.2 3.7 %collective-permute-start = (f32[64,128]{1,0:T(8,128)}, f32[64,128]{1,0:T(8,128)}, u32[]{:S(2)}, u32[]{:S(2)}) collective-permute-start(f32[64,128]{1,0:T(8,128)} %get-tuple-element.12), channel_id=1, source_target_pairs={{0,1},{1,2},{2,3},{3,4},{4,5},{5,6},{6,7},{7,8},{8,9},{9,10},{10,1... | collective-permute-start | bytes 98312 | tf_op jit(solution)/shard_map/ppermute | solution.py:526
  14.9 1.9 %collective-permute-start.1 = (f32[64,128]{1,0:T(8,128)}, f32[64,128]{1,0:T(8,128)}, u32[]{:S(2)}, u32[]{:S(2)}) collective-permute-start(f32[64,128]{1,0:T(8,128)} %get-tuple-element.13), channel_id=1, source_target_pairs={{1,0},{2,1},{3,2},{4,3},{5,4},{6,5},{7,6},{8,7},{9,8},{10,9},{11,1... | collective-permute-start | bytes 98312 | tf_op jit(solution)/shard_map/ppermute | solution.py:527
  16.8 1.9 %fusion.1 = (s32[]{:T(128)}, s32[24]{0:T(128)S(1)}, s32[24]{0:T(128)}) fusion(s32[]{:T(128)S(6)} %axis_index.12, s32[384]{0:T(512)} %param.25, s32[]{:T(128)S(6)} %select_n.27), kind=kLoop, calls=%fused_computation.14 | loop fusion | flops 263 | bytes 300 | tf_op jit(solution)/shard_map/reduce_sum | solution.py:540
  18.8 0.1 select_reduce_fusion.2
  18.9 0.8 %fusion.2 = (f32[24,192]{1,0:T(8,128)S(1)}, f32[24,192]{1,0:T(8,128)S(1)}) fusion(f32[24,192]{1,0:T(8,128)} %param.20), kind=kLoop, calls=%fused_computation.15 | loop fusion | bytes 55296 | tf_op jit(solution)/shard_map/sin | solution.py:549
  19.8 0.1 cos.7
  19.8 0.1 sin.7
  19.9 0.8 %reshape.47 = s32[24,3,64]{2,1,0:T(4,128)S(1)} reshape(s32[24,192]{1,0:T(8,128)} %links.3) | data formatting | bytes 36864 | tf_op jit(solution)/shard_map/reshape | solution.py:499
  20.8 0.8 %reshape.46 = f32[24,3,64]{2,1,0:T(4,128)S(1)} reshape(f32[24,192]{1,0:T(8,128)} %param.19) | data formatting | bytes 36864 | tf_op jit(solution)/shard_map/reshape | solution.py:549
  21.6 1.1 %concatenate.6 = f32[24,16,64]{2,1,0:T(8,128)S(1)} concatenate(f32[24,3,64]{2,1,0:T(4,128)S(1)} %cos.7, f32[24,3,64]{2,1,0:T(4,128)S(1)} %sin.7, f32[24,3,64]{2,1,0:T(4,128)S(1)} %reshape.46, f32[24,3,64]{2,1,0:T(4,128)S(1)} %fusion, f32[24,4,64]{2,1,0:T(4,128)} %param.18), dimensions={1} | concatenate | bytes 196608 | tf_op jit(solution)/shard_map/concatenate | solution.py:548
  22.7 0.8 %pad_maximum_fusion.coefs_in = f32[24,16,128]{2,1,0:T(8,128)} fusion(f32[24,16,64]{2,1,0:T(8,128)S(1)} %concatenate.6), kind=kLoop, calls=%fused_computation | loop fusion | flops 49152 | bytes 294912 | tf_op jit(solution)/shard_map/concatenate | solution.py:551
  23.5 0.6 compare_select_fusion
  24.1 0.7 select_reduce_fusion.1.order
  24.8 0.0 copy-done
  24.8 0.1 copy.23
  24.9 0.7 pad.4.inflow_in
  25.6 0.0 collective-permute-done.before_in
  25.6 0.0 collective-permute-done.1.after_in
  25.6 12.2 %shard_map.168 = f32[16,152,128]{2,1,0:T(8,128)} custom-call(s32[24]{0:T(128)} %select_reduce_fusion.1.order, s32[24]{0:T(128)} %get-tuple-element.20.place, s32[1]{0:T(128)} %bitcast.count, s32[24]{0:T(128)} %wet.3, s32[24,192]{1,0:T(8,128)} %links.3, f32[24,168,128]{2,1,0:T(8,128)} %get-tuple-element.10.fields_in, f32[4608,128]{1,0:T(8,128)} %get-tuple-element.11.pool_in, ...), custom_call_target="tpu_custom_call" | custom-call | tf_op jit(solution)/shard_map/pallas_call | solution.py:565
  37.8 0.0 copy-start.1
  37.8 6.5 %all-to-all-start = ((f32[16,152,128]{2,1,0:T(8,128)}), f32[16,152,128]{2,1,0:T(8,128)}, u32[]{:S(2)}, u32[]{:S(2)}) async-start(f32[16,152,128]{2,1,0:T(8,128)} %shard_map.168), calls=%async_computation | async-start | bytes 2490368 | tf_op jit(solution)/shard_map/all_to_all | solution.py:585
  44.3 0.0 copy-done.1
  44.3 0.2 select_reduce_fusion
  44.5 0.6 compare_convert_fusion.1
  45.0 20.8 %shard_map.169 = (f32[1200,128]{1,0:T(8,128)}, f32[24,10,2,640]{3,2,1,0:T(2,128)}) custom-call(s32[24]{0:T(128)} %select_reduce_fusion.1.order, s32[24]{0:T(128)} %get-tuple-element.20.place, s32[1]{0:T(128)} %bitcast.count, s32[24]{0:T(128)} %wet.3, s32[24,192]{1,0:T(8,128)} %links.3, f32[24,168,128]{2,1,0:T(8,128)} %get-tuple-element.10.fields_in, ...), custom_call_target="tpu_custom_call" | custom-call | tf_op jit(solution)/shard_map/pallas_call | solution.py:565
  65.8 7.7 %all-to-all-done.got = f32[16,152,128]{2,1,0:T(8,128)} async-done(((f32[16,152,128]{2,1,0:T(8,128)}), f32[16,152,128]{2,1,0:T(8,128)}, u32[]{:S(2)}, u32[]{:S(2)}) %all-to-all-start) | async-done | bytes 1245216 | tf_op jit(solution)/shard_map/all_to_all | solution.py:585
  73.5 3.7 %shard_map.170 = (f32[1200,128]{1,0:T(8,128)}, f32[24,10,2,640]{3,2,1,0:T(2,128)}) custom-call(s32[24]{0:T(128)} %get-tuple-element.22.source, s32[24]{0:T(128)} %get-tuple-element.21.arrives, f32[16,152,128]{2,1,0:T(8,128)} %all-to-all-done.got, f32[1200,128]{1,0:T(8,128)} %get-tuple-element.14.depth_in, ...), custom_call_target="tpu_custom_call", output_to_operand_aliasing={{0}: (3, {}), {1}: (4, {})} | custom-call | tf_op jit(solution)/shard_map/pallas_call | solution.py:589
  (3 shorter events, 0.0 us)
Async XLA Ops:
  11.2 13.6 %copy-start = (s32[24,10]{0,1:T(8,128)S(1)}, s32[24,10]{0,1:T(8,128)}, u32[]{:S(2)}) copy-start(s32[24,10]{0,1:T(8,128)} %param.24) | copy-start | bytes 2884
  11.2 14.4 %collective-permute-start = (f32[64,128]{1,0:T(8,128)}, f32[64,128]{1,0:T(8,128)}, u32[]{:S(2)}, u32[]{:S(2)}) collective-permute-start(f32[64,128]{1,0:T(8,128)} %get-tuple-element.12), channel_id=1, source_target_pairs={{0,1},{1,2},{2,3},{3,4},{4,5},{5,6},{6,7},{7,8},{8,9},{9,10},{10,1... | collective-permute-start | bytes 98312 | tf_op jit(solution)/shard_map/ppermute | solution.py:526
  14.9 10.7 %collective-permute-start.1 = (f32[64,128]{1,0:T(8,128)}, f32[64,128]{1,0:T(8,128)}, u32[]{:S(2)}, u32[]{:S(2)}) collective-permute-start(f32[64,128]{1,0:T(8,128)} %get-tuple-element.13), channel_id=1, source_target_pairs={{1,0},{2,1},{3,2},{4,3},{5,4},{6,5},{7,6},{8,7},{9,8},{10,9},{11,1... | collective-permute-start | bytes 98312 | tf_op jit(solution)/shard_map/ppermute | solution.py:527
  37.8 6.5 %copy-start.1 = (s32[384]{0:T(512)S(1)}, s32[384]{0:T(512)}, u32[]{:S(2)}) copy-start(s32[384]{0:T(512)} %param.25) | copy-start | bytes 4612
  37.8 35.7 %all-to-all-start = ((f32[16,152,128]{2,1,0:T(8,128)}), f32[16,152,128]{2,1,0:T(8,128)}, u32[]{:S(2)}, u32[]{:S(2)}) async-start(f32[16,152,128]{2,1,0:T(8,128)} %shard_map.168), calls=%async_computation | async-start | bytes 2490368 | tf_op jit(solution)/shard_map/all_to_all | solution.py:585

commit v2 on v1

--- a/solution.py
+++ b/solution.py
@@ -180,8 +180,8 @@
 
 
 def prepare_kernel(
-    rim, depth_in, flow_in, back_in, eye_in, fields_out, pool_out, head, tail,
-    depth, flow, back, eye, fields, pool, halves, sems, *, t, blocks, elements,
+    rim_in, depth_in, flow_in, back_in, eye_in, fields_out, pool_out, head, tail,
+    rim, depth, flow, back, eye, fields, pool, halves, sems, *, t, blocks, elements,
 ):
     comp, pairs, members, wide = t["comp"], t["pairs"], t["members"], t["wide"]
     tiles = blocks // 8
@@ -191,6 +191,7 @@
         [
             pltpu.make_async_copy(depth_in, depth, sems.at[0]), pltpu.make_async_copy(back_in, back, sems.at[1]),
             pltpu.make_async_copy(eye_in, eye, sems.at[2]),
+            pltpu.make_async_copy(rim_in, rim, sems.at[3 + tiles + 2 * steps]),
         ]
     )
 
@@ -224,8 +225,10 @@
                     fields[b, comp + row : comp + row + 1] = two[0:1]
                     fields[b, 2 * comp + row : 2 * comp + row + 1] = two[1:2]
 
+    def turn_of(i):
+        turn_pair(fields, 2 * i, 2 * i + 1, eye, None, halves, comp)
+
     def faces_of(i):
-        turn_pair(fields, 2 * i, 2 * i + 1, eye, None, halves, comp)
         rows = mm(halves[...], back[...])
         lane = lax.broadcasted_iota(jnp.int32, (LANES, LANES), 1)
         pieces = [rows[c * LANES : (c + 1) * LANES] for c in range(3)]
@@ -237,18 +240,24 @@
 
     part(0).wait()
     build(0)
+    turn_of(0)
+    build(1)
 
     def one(i, carry):
         @pl.when(i % 4 == 0)
         def _():
             part(i // 4).wait()
 
-        faces_of(i - 1)
+        faces_of(i - 2)
+        turn_of(i - 1)
         build(i)
-        start_all(outward(i - 1))
+        start_all(outward(i - 2))
         return carry
 
-    lax.fori_loop(1, steps, one, 0)
+    lax.fori_loop(2, steps, one, 0)
+    faces_of(steps - 2)
+    turn_of(steps - 1)
+    start_all(outward(steps - 2))
     faces_of(steps - 1)
     start_all(outward(steps - 1))
     width = head.shape[0]
@@ -256,8 +265,8 @@
     def pick(i, carry):
         for u in range(16):
             r = i * 16 + u
-            head[pl.ds(r, 1), :] = pool[pl.ds(rim[r], 1), :]
-            tail[pl.ds(r, 1), :] = pool[pl.ds(rim[width + r], 1), :]
+            head[pl.ds(r, 1), :] = pool[pl.ds(rim[0, r], 1), :]
+            tail[pl.ds(r, 1), :] = pool[pl.ds(rim[0, width + r], 1), :]
         return carry
 
     lax.fori_loop(0, width // 16, pick, 0)
@@ -269,31 +278,78 @@
     lax.fori_loop(0, steps, drain, 0)
 
 
+def scan_moves(plan, base, order, place, blocks):
+    def one(i, carry):
+        leaving, staying = carry
+        slot = plan[base + i]
+        away = jnp.logical_or(slot < base, slot >= base + blocks).astype(jnp.int32)
+        order[jnp.where(away == 1, leaving, blocks - 1 - staying)] = i
+        place[i] = lax.div(slot, jnp.int32(blocks))
+        return leaving + away, staying + 1 - away
+
+    return lax.fori_loop(0, blocks, one, (jnp.int32(0), jnp.int32(0)))[0]
+
+
+def scan_origins(plan, own, origin, blocks, devices):
+    def device(d, carry):
+        mark = jnp.where(d == own, -1, d)
+        for i in range(blocks):
+            slot = plan[d * blocks + i] - own * blocks
+            origin[jnp.where(jnp.logical_and(slot >= 0, slot < blocks), slot, blocks)] = mark
+        return carry
+
+    lax.fori_loop(0, devices, device, 0)
+
+
+def face_rows(angle, scale, links, metric, coefs, blocks, elements):
+    shape = (blocks, 3 * elements)
+    own = lax.broadcasted_iota(jnp.int32, shape, 0) * (3 * elements) + lax.broadcasted_iota(jnp.int32, shape, 1)
+    wall = jnp.where(links[...] == own, 1.0, 0.0)
+    lower = lax.broadcasted_iota(jnp.int32, (blocks, LANES), 1) < elements
+    for q, value in enumerate((jnp.cos(angle[...]), jnp.sin(angle[...]), scale[...], wall)):
+        two = value[:, :LANES]
+        swapped = swap_halves(two)
+        third = value[:, LANES:]
+        faces = (
+            jnp.where(lower, two, swapped), jnp.where(lower, swapped, two), jnp.concatenate([third, third], axis=1)
+        )
+        for f in range(3):
+            coefs[pl.ds(3 * q + f, blocks, stride=16), :] = faces[f]
+    for b in range(blocks):
+        factors = metric[b]
+        coefs[b * 16 + 12 : b * 16 + 16] = jnp.concatenate([factors, factors], axis=1)
+
+
 def finish_kernel(
-    order, place, count, wet,
-    links, fields_in, pool_in, before_in, after_in, coefs_in, inflow_in, own_in, spread_in, matrix_in, low_in, eye_in,
-    *rest, t, blocks, elements, leaving,
+    plan_in, wet_in, breach_in, links_in, angle_in, scale_in, metric_in,
+    fields_in, pool_in, before_in, after_in, own_in, spread_in, matrix_in, low_in, eye_in,
+    *rest, t, blocks, elements, leaving, devices,
 ):
-    outs, scratch = (rest[:1], rest[1:]) if leaving else (rest[:2], rest[2:])
-    fields, pool, coefs, inflow, own, spread, matrix, low, eye, turned, halves, traces, factors, outer, pieces, near, *scratch = scratch
+    outs, scratch = (rest[:1], rest[1:]) if leaving else (rest[:3], rest[3:])
+    plan, wet, breach, links, angle, scale, metric, fields, pool, own, spread, matrix, low, eye, *scratch = scratch
+    order, place, coefs, turned, halves, traces, factors, outer, pieces, near, *scratch = scratch
     staged, sems = scratch[0], scratch[-1]
     comp, pairs, members, wide, used = t["comp"], t["pairs"], t["members"], t["wide"], t["used"]
     faces = blocks * 3 * elements
     width = before_in.shape[0]
     loads = [
-        (fields_in, fields), (pool_in, pool.at[pl.ds(0, faces)]), (before_in, pool.at[pl.ds(faces, width)]),
-        (after_in, pool.at[pl.ds(faces + width, width)]), (coefs_in, coefs), (inflow_in, inflow), (own_in, own),
-        (spread_in, spread), (matrix_in, matrix), (low_in, low),
-        (eye_in, eye),
+        (plan_in, plan), (angle_in, angle), (scale_in, scale), (links_in, links), (metric_in, metric),
+        (wet_in, wet), (breach_in, breach), (eye_in, eye), (own_in, own), (fields_in, fields),
+        (pool_in, pool.at[pl.ds(0, faces)]), (before_in, pool.at[pl.ds(faces, width)]),
+        (after_in, pool.at[pl.ds(faces + width, width)]), (spread_in, spread), (matrix_in, matrix), (low_in, low),
     ]
-    begin = 0 if leaving else count[0]
-    end = count[0] if leaving else blocks
     n_loads = len(loads) + 2
+    loads = start_all([pltpu.make_async_copy(a, b, sems.at[i]) for i, (a, b) in enumerate(loads)])
+    index = lax.axis_index("mesh")
+    loads[0].wait()
+    n_leaving = scan_moves(plan, index * blocks, order, place, blocks)
+    begin = 0 if leaving else n_leaving
+    end = n_leaving if leaving else blocks
 
     def indices(i):
         at = (begin + 2 * i, jnp.minimum(begin + 2 * i + 1, end - 1))
         return [
-            pltpu.make_async_copy(links.at[order[at[u]]], near.at[u], sems.at[len(loads) + u]) for u in range(2)
+            pltpu.make_async_copy(links_in.at[order[at[u]]], near.at[u], sems.at[n_loads - 2 + u]) for u in range(2)
         ]
 
     steps = (end - begin + 1) // 2
@@ -302,7 +358,11 @@
     def _():
         start_all(indices(0))
 
-    wait_all(start_all([pltpu.make_async_copy(a, b, sems.at[i]) for i, (a, b) in enumerate(loads)]))
+    wait_all(loads[1:5])
+    face_rows(angle, scale, links, metric, coefs, blocks, elements)
+    if not leaving:
+        scan_origins(plan, index, scratch[3], blocks, devices)
+    wait_all(loads[5:])
     step = 16
     chunks = [slice(i * step, (i + 1) * step) for i in range(LANES // step)]
 
@@ -327,13 +387,20 @@
         for c in range(3):
             traces[c] = inner[c * LANES : (c + 1) * LANES]
         lower = lax.broadcasted_iota(jnp.int32, (16, LANES), 1) < elements
-        values = jnp.where(lower, coefs[both[0]], coefs[both[1]])
+        values = jnp.where(lower, coefs[pl.ds(both[0] * 16, 16), :], coefs[pl.ds(both[1] * 16, 16), :])
         rough = values.astype(jnp.bfloat16).astype(jnp.float32)
         stacked = jnp.concatenate([rough, values - rough], axis=0).astype(jnp.bfloat16)
         stacked = mm(eye[:, :LANES], stacked, ((1,), (1,))).astype(jnp.bfloat16)
         factors[...] = mm(stacked, spread[...])
 
         lane = lax.broadcasted_iota(jnp.int32, (step, LANES), 1)
+        inflow = []
+        for b in both:
+            row = jnp.zeros((1, LANES), jnp.float32)
+            for s in range(members):
+                level = breach[s, b].astype(jnp.float32)
+                row = jnp.where(lax.broadcasted_iota(jnp.int32, (1, LANES), 1) == 2 * comp + s, level, row)
+            inflow.append(row)
         for rows in chunks:
             n_x, n_y, scale, wall, rx, sx, ry, sy = (
                 factors[rows, q * LANES : (q + 1) * LANES] for q in range(8)
@@ -346,7 +413,7 @@
             cross = flow_y * speed_x
             flux_f = (flow_x, flow_x * speed_x + pressure, cross)
             flux_g = (flow_y, cross, flow_y * speed_y + pressure)
-            add = inflow[pl.ds(both[0] if rows.start < elements else both[1], 1), :]
+            add = inflow[rows.start // elements]
             for c in range(3):
                 along_r = rx * flux_f[c] + ry * flux_g[c]
                 along_s = sx * flux_f[c] + sy * flux_g[c]
@@ -417,7 +484,12 @@
         lax.fori_loop(0, end, finish, 0)
     else:
         wait_all(
-            start_all([pltpu.make_async_copy(scratch[1 + i], outs[i], sems.at[n_loads + i]) for i in range(2)])
+            start_all(
+                [
+                    pltpu.make_async_copy(a, outs[i], sems.at[n_loads + i])
+                    for i, a in enumerate((scratch[1], scratch[2], scratch[3].at[pl.ds(0, outs[2].shape[0])]))
+                ]
+            )
         )
 
 
@@ -433,19 +505,24 @@
             flow[b, s, 1:2, j * LANES : (j + 1) * LANES] = rows[2 * step + row : 2 * step + row + 1]
 
 
-def merge_kernel(source, arrives, got, depth_in, flow_in, depth_out, flow_out, depth, flow, came, sems, *, t, blocks):
+def merge_kernel(
+    origin_in, got, depth_in, flow_in, depth_out, flow_out, origin, depth, flow, came, sems, *, t, blocks
+):
     def arrival(b):
-        return pltpu.make_async_copy(got.at[source[b]], came.at[b], sems.at[b])
+        return pltpu.make_async_copy(got.at[origin[b]], came.at[b], sems.at[b])
 
     def leave(b):
         return pltpu.make_async_copy(flow.at[b], flow_out.at[b], sems.at[blocks + b])
 
     whole = pltpu.make_async_copy(depth_in, depth, sems.at[2 * blocks])
+    first = pltpu.make_async_copy(origin_in, origin, sems.at[2 * blocks + 1])
+    first.start()
     whole.start()
+    first.wait()
 
     def each(act):
         def one(b, carry):
-            @pl.when(arrives[b] == 1)
+            @pl.when(origin[b] >= 0)
             def _():
                 act(b)
 
@@ -496,10 +573,8 @@
     tiles = blocks // 8
     depth_rows = water_depth.reshape(tiles, 8, members, pairs, LANES).transpose(2, 0, 3, 1, 4).reshape(-1, LANES)
     flow_rows = momentum.transpose(0, 2, 1, 3)
-    links = face_map.reshape(-1)
-    faces = links.shape[0]
-    rim_list = rim_faces.reshape(-1)
-    width = rim_list.shape[0] // 2
+    faces = face_map.size
+    width = rim_faces.shape[1] // 2
     dma = pltpu.SemaphoreType.DMA
 
     back = jnp.asarray(np.tile(t["back"], (2, 1)), bf16)
@@ -512,44 +587,20 @@
             jax.ShapeDtypeStruct((width, LANES), f32),
             jax.ShapeDtypeStruct((width, LANES), f32),
         ),
-        1, 4,
+        0, 5,
         [
-            pltpu.VMEM(depth_rows.shape, f32), pltpu.VMEM(flow_rows.shape, f32), pltpu.VMEM(back.shape, bf16),
+            pltpu.SMEM(rim_faces.shape, jnp.int32), pltpu.VMEM(depth_rows.shape, f32), pltpu.VMEM(flow_rows.shape, f32), pltpu.VMEM(back.shape, bf16),
             pltpu.VMEM(eye.shape, bf16),
             pltpu.VMEM((blocks, 3 * comp, LANES), f32), pltpu.VMEM((faces, LANES), f32),
-            pltpu.VMEM((3 * LANES, 2 * LANES), bf16), dma((3 + tiles + blocks,)),
+            pltpu.VMEM((3 * LANES, 2 * LANES), bf16), dma((4 + tiles + blocks,)),
         ],
         (HBM, HBM, VMEM, VMEM),
-    )(rim_list, depth_rows, flow_rows, back, eye)
+    )(rim_faces, depth_rows, flow_rows, back, eye)
 
     count = lax.axis_size("mesh")
     before = lax.ppermute(tail, "mesh", [(i, i + 1) for i in range(count - 1)])
     after = lax.ppermute(head, "mesh", [(i + 1, i) for i in range(count - 1)])
 
-    own_index = lax.axis_index("mesh")
-    all_slots = block_plan.shape[0]
-    local_ids = jnp.arange(blocks, dtype=jnp.int32)
-    slot_ids = own_index * blocks + local_ids
-    targets = lax.dynamic_slice_in_dim(block_plan, own_index * blocks, blocks)
-    target_dev = targets // blocks
-    leaves = (target_dev != own_index).astype(jnp.int32)
-    every_slot = jnp.arange(all_slots, dtype=jnp.int32)
-    source = jnp.sum(jnp.where(block_plan[None, :] == slot_ids[:, None], every_slot[None, :], 0), axis=1)
-    source_dev = source // blocks
-    arrives = (source_dev != own_index).astype(jnp.int32)
-    n_leaving = jnp.sum(leaves)
-    earlier = local_ids[None, :] < local_ids[:, None]
-    rank_leave = jnp.sum(jnp.where(earlier, leaves[None, :], 0), axis=1)
-    rank = jnp.where(leaves == 1, rank_leave, n_leaving + local_ids - rank_leave)
-    order = jnp.sum(jnp.where(rank[None, :] == local_ids[:, None], local_ids[None, :], 0), axis=1)
-
-    walls = (links == jnp.arange(faces, dtype=jnp.int32)).astype(f32).reshape(blocks, 3, elements)
-    angles = face_angle.reshape(blocks, 3, elements)
-    coefs = jnp.concatenate(
-        [jnp.cos(angles), jnp.sin(angles), face_scale.reshape(blocks, 3, elements), walls, metric], axis=1
-    )
-    coefs = jnp.concatenate([coefs, coefs], axis=2)
-    inflow = jnp.pad(breach.astype(f32), ((0, 0), (2 * comp, LANES - 2 * comp - members)))
     lift_h, lift_l = high_low(t["lift"])
     matrix = np.concatenate(
         [t["along"][0], t["along"][0], t["along"][1], t["along"][1], lift_h.astype(np.float32), lift_h.astype(np.float32)],
@@ -563,21 +614,30 @@
 
     def finish(leaving, out_shape, extra, n_sems):
         return call(
-            functools.partial(finish_kernel, t=t, blocks=blocks, elements=elements, leaving=leaving),
+            functools.partial(
+                finish_kernel, t=t, blocks=blocks, elements=elements, leaving=leaving, devices=count
+            ),
             out_shape,
-            4, 12,
+            0, 16,
             [
+                pltpu.SMEM(block_plan.shape, jnp.int32), pltpu.SMEM(wet_blocks.shape, jnp.int32),
+                pltpu.SMEM((members, blocks), jnp.int32), pltpu.VMEM(face_map.shape, jnp.int32),
+                pltpu.VMEM(face_angle.shape, f32), pltpu.VMEM(face_scale.shape, f32), pltpu.VMEM(metric.shape, f32),
                 pltpu.VMEM((blocks, 3 * comp, LANES), f32), pltpu.VMEM((faces + 2 * width, LANES), f32),
-                pltpu.VMEM(coefs.shape, f32), pltpu.VMEM(inflow.shape, f32),
                 *[pltpu.VMEM(m.shape, bf16) for m in mats],
+                pltpu.SMEM((blocks,), jnp.int32), pltpu.SMEM((blocks,), jnp.int32),
+                pltpu.VMEM((blocks * 16, LANES), f32),
                 pltpu.VMEM((3, LANES, LANES), f32), pltpu.VMEM((3 * LANES, 2 * LANES), bf16),
                 pltpu.VMEM((3, LANES, LANES), f32), pltpu.VMEM((LANES, 8 * LANES), f32),
                 pltpu.VMEM((3 * LANES, LANES), f32), pltpu.VMEM((3, LANES, 6 * LANES), bf16),
                 pltpu.SMEM((2, face_map.shape[1]), jnp.int32),
-                *extra, dma((13 + n_sems,)),
+                *extra, dma((18 + n_sems,)),
             ],
             jax.tree.map(lambda _: HBM, out_shape),
-        )(order, target_dev, n_leaving.reshape(1), wet_blocks, face_map, fields, pool, before, after, coefs, inflow, *mats)
+        )(
+            block_plan, wet_blocks, breach.T, face_map, face_angle, face_scale, metric, fields, pool, before, after,
+            *mats,
+        )
 
     sent = finish(
         True, jax.ShapeDtypeStruct((count, packed, LANES), f32), [pltpu.VMEM((blocks, packed, LANES), f32)], blocks
@@ -585,15 +645,19 @@
     got = lax.all_to_all(sent, "mesh", split_axis=0, concat_axis=0, tiled=True)
     final = (jax.ShapeDtypeStruct(depth_rows.shape, f32), jax.ShapeDtypeStruct(flow_rows.shape, f32))
     whole = [pltpu.VMEM(depth_rows.shape, f32), pltpu.VMEM(flow_rows.shape, f32)]
-    kept = finish(False, final, [pltpu.VMEM((2, 3 * comp, LANES), f32), *whole], 2)
+    slots = LANES
+    depth_kept, flow_kept, origin = finish(
+        False, (*final, jax.ShapeDtypeStruct((slots,), jnp.int32)),
+        [pltpu.VMEM((2, 3 * comp, LANES), f32), *whole, pltpu.SMEM((slots,), jnp.int32)], 3,
+    )
     depth_new, flow_new = call(
         functools.partial(merge_kernel, t=t, blocks=blocks),
         final,
-        2, 3,
-        [*whole, pltpu.VMEM((blocks, packed, LANES), f32), dma((2 * blocks + 1,))],
+        0, 4,
+        [pltpu.SMEM((slots,), jnp.int32), *whole, pltpu.VMEM((blocks, packed, LANES), f32), dma((2 * blocks + 2,))],
         (HBM, HBM),
-        input_output_aliases={3: 0, 4: 1},
-    )(source_dev, arrives, got, *kept)
+        input_output_aliases={2: 0, 3: 1},
+    )(origin, got, depth_kept, flow_kept)
     depth_out = depth_new.reshape(members, tiles, pairs, 8, LANES).transpose(1, 3, 0, 2, 4).reshape(water_depth.shape)
     return depth_out, flow_new.transpose(0, 2, 1, 3)
 

time: 78 us -> 67.5 us (0.87)
  waiting for transfers between devices: 7.71 us -> 14.2 us
  Pallas kernels: 47.2 us -> 41.6 us
  other arithmetic: 4.95 us -> 0 us
  local copies, waits for them, and re-layouts: 4.52 us -> 0 us
  starting transfers between devices: 12.1 us -> 10.6 us
    ppermute x1, waiting for transfers between devices: 0.01 us -> 4.51 us  [body(): after = lax.ppermute(head, 'mesh', [(i + 1, i) for i in range(count - 1)])]
    pallas_call x1, Pallas kernels: 10.5 us -> 7.5 us  [body(): call(functools.partial(prepare_kernel, t=t, blocks=blocks, elements=eleme...]
    reduce_sum x4 -> x0, other arithmetic: 2.93 us -> none  [the longest x1 1.95 us: body(): n_leaving = jnp.sum(leaves)]
    pallas_call x2, Pallas kernels: 33 us -> 30.6 us  [finish(): call(functools.partial(finish_kernel, t=t, blocks=blocks, elements=elemen...]
    all_to_all x1, waiting for transfers between devices: 7.7 us -> 9.69 us  [body(): got = lax.all_to_all(sent, 'mesh', split_axis=0, concat_axis=0, tiled=True)]
    reshape x2 -> x0, local copies, waits for them, and re-layouts: 1.64 us -> none  [the longest x1 0.82 us: body(): links = face_map.reshape(-1)]
    all_to_all x1, starting transfers between devices: 6.46 us -> 4.93 us  [body(): got = lax.all_to_all(sent, 'mesh', split_axis=0, concat_axis=0, tiled=True)]
    concatenate x1 -> x0, local copies, waits for them, and re-layouts: 1.09 us -> none  [body(): jnp.concatenate([jnp.cos(angles), jnp.sin(angles), face_scale.reshape(blo...]
  transfers between devices with their start and end apart: 3 -> 3, of which waited for: 1 -> 2; matrix products, arithmetic and copies ran while one was open for 12% -> 0% of each run, Pallas kernels for 27% -> 29%
where the time goes in v2:
time: 67.5 us; the launch traced here: 67 us
  Pallas kernels  41.6 us (62%)
  waiting for transfers between devices  14.2 us (21%)
  starting transfers between devices  10.6 us (16%)
  between operations  0.68 us (1%)
    pallas_call x2, Pallas kernels, finish(): call(functools.partial(finish_kernel, t=t, blocks=blocks, elements=elemen...  30.6 us
    all_to_all x1, waiting for transfers between devices, body(): got = lax.all_to_all(sent, 'mesh', split_axis=0, concat_axis=0, tiled=True)  9.69 us
    pallas_call x1, Pallas kernels, body(): call(functools.partial(prepare_kernel, t=t, blocks=blocks, elements=eleme...  7.5 us
    all_to_all x1, starting transfers between devices, body(): got = lax.all_to_all(sent, 'mesh', split_axis=0, concat_axis=0, tiled=True)  4.93 us
    ppermute x1, waiting for transfers between devices, body(): after = lax.ppermute(head, 'mesh', [(i + 1, i) for i in range(count - 1)])  4.51 us
    ppermute x1, starting transfers between devices, body(): before = lax.ppermute(tail, 'mesh', [(i, i + 1) for i in range(count - 1)])  3.71 us
    pallas_call x1, Pallas kernels, body(): call(functools.partial(merge_kernel, t=t, blocks=blocks), final, 0, 4, [p...  3.55 us
    ppermute x1, starting transfers between devices, body(): after = lax.ppermute(head, 'mesh', [(i + 1, i) for i in range(count - 1)])  1.92 us
  transfers between devices with their start and end apart: 3, of which 2 were waited for; matrix products, arithmetic and copies ran while one was open for 0% of the time, Pallas kernels for 29%

profile of v2, /device:TPU:15, one launch (start us, length us, event | category | flops | bytes accessed | tf_op | source)
XLA Modules:
  0.0 67.0 jit_solution(5580333352288957081)
XLA Ops:
  0.6 7.5 %shard_map.167 = (f32[24,168,128]{2,1,0:T(8,128)}, f32[4608,128]{1,0:T(8,128)}, f32[64,128]{1,0:T(8,128)}, f32[64,128]{1,0:T(8,128)}) custom-call(s32[1,128]{1,0:T(1,128)} %rim_in.1, f32[1200,128]{1,0:T(8,128)} %bitcast.16, f32[24,10,2,640]{3,2,1,0:T(2,128)} %bitcast.14, bf16[256,128]{1,0:T(8,128)(2,1)} %constant.12.clone.back_in, ...), custom_call_target="tpu_custom_call" | custom-call | tf_op jit(solution)/shard_map/pallas_call | solution.py:582
  8.1 3.7 %collective-permute-start = (f32[64,128]{1,0:T(8,128)}, f32[64,128]{1,0:T(8,128)}, u32[]{:S(2)}, u32[]{:S(2)}) collective-permute-start(f32[64,128]{1,0:T(8,128)} %get-tuple-element.13), channel_id=1, source_target_pairs={{0,1},{1,2},{2,3},{3,4},{4,5},{5,6},{6,7},{7,8},{8,9},{9,10},{10,1... | collective-permute-start | bytes 98312 | tf_op jit(solution)/shard_map/ppermute | solution.py:601
  11.9 1.9 %collective-permute-start.1 = (f32[64,128]{1,0:T(8,128)}, f32[64,128]{1,0:T(8,128)}, u32[]{:S(2)}, u32[]{:S(2)}) collective-permute-start(f32[64,128]{1,0:T(8,128)} %get-tuple-element.14), channel_id=1, source_target_pairs={{1,0},{2,1},{3,2},{4,3},{5,4},{6,5},{7,6},{8,7},{9,8},{10,9},{11,1... | collective-permute-start | bytes 98312 | tf_op jit(solution)/shard_map/ppermute | solution.py:602
  13.8 0.0 collective-permute-done.before_in
  13.8 4.5 %collective-permute-done.1.after_in = f32[64,128]{1,0:T(8,128)} collective-permute-done((f32[64,128]{1,0:T(8,128)}, f32[64,128]{1,0:T(8,128)}, u32[]{:S(2)}, u32[]{:S(2)}) %collective-permute-start.1) | collective-permute-done | bytes 32800 | tf_op jit(solution)/shard_map/ppermute | solution.py:602
  18.3 11.0 %shard_map.169 = f32[16,152,128]{2,1,0:T(8,128)} custom-call(s32[384]{0:T(512)} %plan_in.3, s32[24]{0:T(128)} %wet_in.3, s32[10,24]{1,0:T(8,128)} %bitcast.17, s32[24,192]{1,0:T(8,128)} %links_in.3, f32[24,192]{1,0:T(8,128)} %angle_in.3, f32[24,192]{1,0:T(8,128)} %scale_in.3, f32[24,4,64]{2,1,0:T(4,128)} %metric_in.3, ...), custom_call_target="tpu_custom_call" | custom-call | tf_op jit(solution)/shard_map/pallas_call | solution.py:616
  29.3 4.9 %all-to-all-start = ((f32[16,152,128]{2,1,0:T(8,128)}), f32[16,152,128]{2,1,0:T(8,128)}, u32[]{:S(2)}, u32[]{:S(2)}) async-start(f32[16,152,128]{2,1,0:T(8,128)} %shard_map.169), calls=%async_computation | async-start | bytes 2490368 | tf_op jit(solution)/shard_map/all_to_all | solution.py:645
  34.2 19.6 %shard_map.168 = (f32[1200,128]{1,0:T(8,128)}, f32[24,10,2,640]{3,2,1,0:T(2,128)}, s32[128]{0:T(128)}) custom-call(s32[384]{0:T(512)} %plan_in.3, s32[24]{0:T(128)} %wet_in.3, s32[10,24]{1,0:T(8,128)} %bitcast.18, s32[24,192]{1,0:T(8,128)} %links_in.3, f32[24,192]{1,0:T(8,128)} %angle_in.3, f32[24,192]{1,0:T(8,128)} %scale_in.3, f32[24,4,64]{2,1,0:T(4,128)} %metric_in.3, ...), custom_call_target="tpu_custom_call" | custom-call | tf_op jit(solution)/shard_map/pallas_call | solution.py:616
  53.8 9.7 %all-to-all-done.got = f32[16,152,128]{2,1,0:T(8,128)} async-done(((f32[16,152,128]{2,1,0:T(8,128)}), f32[16,152,128]{2,1,0:T(8,128)}, u32[]{:S(2)}, u32[]{:S(2)}) %all-to-all-start) | async-done | bytes 1245216 | tf_op jit(solution)/shard_map/all_to_all | solution.py:645
  63.5 3.5 %shard_map.170 = (f32[1200,128]{1,0:T(8,128)}, f32[24,10,2,640]{3,2,1,0:T(2,128)}) custom-call(s32[128]{0:T(128)} %get-tuple-element.15.origin_in, f32[16,152,128]{2,1,0:T(8,128)} %all-to-all-done.got, f32[1200,128]{1,0:T(8,128)} %get-tuple-element.16.depth_in, ...), custom_call_target="tpu_custom_call", output_to_operand_aliasing={{0}: (2, {}), {1}: (3, {})} | custom-call | tf_op jit(solution)/shard_map/pallas_call | solution.py:653
Async XLA Ops:
  8.1 5.7 %collective-permute-start = (f32[64,128]{1,0:T(8,128)}, f32[64,128]{1,0:T(8,128)}, u32[]{:S(2)}, u32[]{:S(2)}) collective-permute-start(f32[64,128]{1,0:T(8,128)} %get-tuple-element.13), channel_id=1, source_target_pairs={{0,1},{1,2},{2,3},{3,4},{4,5},{5,6},{6,7},{7,8},{8,9},{9,10},{10,1... | collective-permute-start | bytes 98312 | tf_op jit(solution)/shard_map/ppermute | solution.py:601
  11.9 6.5 %collective-permute-start.1 = (f32[64,128]{1,0:T(8,128)}, f32[64,128]{1,0:T(8,128)}, u32[]{:S(2)}, u32[]{:S(2)}) collective-permute-start(f32[64,128]{1,0:T(8,128)} %get-tuple-element.14), channel_id=1, source_target_pairs={{1,0},{2,1},{3,2},{4,3},{5,4},{6,5},{7,6},{8,7},{9,8},{10,9},{11,1... | collective-permute-start | bytes 98312 | tf_op jit(solution)/shard_map/ppermute | solution.py:602
  29.3 34.2 %all-to-all-start = ((f32[16,152,128]{2,1,0:T(8,128)}), f32[16,152,128]{2,1,0:T(8,128)}, u32[]{:S(2)}, u32[]{:S(2)}) async-start(f32[16,152,128]{2,1,0:T(8,128)} %shard_map.169), calls=%async_computation | async-start | bytes 2490368 | tf_op jit(solution)/shard_map/all_to_all | solution.py:645

commit v3 on v2

--- a/solution.py
+++ b/solution.py
@@ -92,6 +92,7 @@
         return (n % 2) * comp + s * pairs + n // 2
 
     own = np.zeros((LANES, LANES), np.float32)
+    own[2 * comp, 3 * wide :] = 1.0
     back = np.zeros((LANES, LANES), np.float32)
     lift = np.zeros((2 * comp, LANES), np.float32)
     along = np.zeros((2, 2 * comp, LANES), np.float32)
@@ -113,7 +114,7 @@
     for q in range(4):
         for f in range(3):
             spread[3 * q + f, q * LANES + f * wide : q * LANES + (f + 1) * wide] = 1.0
-        spread[12 + q, (4 + q) * LANES : (5 + q) * LANES] = 1.0
+        spread[12 + q, (4 + q) * LANES : (4 + q) * LANES + 2 * comp] = 1.0
     return dict(
         own=own, back=back, lift=lift, along=along, spread=spread,
         comp=comp, pairs=pairs, used=used, wide=wide, nodes=nodes, members=members,
@@ -304,9 +305,9 @@
 def face_rows(angle, scale, links, metric, coefs, blocks, elements):
     shape = (blocks, 3 * elements)
     own = lax.broadcasted_iota(jnp.int32, shape, 0) * (3 * elements) + lax.broadcasted_iota(jnp.int32, shape, 1)
-    wall = jnp.where(links[...] == own, 1.0, 0.0)
+    free = jnp.where(links[...] == own, 0.0, 1.0)
     lower = lax.broadcasted_iota(jnp.int32, (blocks, LANES), 1) < elements
-    for q, value in enumerate((jnp.cos(angle[...]), jnp.sin(angle[...]), scale[...], wall)):
+    for q, value in enumerate((jnp.cos(angle[...]), jnp.sin(angle[...]), scale[...], free)):
         two = value[:, :LANES]
         swapped = swap_halves(two)
         third = value[:, LANES:]
@@ -320,16 +321,297 @@
         coefs[b * 16 + 12 : b * 16 + 16] = jnp.concatenate([factors, factors], axis=1)
 
 
+def spread_pair(coefs, both, eye, spread, factors, elements):
+    lower = lax.broadcasted_iota(jnp.int32, (16, LANES), 1) < elements
+    values = jnp.where(lower, coefs[pl.ds(both[0] * 16, 16), :], coefs[pl.ds(both[1] * 16, 16), :])
+    rough = values.astype(jnp.bfloat16).astype(jnp.float32)
+    stacked = jnp.concatenate([rough, values - rough], axis=0).astype(jnp.bfloat16)
+    stacked = mm(eye[:, :LANES], stacked, ((1,), (1,))).astype(jnp.bfloat16)
+    factors[...] = mm(stacked, spread[...])
+
+
+def inflow_rows(breach, both, t):
+    rows = []
+    for b in both:
+        row = jnp.zeros((1, LANES), jnp.float32)
+        for s in range(t["members"]):
+            level = breach[s, b].astype(jnp.float32)
+            row = jnp.where(lax.broadcasted_iota(jnp.int32, (1, LANES), 1) == 2 * t["comp"] + s, level, row)
+        rows.append(row)
+    return rows
+
+
+def volume_rows(rows, turned, factors, first, inflow, pieces):
+    rx, sx, ry, sy = (factors[rows, q * LANES : (q + 1) * LANES] for q in range(first, first + 4))
+    height, flow_x, flow_y = (turned[c, rows] for c in range(3))
+    pressure = 0.5 * gravity * height * height
+    inverse = 1.0 / height
+    speed_x = flow_x * inverse
+    speed_y = flow_y * inverse
+    cross = flow_y * speed_x
+    flux_f = (flow_x, flow_x * speed_x + pressure, cross)
+    flux_g = (flow_y, cross, flow_y * speed_y + pressure)
+    for c in range(3):
+        along_r = rx * flux_f[c] + ry * flux_g[c]
+        along_s = sx * flux_f[c] + sy * flux_g[c]
+        if c == 0:
+            along_r = along_r + inflow
+        pieces[c, rows, 0:LANES], pieces[c, rows, LANES : 2 * LANES] = split(along_r)
+        pieces[c, rows, 2 * LANES : 3 * LANES], pieces[c, rows, 3 * LANES : 4 * LANES] = split(along_s)
+
+
+def flux_rows(rows, traces, outer, factors, pieces, first, wide):
+    lane = lax.broadcasted_iota(jnp.int32, (rows.stop - rows.start, LANES), 1)
+    n_x, n_y, scale, free = (factors[rows, q * LANES : (q + 1) * LANES] for q in range(4))
+    theirs = [outer[f * LANES + rows.start : f * LANES + rows.stop] for f in range(3)]
+    height, flow_x, flow_y = (traces[c, rows] for c in range(3))
+    is_wall = free < 0.5
+    through = flow_x * n_x + flow_y * n_y
+    twice = through + through
+    height_o = jnp.where(is_wall, height, place_face(theirs, 0, wide, lane))
+    flow_xo = jnp.where(is_wall, flow_x - twice * n_x, place_face(theirs, 1, wide, lane))
+    flow_yo = jnp.where(is_wall, flow_y - twice * n_y, place_face(theirs, 2, wide, lane))
+    speed = through / height
+    speed_o = (flow_xo * n_x + flow_yo * n_y) / height_o
+    fast = jnp.maximum(
+        jnp.abs(speed) + root(gravity * height), jnp.abs(speed_o) + root(gravity * height_o)
+    )
+    ours, others = speed - fast, speed_o - fast
+    half = 0.5 * scale
+    push = 0.5 * gravity * (height * height - height_o * height_o)
+    jumps = (
+        half * (height * ours - height_o * others),
+        half * (flow_x * ours - flow_xo * others + push * n_x),
+        half * (flow_y * ours - flow_yo * others + push * n_y),
+    )
+    for c in range(3):
+        pieces[c, rows, first : first + LANES], pieces[c, rows, first + LANES : first + 2 * LANES] = split(jumps[c])
+
+
+def lift_mm(lift, low, pieces, c, first):
+    last = ((1,), (1,))
+    return mm(lift, pieces[c, :, : first + 2 * LANES], last) + mm(low[...], pieces[c, :, first : first + LANES], last)
+
+
+def pair_gains(tall, comp, elements):
+    narrow = lax.broadcasted_iota(jnp.int32, (comp, LANES), 1) < elements
+    even, odd = tall[:comp], tall[comp:]
+    return jnp.where(narrow, even, swap_halves(odd)), jnp.where(narrow, swap_halves(even), odd)
+
+
+def gather_pair(near, pool, outer, elements):
+    for u in range(2):
+        for f in range(3):
+            for e in range(elements):
+                row = f * LANES + u * elements + e
+                outer[row : row + 1, :] = pool[pl.ds(near[u, f * elements + e], 1), :]
+
+
+def row_chunks(step):
+    return [slice(i * step, (i + 1) * step) for i in range(LANES // step)]
+
+
+def volume_kernel(
+    plan_in, wet_in, breach_in, links_in, angle_in, scale_in, metric_in, fields_in, own_in, spread_in, matrix_in,
+    eye_in, base_out, traces_out, coefs_out, near_out, facts_out,
+    plan, wet, breach, links, angle, scale, metric, own, spread, matrix, eye,
+    order, facts, coefs, fields, turned, halves, traces, factors, pieces, base, sems, *, t, blocks, elements,
+):
+    comp = t["comp"]
+    loads = [
+        (plan_in, plan), (angle_in, angle), (scale_in, scale), (links_in, links), (metric_in, metric),
+        (wet_in, wet), (breach_in, breach), (eye_in, eye), (own_in, own), (spread_in, spread), (matrix_in, matrix),
+    ]
+    n = len(loads)
+    loads = start_all([pltpu.make_async_copy(a, b, sems.at[i]) for i, (a, b) in enumerate(loads)])
+    index = lax.axis_index("mesh")
+    loads[0].wait()
+    loads[5].wait()
+    end = scan_moves(plan, index * blocks, order, facts, blocks)
+
+    def fetch(p):
+        return pltpu.make_async_copy(fields_in.at[order[p]], fields.at[p], sems.at[n + p])
+
+    def relay(p):
+        return pltpu.make_async_copy(
+            links_in.at[order[jnp.minimum(p, end - 1)]], near_out.at[p], sems.at[n + blocks + p]
+        )
+
+    def keep(p):
+        return pltpu.make_async_copy(base.at[p], base_out.at[p], sems.at[n + 2 * blocks + p])
+
+    def hold(i):
+        return pltpu.make_async_copy(traces.at[i], traces_out.at[i], sems.at[n + 3 * blocks + i])
+
+    def each(stop, act):
+        def one(p, carry):
+            act(p)
+            return carry
+
+        lax.fori_loop(0, stop, one, 0)
+
+    steps = (end + 1) // 2
+    each(end, lambda p: fetch(p).start())
+    each(2 * steps, lambda p: relay(p).start())
+    wait_all(loads[1:5])
+    face_rows(angle, scale, links, metric, coefs, blocks, elements)
+
+    def describe(p):
+        facts[2 * blocks + p] = wet[order[p]]
+        facts[3 * blocks + p] = facts[order[p]]
+
+    facts[4 * blocks] = end
+    each(end, describe)
+    extra = start_all(
+        [
+            pltpu.make_async_copy(facts, facts_out, sems.at[n + 4 * blocks]),
+        ]
+    )
+    wait_all(loads[6:])
+
+    def one(i, carry):
+        at = (2 * i, jnp.minimum(2 * i + 1, end - 1))
+        both = (order[at[0]], order[at[1]])
+        fetch(at[0]).wait()
+
+        @pl.when(2 * i + 1 < end)
+        def _():
+            fetch(at[1]).wait()
+
+        turn_pair(fields, at[0], at[1], eye, turned, halves, comp)
+        inner = mm(halves[...], own[...])
+        for c in range(3):
+            traces[i, c] = inner[c * LANES : (c + 1) * LANES]
+        lower = lax.broadcasted_iota(jnp.int32, (16, LANES), 1) < elements
+        values = jnp.where(lower, coefs[pl.ds(both[0] * 16, 16), :], coefs[pl.ds(both[1] * 16, 16), :])
+        coefs_pair = pl.ds(blocks * 16 + i * 16, 16)
+        coefs[coefs_pair, :] = values
+        spread_pair(coefs, both, eye, spread, factors, elements)
+        inflow = inflow_rows(breach, both, t)
+        for rows in row_chunks(16):
+            volume_rows(rows, turned, factors, 0, inflow[rows.start // elements], pieces)
+        for c in range(3):
+            gains = pair_gains(mm(matrix[...], pieces[c], ((1,), (1,))), comp, elements)
+            for u in range(2):
+                rate = time_step * wet[both[u]].astype(jnp.float32)
+                span = slice(c * comp, (c + 1) * comp)
+                base[at[u], span] = fields[at[u], span] + rate * gains[u]
+        hold(i).start()
+        keep(at[0]).start()
+
+        @pl.when(2 * i + 1 < end)
+        def _():
+            keep(at[1]).start()
+
+        return carry
+
+    lax.fori_loop(0, steps, one, 0)
+    spare = pltpu.make_async_copy(
+        coefs.at[pl.ds(blocks * 16, blocks * 8)], coefs_out, sems.at[n + 4 * blocks + 1]
+    )
+    spare.start()
+
+    each(end, lambda p: keep(p).wait())
+    each(2 * steps, lambda p: relay(p).wait())
+    each(steps, lambda i: hold(i).wait())
+    wait_all(extra)
+    spare.wait()
+
+
+def face_kernel(
+    facts_in, near_in, pool_in, before_in, after_in, base_in, traces_in, coefs_in, spread_in, matrix_in, low_in, eye_in,
+    sent, facts, near, pool, base, traces, coefs, spread, matrix, low, eye, factors, outer, pieces, staged, sems,
+    *, t, blocks, elements,
+):
+    comp, wide, used = t["comp"], t["wide"], t["used"]
+    faces = blocks * 3 * elements
+    width = before_in.shape[0]
+    loads = [
+        (facts_in, facts), (near_in.at[pl.ds(0, 2)], near), (coefs_in, coefs), (eye_in, eye), (spread_in, spread),
+        (pool_in, pool.at[pl.ds(0, faces)]), (before_in, pool.at[pl.ds(faces, width)]),
+        (after_in, pool.at[pl.ds(faces + width, width)]), (matrix_in, matrix), (low_in, low),
+    ]
+    n = len(loads)
+    loads = start_all([pltpu.make_async_copy(a, b, sems.at[i]) for i, (a, b) in enumerate(loads)])
+    loads[0].wait()
+    end = facts[4 * blocks]
+    steps = (end + 1) // 2
+
+    def indices(i):
+        return pltpu.make_async_copy(near_in.at[pl.ds(2 * i, 2)], near, sems.at[1])
+
+    def get_base(p):
+        return pltpu.make_async_copy(base_in.at[p], base.at[p], sems.at[n + p])
+
+    def get_traces(i):
+        return pltpu.make_async_copy(traces_in.at[i], traces.at[i], sems.at[n + blocks + i])
+
+    def send(p):
+        return pltpu.make_async_copy(
+            staged.at[p], sent.at[facts[3 * blocks + p]], sems.at[n + 2 * blocks + p]
+        )
+
+    def each(stop, act):
+        def one(p, carry):
+            act(p)
+            return carry
+
+        lax.fori_loop(0, stop, one, 0)
+
+    each(steps, lambda i: get_traces(i).start())
+    each(end, lambda p: get_base(p).start())
+    wait_all(loads[1:])
+
+    def one(i, carry):
+        at = (2 * i, jnp.minimum(2 * i + 1, end - 1))
+
+        @pl.when(i > 0)
+        def _():
+            indices(i).wait()
+
+        get_traces(i).wait()
+        get_base(at[0]).wait()
+
+        @pl.when(2 * i + 1 < end)
+        def _():
+            get_base(at[1]).wait()
+
+        gather_pair(near, pool, outer, elements)
+
+        @pl.when(i + 1 < steps)
+        def _():
+            indices(i + 1).start()
+
+        spread_pair(coefs, (i, i), eye, spread, factors, elements)
+        for rows in row_chunks(16):
+            flux_rows(rows, traces.at[i], outer, factors, pieces, 0, wide)
+        for c in range(3):
+            gains = pair_gains(lift_mm(matrix[...], low, pieces, c, 0), comp, elements)
+            for u in range(2):
+                rate = time_step * facts[2 * blocks + at[u]].astype(jnp.float32)
+                done = base[at[u], c * comp : (c + 1) * comp] + rate * gains[u]
+                staged[at[u], c * used : (c + 1) * used] = done[:used]
+        send(at[0]).start()
+
+        @pl.when(2 * i + 1 < end)
+        def _():
+            send(at[1]).start()
+
+        return carry
+
+    lax.fori_loop(0, steps, one, 0)
+    each(end, lambda p: send(p).wait())
+
+
 def finish_kernel(
     plan_in, wet_in, breach_in, links_in, angle_in, scale_in, metric_in,
     fields_in, pool_in, before_in, after_in, own_in, spread_in, matrix_in, low_in, eye_in,
-    *rest, t, blocks, elements, leaving, devices,
+    depth_out, flow_out, origin_out,
+    plan, wet, breach, links, angle, scale, metric, fields, pool, own, spread, matrix, low, eye,
+    order, place, coefs, turned, halves, traces, factors, outer, pieces, near, staged, depth, flow, origin, sems,
+    *, t, blocks, elements, devices,
 ):
-    outs, scratch = (rest[:1], rest[1:]) if leaving else (rest[:3], rest[3:])
-    plan, wet, breach, links, angle, scale, metric, fields, pool, own, spread, matrix, low, eye, *scratch = scratch
-    order, place, coefs, turned, halves, traces, factors, outer, pieces, near, *scratch = scratch
-    staged, sems = scratch[0], scratch[-1]
-    comp, pairs, members, wide, used = t["comp"], t["pairs"], t["members"], t["wide"], t["used"]
+    comp, wide = t["comp"], t["wide"]
     faces = blocks * 3 * elements
     width = before_in.shape[0]
     loads = [
@@ -338,19 +620,16 @@
         (pool_in, pool.at[pl.ds(0, faces)]), (before_in, pool.at[pl.ds(faces, width)]),
         (after_in, pool.at[pl.ds(faces + width, width)]), (spread_in, spread), (matrix_in, matrix), (low_in, low),
     ]
-    n_loads = len(loads) + 2
+    n = len(loads)
     loads = start_all([pltpu.make_async_copy(a, b, sems.at[i]) for i, (a, b) in enumerate(loads)])
     index = lax.axis_index("mesh")
     loads[0].wait()
-    n_leaving = scan_moves(plan, index * blocks, order, place, blocks)
-    begin = 0 if leaving else n_leaving
-    end = n_leaving if leaving else blocks
+    begin = scan_moves(plan, index * blocks, order, place, blocks)
+    end = blocks
 
     def indices(i):
         at = (begin + 2 * i, jnp.minimum(begin + 2 * i + 1, end - 1))
-        return [
-            pltpu.make_async_copy(links_in.at[order[at[u]]], near.at[u], sems.at[n_loads - 2 + u]) for u in range(2)
-        ]
+        return [pltpu.make_async_copy(links_in.at[order[at[u]]], near.at[u], sems.at[n + u]) for u in range(2)]
 
     steps = (end - begin + 1) // 2
 
@@ -360,23 +639,13 @@
 
     wait_all(loads[1:5])
     face_rows(angle, scale, links, metric, coefs, blocks, elements)
-    if not leaving:
-        scan_origins(plan, index, scratch[3], blocks, devices)
+    scan_origins(plan, index, origin, blocks, devices)
     wait_all(loads[5:])
-    step = 16
-    chunks = [slice(i * step, (i + 1) * step) for i in range(LANES // step)]
 
     def one(i, carry):
-        at = (begin + 2 * i, jnp.minimum(begin + 2 * i + 1, end - 1))
-        both = (order[at[0]], order[at[1]])
-
+        both = (order[begin + 2 * i], order[jnp.minimum(begin + 2 * i + 1, end - 1)])
         wait_all(indices(i))
-        for u in range(2):
-            for f in range(3):
-                for e in range(elements):
-                    v = near[u, f * elements + e]
-                    row = f * LANES + u * elements + e
-                    outer[row : row + 1, :] = pool[pl.ds(v, 1), :]
+        gather_pair(near, pool, outer, elements)
 
         @pl.when(i + 1 < steps)
         def _():
@@ -386,111 +655,24 @@
         inner = mm(halves[...], own[...])
         for c in range(3):
             traces[c] = inner[c * LANES : (c + 1) * LANES]
-        lower = lax.broadcasted_iota(jnp.int32, (16, LANES), 1) < elements
-        values = jnp.where(lower, coefs[pl.ds(both[0] * 16, 16), :], coefs[pl.ds(both[1] * 16, 16), :])
-        rough = values.astype(jnp.bfloat16).astype(jnp.float32)
-        stacked = jnp.concatenate([rough, values - rough], axis=0).astype(jnp.bfloat16)
-        stacked = mm(eye[:, :LANES], stacked, ((1,), (1,))).astype(jnp.bfloat16)
-        factors[...] = mm(stacked, spread[...])
-
-        lane = lax.broadcasted_iota(jnp.int32, (step, LANES), 1)
-        inflow = []
-        for b in both:
-            row = jnp.zeros((1, LANES), jnp.float32)
-            for s in range(members):
-                level = breach[s, b].astype(jnp.float32)
-                row = jnp.where(lax.broadcasted_iota(jnp.int32, (1, LANES), 1) == 2 * comp + s, level, row)
-            inflow.append(row)
-        for rows in chunks:
-            n_x, n_y, scale, wall, rx, sx, ry, sy = (
-                factors[rows, q * LANES : (q + 1) * LANES] for q in range(8)
-            )
-            height, flow_x, flow_y = (turned[c, rows] for c in range(3))
-            pressure = 0.5 * gravity * height * height
-            inverse = 1.0 / height
-            speed_x = flow_x * inverse
-            speed_y = flow_y * inverse
-            cross = flow_y * speed_x
-            flux_f = (flow_x, flow_x * speed_x + pressure, cross)
-            flux_g = (flow_y, cross, flow_y * speed_y + pressure)
-            add = inflow[rows.start // elements]
-            for c in range(3):
-                along_r = rx * flux_f[c] + ry * flux_g[c]
-                along_s = sx * flux_f[c] + sy * flux_g[c]
-                along_r = jnp.where(lane < 2 * comp, along_r, add if c == 0 else 0.0)
-                pieces[c, rows, 0:LANES], pieces[c, rows, LANES : 2 * LANES] = split(along_r)
-                pieces[c, rows, 2 * LANES : 3 * LANES], pieces[c, rows, 3 * LANES : 4 * LANES] = split(along_s)
-
-            live = lane < 3 * wide
-            theirs = [outer[f * LANES + rows.start : f * LANES + rows.stop] for f in range(3)]
-            height = jnp.where(live, traces[0, rows], 1.0)
-            flow_x, flow_y = traces[1, rows], traces[2, rows]
-            is_wall = wall > 0.5
-            through = flow_x * n_x + flow_y * n_y
-            height_o = jnp.where(live, jnp.where(is_wall, height, place_face(theirs, 0, wide, lane)), 1.0)
-            flow_xo = jnp.where(is_wall, flow_x - 2.0 * through * n_x, place_face(theirs, 1, wide, lane))
-            flow_yo = jnp.where(is_wall, flow_y - 2.0 * through * n_y, place_face(theirs, 2, wide, lane))
-            through_o = flow_xo * n_x + flow_yo * n_y
-            speed = through / height
-            speed_o = through_o / height_o
-            fast = jnp.maximum(
-                jnp.abs(speed) + root(gravity * height), jnp.abs(speed_o) + root(gravity * height_o)
-            )
-            push = 0.5 * gravity * (height * height - height_o * height_o)
-            half = 0.5 * scale
-            jumps = (
-                half * (through - through_o + fast * (height_o - height)),
-                half * (flow_x * speed - flow_xo * speed_o + push * n_x + fast * (flow_xo - flow_x)),
-                half * (flow_y * speed - flow_yo * speed_o + push * n_y + fast * (flow_yo - flow_y)),
-            )
-            for c in range(3):
-                jump = jnp.where(live, jumps[c], 0.0)
-                pieces[c, rows, 4 * LANES : 5 * LANES], pieces[c, rows, 5 * LANES : 6 * LANES] = split(jump)
-
-        rates = [time_step * wet[b].astype(jnp.float32) for b in both]
-        last = ((1,), (1,))
-        narrow = lax.broadcasted_iota(jnp.int32, (comp, LANES), 1) < elements
+        spread_pair(coefs, both, eye, spread, factors, elements)
+        inflow = inflow_rows(breach, both, t)
+        for rows in row_chunks(16):
+            volume_rows(rows, turned, factors, 4, inflow[rows.start // elements], pieces)
+            flux_rows(rows, traces, outer, factors, pieces, 4 * LANES, wide)
         for c in range(3):
-            tall = mm(matrix[...], pieces[c], last) + mm(low[...], pieces[c, :, 4 * LANES : 5 * LANES], last)
-            even, odd = tall[:comp], tall[comp:]
-            gains = (jnp.where(narrow, even, swap_halves(odd)), jnp.where(narrow, swap_halves(even), odd))
+            gains = pair_gains(lift_mm(matrix[...], low, pieces, c, 4 * LANES), comp, elements)
             for u in range(2):
-                done = fields[both[u], c * comp : (c + 1) * comp] + rates[u] * gains[u]
-                if leaving:
-                    staged[at[u], c * used : (c + 1) * used] = done[:used]
-                else:
-                    staged[u, c * comp : (c + 1) * comp] = done
-
-        if leaving:
-            for u in range(2):
-
-                @pl.when(begin + 2 * i + u < end)
-                def _():
-                    pltpu.make_async_copy(
-                        staged.at[at[u]], outs[0].at[place[both[u]]], sems.at[n_loads + at[u]]
-                    ).start()
-        else:
-            for u in range(2):
-                write_block(both[u], staged.at[u], comp, scratch[1], scratch[2], t, blocks)
+                span = slice(c * comp, (c + 1) * comp)
+                rate = time_step * wet[both[u]].astype(jnp.float32)
+                staged[u, span] = fields[both[u], span] + rate * gains[u]
+        for u in range(2):
+            write_block(both[u], staged.at[u], comp, depth, flow, t, blocks)
         return carry
 
     lax.fori_loop(0, steps, one, 0)
-    if leaving:
-
-        def finish(i, carry):
-            pltpu.make_async_copy(staged.at[i], outs[0].at[place[order[i]]], sems.at[n_loads + i]).wait()
-            return carry
-
-        lax.fori_loop(0, end, finish, 0)
-    else:
-        wait_all(
-            start_all(
-                [
-                    pltpu.make_async_copy(a, outs[i], sems.at[n_loads + i])
-                    for i, a in enumerate((scratch[1], scratch[2], scratch[3].at[pl.ds(0, outs[2].shape[0])]))
-                ]
-            )
-        )
+    kept = ((depth, depth_out), (flow, flow_out), (origin.at[pl.ds(0, origin_out.shape[0])], origin_out))
+    wait_all(start_all([pltpu.make_async_copy(a, b, sems.at[n + i]) for i, (a, b) in enumerate(kept)]))
 
 
 def write_block(b, rows, step, depth, flow, t, blocks):
@@ -612,43 +794,78 @@
     ]
     packed = round_up(3 * used, 8)
 
-    def finish(leaving, out_shape, extra, n_sems):
-        return call(
-            functools.partial(
-                finish_kernel, t=t, blocks=blocks, elements=elements, leaving=leaving, devices=count
-            ),
-            out_shape,
-            0, 16,
-            [
-                pltpu.SMEM(block_plan.shape, jnp.int32), pltpu.SMEM(wet_blocks.shape, jnp.int32),
-                pltpu.SMEM((members, blocks), jnp.int32), pltpu.VMEM(face_map.shape, jnp.int32),
-                pltpu.VMEM(face_angle.shape, f32), pltpu.VMEM(face_scale.shape, f32), pltpu.VMEM(metric.shape, f32),
-                pltpu.VMEM((blocks, 3 * comp, LANES), f32), pltpu.VMEM((faces + 2 * width, LANES), f32),
-                *[pltpu.VMEM(m.shape, bf16) for m in mats],
-                pltpu.SMEM((blocks,), jnp.int32), pltpu.SMEM((blocks,), jnp.int32),
-                pltpu.VMEM((blocks * 16, LANES), f32),
-                pltpu.VMEM((3, LANES, LANES), f32), pltpu.VMEM((3 * LANES, 2 * LANES), bf16),
-                pltpu.VMEM((3, LANES, LANES), f32), pltpu.VMEM((LANES, 8 * LANES), f32),
-                pltpu.VMEM((3 * LANES, LANES), f32), pltpu.VMEM((3, LANES, 6 * LANES), bf16),
-                pltpu.SMEM((2, face_map.shape[1]), jnp.int32),
-                *extra, dma((18 + n_sems,)),
-            ],
-            jax.tree.map(lambda _: HBM, out_shape),
-        )(
-            block_plan, wet_blocks, breach.T, face_map, face_angle, face_scale, metric, fields, pool, before, after,
-            *mats,
-        )
-
-    sent = finish(
-        True, jax.ShapeDtypeStruct((count, packed, LANES), f32), [pltpu.VMEM((blocks, packed, LANES), f32)], blocks
-    )
+    own_mat, spread_mat, full_mat, low_mat = mats[:4]
+    face_cols, volume_cols = spread_mat[:, : 4 * LANES], spread_mat[:, 4 * LANES :]
+    volume_mat, lift_mat = full_mat[:, : 4 * LANES], full_mat[:, 4 * LANES :]
+    i32 = jnp.int32
+    tables = [
+        pltpu.SMEM(block_plan.shape, i32), pltpu.SMEM(wet_blocks.shape, i32), pltpu.SMEM((members, blocks), i32),
+        pltpu.VMEM(face_map.shape, i32), pltpu.VMEM(face_angle.shape, f32), pltpu.VMEM(face_scale.shape, f32),
+        pltpu.VMEM(metric.shape, f32),
+    ]
+    rows_of = (3 * comp, LANES)
+    base, traces, coefs, near, facts = call(
+        functools.partial(volume_kernel, t=t, blocks=blocks, elements=elements),
+        (
+            jax.ShapeDtypeStruct((blocks, *rows_of), f32),
+            jax.ShapeDtypeStruct((blocks // 2, 3, LANES, LANES), f32),
+            jax.ShapeDtypeStruct((blocks * 8, LANES), f32),
+            jax.ShapeDtypeStruct(face_map.shape, i32),
+            jax.ShapeDtypeStruct((LANES,), i32),
+        ),
+        0, 12,
+        [
+            *tables, pltpu.VMEM(own_mat.shape, bf16), pltpu.VMEM(volume_cols.shape, bf16),
+            pltpu.VMEM(volume_mat.shape, bf16), pltpu.VMEM(eye.shape, bf16),
+            pltpu.SMEM((blocks,), i32), pltpu.SMEM((LANES,), i32), pltpu.VMEM((blocks * 24, LANES), f32),
+            pltpu.VMEM((blocks, *rows_of), f32), pltpu.VMEM((3, LANES, LANES), f32),
+            pltpu.VMEM((3 * LANES, 2 * LANES), bf16), pltpu.VMEM((blocks // 2, 3, LANES, LANES), f32),
+            pltpu.VMEM((LANES, 4 * LANES), f32), pltpu.VMEM((3, LANES, 4 * LANES), bf16),
+            pltpu.VMEM((blocks, *rows_of), f32), dma((11 + 5 * blocks,)),
+        ],
+        (HBM,) * 5,
+    )(
+        block_plan, wet_blocks, breach.T, face_map, face_angle, face_scale, metric, fields,
+        own_mat, volume_cols, volume_mat, eye,
+    )
+    sent = call(
+        functools.partial(face_kernel, t=t, blocks=blocks, elements=elements),
+        jax.ShapeDtypeStruct((count, packed, LANES), f32),
+        0, 12,
+        [
+            pltpu.SMEM((LANES,), i32), pltpu.SMEM((2, face_map.shape[1]), i32),
+            pltpu.VMEM((faces + 2 * width, LANES), f32), pltpu.VMEM((blocks, *rows_of), f32),
+            pltpu.VMEM((blocks // 2, 3, LANES, LANES), f32), pltpu.VMEM((blocks * 8, LANES), f32),
+            pltpu.VMEM(face_cols.shape, bf16), pltpu.VMEM(lift_mat.shape, bf16), pltpu.VMEM(low_mat.shape, bf16),
+            pltpu.VMEM(eye.shape, bf16), pltpu.VMEM((LANES, 4 * LANES), f32), pltpu.VMEM((3 * LANES, LANES), f32),
+            pltpu.VMEM((3, LANES, 2 * LANES), bf16), pltpu.VMEM((blocks, packed, LANES), f32),
+            dma((10 + 3 * blocks,)),
+        ],
+        HBM,
+    )(facts, near, pool, before, after, base, traces, coefs, face_cols, lift_mat, low_mat, eye)
     got = lax.all_to_all(sent, "mesh", split_axis=0, concat_axis=0, tiled=True)
     final = (jax.ShapeDtypeStruct(depth_rows.shape, f32), jax.ShapeDtypeStruct(flow_rows.shape, f32))
     whole = [pltpu.VMEM(depth_rows.shape, f32), pltpu.VMEM(flow_rows.shape, f32)]
     slots = LANES
-    depth_kept, flow_kept, origin = finish(
-        False, (*final, jax.ShapeDtypeStruct((slots,), jnp.int32)),
-        [pltpu.VMEM((2, 3 * comp, LANES), f32), *whole, pltpu.SMEM((slots,), jnp.int32)], 3,
+    depth_kept, flow_kept, origin = call(
+        functools.partial(finish_kernel, t=t, blocks=blocks, elements=elements, devices=count),
+        (*final, jax.ShapeDtypeStruct((slots,), i32)),
+        0, 16,
+        [
+            *tables, pltpu.VMEM((blocks, *rows_of), f32), pltpu.VMEM((faces + 2 * width, LANES), f32),
+            *[pltpu.VMEM(m.shape, bf16) for m in mats],
+            pltpu.SMEM((blocks,), i32), pltpu.SMEM((blocks,), i32),
+            pltpu.VMEM((blocks * 16, LANES), f32),
+            pltpu.VMEM((3, LANES, LANES), f32), pltpu.VMEM((3 * LANES, 2 * LANES), bf16),
+            pltpu.VMEM((3, LANES, LANES), f32), pltpu.VMEM((LANES, 8 * LANES), f32),
+            pltpu.VMEM((3 * LANES, LANES), f32), pltpu.VMEM((3, LANES, 6 * LANES), bf16),
+            pltpu.SMEM((2, face_map.shape[1]), i32),
+            pltpu.VMEM((2, *rows_of), f32), *whole, pltpu.SMEM((slots,), i32), dma((19,)),
+        ],
+        (HBM,) * 3,
+    )(
+        block_plan, wet_blocks, breach.T, face_map, face_angle, face_scale, metric, fields, pool, before, after,
+        *mats,
     )
     depth_new, flow_new = call(
         functools.partial(merge_kernel, t=t, blocks=blocks),

time: 67.5 us -> 70 us (1.037)
  Pallas kernels: 41.6 us -> 46.7 us
  waiting for transfers between devices: 14.2 us -> 9.93 us
  starting transfers between devices: 10.6 us -> 12.1 us
    pallas_call x2 -> x3, Pallas kernels: 30.6 us -> 35.7 us  [the longest x1 19.3 us: body(): call(functools.partial(finish_kernel, t=t, blocks=blocks, elements=elemen...]
    ppermute x1, waiting for transfers between devices: 4.51 us -> 0.01 us  [body(): after = lax.ppermute(head, 'mesh', [(i + 1, i) for i in range(count - 1)])]
    all_to_all x1, starting transfers between devices: 4.93 us -> 6.46 us  [body(): got = lax.all_to_all(sent, 'mesh', split_axis=0, concat_axis=0, tiled=True)]
  transfers between devices with their start and end apart: 3 -> 3, of which waited for: 2 -> 1; matrix products, arithmetic and copies ran while one was open for 0% -> 0% of each run, Pallas kernels for 29% -> 39%
where the time goes in v3:
time: 70 us; the launch traced here: 69.4 us
  Pallas kernels  46.7 us (67%)
  starting transfers between devices  12.1 us (17%)
  waiting for transfers between devices  9.93 us (14%)
    pallas_call x1, Pallas kernels, body(): call(functools.partial(finish_kernel, t=t, blocks=blocks, elements=elemen...  19.3 us
    all_to_all x1, waiting for transfers between devices, body(): got = lax.all_to_all(sent, 'mesh', split_axis=0, concat_axis=0, tiled=True)  9.93 us
    pallas_call x1, Pallas kernels, body(): call(functools.partial(face_kernel, t=t, blocks=blocks, elements=elements...  8.58 us
    pallas_call x1, Pallas kernels, body(): call(functools.partial(volume_kernel, t=t, blocks=blocks, elements=elemen...  7.75 us
    pallas_call x1, Pallas kernels, body(): call(functools.partial(prepare_kernel, t=t, blocks=blocks, elements=eleme...  7.48 us
    all_to_all x1, starting transfers between devices, body(): got = lax.all_to_all(sent, 'mesh', split_axis=0, concat_axis=0, tiled=True)  6.46 us
    ppermute x1, starting transfers between devices, body(): before = lax.ppermute(tail, 'mesh', [(i, i + 1) for i in range(count - 1)])  3.71 us
    pallas_call x1, Pallas kernels, body(): call(functools.partial(merge_kernel, t=t, blocks=blocks), final, 0, 4, [p...  3.56 us
  transfers between devices with their start and end apart: 3, of which 1 were waited for; matrix products, arithmetic and copies ran while one was open for 0% of the time, Pallas kernels for 39%

profile of v3, /device:TPU:15, one launch (start us, length us, event | category | flops | bytes accessed | tf_op | source)
XLA Modules:
  0.0 69.4 jit_solution(7111533386068576605)
XLA Ops:
  0.6 7.5 %shard_map.167 = (f32[24,168,128]{2,1,0:T(8,128)}, f32[4608,128]{1,0:T(8,128)}, f32[64,128]{1,0:T(8,128)}, f32[64,128]{1,0:T(8,128)}) custom-call(s32[1,128]{1,0:T(1,128)} %rim_in.1, f32[1200,128]{1,0:T(8,128)} %bitcast.16, f32[24,10,2,640]{3,2,1,0:T(2,128)} %bitcast.14, bf16[256,128]{1,0:T(8,128)(2,1)} %constant.12.clone.back_in, ...), custom_call_target="tpu_custom_call" | custom-call | tf_op jit(solution)/shard_map/pallas_call | solution.py:764
  8.1 3.7 %collective-permute-start = (f32[64,128]{1,0:T(8,128)}, f32[64,128]{1,0:T(8,128)}, u32[]{:S(2)}, u32[]{:S(2)}) collective-permute-start(f32[64,128]{1,0:T(8,128)} %get-tuple-element.18), channel_id=1, source_target_pairs={{0,1},{1,2},{2,3},{3,4},{4,5},{5,6},{6,7},{7,8},{8,9},{9,10},{10,1... | collective-permute-start | bytes 98312 | tf_op jit(solution)/shard_map/ppermute | solution.py:783
  11.8 1.9 %collective-permute-start.1 = (f32[64,128]{1,0:T(8,128)}, f32[64,128]{1,0:T(8,128)}, u32[]{:S(2)}, u32[]{:S(2)}) collective-permute-start(f32[64,128]{1,0:T(8,128)} %get-tuple-element.19), channel_id=1, source_target_pairs={{1,0},{2,1},{3,2},{4,3},{5,4},{6,5},{7,6},{8,7},{9,8},{10,9},{11,1... | collective-permute-start | bytes 98312 | tf_op jit(solution)/shard_map/ppermute | solution.py:784
  13.8 7.7 %shard_map.169 = (f32[24,168,128]{2,1,0:T(8,128)}, f32[12,3,128,128]{3,2,1,0:T(8,128)}, f32[192,128]{1,0:T(8,128)}, s32[24,192]{1,0:T(8,128)}, s32[128]{0:T(128)}) custom-call(s32[384]{0:T(512)} %plan_in.3, s32[24]{0:T(128)} %wet_in.3, s32[10,24]{1,0:T(8,128)} %bitcast.17, s32[24,192]{1,0:T(8,128)} %links_in.3, f32[24,192]{1,0:T(8,128)} %angle_in.3, ...), custom_call_target="tpu_custom_call" | custom-call | tf_op jit(solution)/shard_map/pallas_call | solution.py:807
  21.5 0.0 collective-permute-done.before_in
  21.5 0.0 collective-permute-done.1.after_in
  21.5 8.6 %shard_map.170 = f32[16,152,128]{2,1,0:T(8,128)} custom-call(s32[128]{0:T(128)} %get-tuple-element.21.facts_in, s32[24,192]{1,0:T(8,128)} %get-tuple-element.22.near_in, f32[4608,128]{1,0:T(8,128)} %get-tuple-element.17.pool_in, f32[64,128]{1,0:T(8,128)} %collective-permute-done.before_in, f32[64,128]{1,0:T(8,128)} %collective-permute-done.1.after_in, ...), custom_call_target="tpu_custom_call" | custom-call | tf_op jit(solution)/shard_map/pallas_call | solution.py:831
  30.1 6.5 %all-to-all-start = ((f32[16,152,128]{2,1,0:T(8,128)}), f32[16,152,128]{2,1,0:T(8,128)}, u32[]{:S(2)}, u32[]{:S(2)}) async-start(f32[16,152,128]{2,1,0:T(8,128)} %shard_map.170), calls=%async_computation | async-start | bytes 2490368 | tf_op jit(solution)/shard_map/all_to_all | solution.py:846
  36.6 19.3 %shard_map.168 = (f32[1200,128]{1,0:T(8,128)}, f32[24,10,2,640]{3,2,1,0:T(2,128)}, s32[128]{0:T(128)}) custom-call(s32[384]{0:T(512)} %plan_in.3, s32[24]{0:T(128)} %wet_in.3, s32[10,24]{1,0:T(8,128)} %bitcast.18, s32[24,192]{1,0:T(8,128)} %links_in.3, f32[24,192]{1,0:T(8,128)} %angle_in.3, f32[24,192]{1,0:T(8,128)} %scale_in.3, f32[24,4,64]{2,1,0:T(4,128)} %metric_in.3, ...), custom_call_target="tpu_custom_call" | custom-call | tf_op jit(solution)/shard_map/pallas_call | solution.py:850
  55.9 9.9 %all-to-all-done.got = f32[16,152,128]{2,1,0:T(8,128)} async-done(((f32[16,152,128]{2,1,0:T(8,128)}), f32[16,152,128]{2,1,0:T(8,128)}, u32[]{:S(2)}, u32[]{:S(2)}) %all-to-all-start) | async-done | bytes 1245216 | tf_op jit(solution)/shard_map/all_to_all | solution.py:846
  65.8 3.6 %shard_map.171 = (f32[1200,128]{1,0:T(8,128)}, f32[24,10,2,640]{3,2,1,0:T(2,128)}) custom-call(s32[128]{0:T(128)} %get-tuple-element.20.origin_in, f32[16,152,128]{2,1,0:T(8,128)} %all-to-all-done.got, f32[1200,128]{1,0:T(8,128)} %get-tuple-element.26.depth_in, ...), custom_call_target="tpu_custom_call", output_to_operand_aliasing={{0}: (2, {}), {1}: (3, {})} | custom-call | tf_op jit(solution)/shard_map/pallas_call | solution.py:870
Async XLA Ops:
  8.1 13.4 %collective-permute-start = (f32[64,128]{1,0:T(8,128)}, f32[64,128]{1,0:T(8,128)}, u32[]{:S(2)}, u32[]{:S(2)}) collective-permute-start(f32[64,128]{1,0:T(8,128)} %get-tuple-element.18), channel_id=1, source_target_pairs={{0,1},{1,2},{2,3},{3,4},{4,5},{5,6},{6,7},{7,8},{8,9},{9,10},{10,1... | collective-permute-start | bytes 98312 | tf_op jit(solution)/shard_map/ppermute | solution.py:783
  11.8 9.7 %collective-permute-start.1 = (f32[64,128]{1,0:T(8,128)}, f32[64,128]{1,0:T(8,128)}, u32[]{:S(2)}, u32[]{:S(2)}) collective-permute-start(f32[64,128]{1,0:T(8,128)} %get-tuple-element.19), channel_id=1, source_target_pairs={{1,0},{2,1},{3,2},{4,3},{5,4},{6,5},{7,6},{8,7},{9,8},{10,9},{11,1... | collective-permute-start | bytes 98312 | tf_op jit(solution)/shard_map/ppermute | solution.py:784
  30.1 35.7 %all-to-all-start = ((f32[16,152,128]{2,1,0:T(8,128)}), f32[16,152,128]{2,1,0:T(8,128)}, u32[]{:S(2)}, u32[]{:S(2)}) async-start(f32[16,152,128]{2,1,0:T(8,128)} %shard_map.170), calls=%async_computation | async-start | bytes 2490368 | tf_op jit(solution)/shard_map/all_to_all | solution.py:846

commit v4 on v2

--- a/solution.py
+++ b/solution.py
@@ -92,6 +92,7 @@
         return (n % 2) * comp + s * pairs + n // 2
 
     own = np.zeros((LANES, LANES), np.float32)
+    own[2 * comp, 3 * wide :] = 1.0
     back = np.zeros((LANES, LANES), np.float32)
     lift = np.zeros((2 * comp, LANES), np.float32)
     along = np.zeros((2, 2 * comp, LANES), np.float32)
@@ -113,7 +114,7 @@
     for q in range(4):
         for f in range(3):
             spread[3 * q + f, q * LANES + f * wide : q * LANES + (f + 1) * wide] = 1.0
-        spread[12 + q, (4 + q) * LANES : (5 + q) * LANES] = 1.0
+        spread[12 + q, (4 + q) * LANES : (4 + q) * LANES + 2 * comp] = 1.0
     return dict(
         own=own, back=back, lift=lift, along=along, spread=spread,
         comp=comp, pairs=pairs, used=used, wide=wide, nodes=nodes, members=members,
@@ -304,9 +305,9 @@
 def face_rows(angle, scale, links, metric, coefs, blocks, elements):
     shape = (blocks, 3 * elements)
     own = lax.broadcasted_iota(jnp.int32, shape, 0) * (3 * elements) + lax.broadcasted_iota(jnp.int32, shape, 1)
-    wall = jnp.where(links[...] == own, 1.0, 0.0)
+    free = jnp.where(links[...] == own, 0.0, 1.0)
     lower = lax.broadcasted_iota(jnp.int32, (blocks, LANES), 1) < elements
-    for q, value in enumerate((jnp.cos(angle[...]), jnp.sin(angle[...]), scale[...], wall)):
+    for q, value in enumerate((jnp.cos(angle[...]), jnp.sin(angle[...]), scale[...], free)):
         two = value[:, :LANES]
         swapped = swap_halves(two)
         third = value[:, LANES:]
@@ -320,16 +321,100 @@
         coefs[b * 16 + 12 : b * 16 + 16] = jnp.concatenate([factors, factors], axis=1)
 
 
+def spread_pair(coefs, both, eye, spread, factors, elements):
+    lower = lax.broadcasted_iota(jnp.int32, (16, LANES), 1) < elements
+    values = jnp.where(lower, coefs[pl.ds(both[0] * 16, 16), :], coefs[pl.ds(both[1] * 16, 16), :])
+    rough = values.astype(jnp.bfloat16).astype(jnp.float32)
+    stacked = jnp.concatenate([rough, values - rough], axis=0).astype(jnp.bfloat16)
+    stacked = mm(eye[:, :LANES], stacked, ((1,), (1,))).astype(jnp.bfloat16)
+    factors[...] = mm(stacked, spread[...])
+
+
+def inflow_rows(breach, both, t):
+    rows = []
+    for b in both:
+        row = jnp.zeros((1, LANES), jnp.float32)
+        for s in range(t["members"]):
+            level = breach[s, b].astype(jnp.float32)
+            row = jnp.where(lax.broadcasted_iota(jnp.int32, (1, LANES), 1) == 2 * t["comp"] + s, level, row)
+        rows.append(row)
+    return rows
+
+
+def volume_rows(rows, turned, factors, first, inflow, pieces):
+    rx, sx, ry, sy = (factors[rows, q * LANES : (q + 1) * LANES] for q in range(first, first + 4))
+    height, flow_x, flow_y = (turned[c, rows] for c in range(3))
+    pressure = 0.5 * gravity * height * height
+    inverse = 1.0 / height
+    speed_x = flow_x * inverse
+    speed_y = flow_y * inverse
+    cross = flow_y * speed_x
+    flux_f = (flow_x, flow_x * speed_x + pressure, cross)
+    flux_g = (flow_y, cross, flow_y * speed_y + pressure)
+    for c in range(3):
+        along_r = rx * flux_f[c] + ry * flux_g[c]
+        along_s = sx * flux_f[c] + sy * flux_g[c]
+        if c == 0:
+            along_r = along_r + inflow
+        pieces[c, rows, 0:LANES], pieces[c, rows, LANES : 2 * LANES] = split(along_r)
+        pieces[c, rows, 2 * LANES : 3 * LANES], pieces[c, rows, 3 * LANES : 4 * LANES] = split(along_s)
+
+
+def flux_rows(rows, traces, outer, factors, pieces, first, wide):
+    lane = lax.broadcasted_iota(jnp.int32, (rows.stop - rows.start, LANES), 1)
+    n_x, n_y, scale, free = (factors[rows, q * LANES : (q + 1) * LANES] for q in range(4))
+    theirs = [outer[f * LANES + rows.start : f * LANES + rows.stop] for f in range(3)]
+    height, flow_x, flow_y = (traces[c, rows] for c in range(3))
+    is_wall = free < 0.5
+    through = flow_x * n_x + flow_y * n_y
+    twice = through + through
+    height_o = jnp.where(is_wall, height, place_face(theirs, 0, wide, lane))
+    flow_xo = jnp.where(is_wall, flow_x - twice * n_x, place_face(theirs, 1, wide, lane))
+    flow_yo = jnp.where(is_wall, flow_y - twice * n_y, place_face(theirs, 2, wide, lane))
+    speed = through / height
+    speed_o = (flow_xo * n_x + flow_yo * n_y) / height_o
+    fast = jnp.maximum(
+        jnp.abs(speed) + root(gravity * height), jnp.abs(speed_o) + root(gravity * height_o)
+    )
+    ours, others = speed - fast, speed_o - fast
+    half = 0.5 * scale
+    push = 0.5 * gravity * (height * height - height_o * height_o)
+    jumps = (
+        half * (height * ours - height_o * others),
+        half * (flow_x * ours - flow_xo * others + push * n_x),
+        half * (flow_y * ours - flow_yo * others + push * n_y),
+    )
+    for c in range(3):
+        pieces[c, rows, first : first + LANES], pieces[c, rows, first + LANES : first + 2 * LANES] = split(jumps[c])
+
+
+def lift_mm(lift, low, pieces, c, first):
+    last = ((1,), (1,))
+    return mm(lift, pieces[c, :, : first + 2 * LANES], last) + mm(low[...], pieces[c, :, first : first + LANES], last)
+
+
+def pair_gains(tall, comp, elements):
+    narrow = lax.broadcasted_iota(jnp.int32, (comp, LANES), 1) < elements
+    even, odd = tall[:comp], tall[comp:]
+    return jnp.where(narrow, even, swap_halves(odd)), jnp.where(narrow, swap_halves(even), odd)
+
+
+def row_chunks(step):
+    return [slice(i * step, (i + 1) * step) for i in range(LANES // step)]
+
+
+RING = 8
+
+
 def finish_kernel(
     plan_in, wet_in, breach_in, links_in, angle_in, scale_in, metric_in,
     fields_in, pool_in, before_in, after_in, own_in, spread_in, matrix_in, low_in, eye_in,
-    *rest, t, blocks, elements, leaving, devices,
+    *rest, t, blocks, elements, devices, leaving,
 ):
     outs, scratch = (rest[:1], rest[1:]) if leaving else (rest[:3], rest[3:])
     plan, wet, breach, links, angle, scale, metric, fields, pool, own, spread, matrix, low, eye, *scratch = scratch
-    order, place, coefs, turned, halves, traces, factors, outer, pieces, near, *scratch = scratch
-    staged, sems = scratch[0], scratch[-1]
-    comp, pairs, members, wide, used = t["comp"], t["pairs"], t["members"], t["wide"], t["used"]
+    order, place, coefs, turned, halves, traces, factors, outer, pieces, near, sems, staged, *scratch = scratch
+    comp, wide, used = t["comp"], t["wide"], t["used"]
     faces = blocks * 3 * elements
     width = before_in.shape[0]
     loads = [
@@ -338,21 +423,23 @@
         (pool_in, pool.at[pl.ds(0, faces)]), (before_in, pool.at[pl.ds(faces, width)]),
         (after_in, pool.at[pl.ds(faces + width, width)]), (spread_in, spread), (matrix_in, matrix), (low_in, low),
     ]
-    n_loads = len(loads) + 2
+    n = len(loads)
     loads = start_all([pltpu.make_async_copy(a, b, sems.at[i]) for i, (a, b) in enumerate(loads)])
     index = lax.axis_index("mesh")
     loads[0].wait()
     n_leaving = scan_moves(plan, index * blocks, order, place, blocks)
     begin = 0 if leaving else n_leaving
     end = n_leaving if leaving else blocks
+    steps = (end - begin + 3) // 4
+
+    def at(i, u):
+        return jnp.minimum(begin + 4 * i + u, end - 1)
 
     def indices(i):
-        at = (begin + 2 * i, jnp.minimum(begin + 2 * i + 1, end - 1))
-        return [
-            pltpu.make_async_copy(links_in.at[order[at[u]]], near.at[u], sems.at[n_loads - 2 + u]) for u in range(2)
-        ]
-
-    steps = (end - begin + 1) // 2
+        return [pltpu.make_async_copy(links_in.at[order[at(i, u)]], near.at[u], sems.at[n + u]) for u in range(4)]
+
+    def send(p):
+        return pltpu.make_async_copy(staged.at[p], outs[0].at[place[order[p]]], sems.at[n + 4 + p % RING])
 
     @pl.when(steps > 0)
     def _():
@@ -361,136 +448,95 @@
     wait_all(loads[1:5])
     face_rows(angle, scale, links, metric, coefs, blocks, elements)
     if not leaving:
-        scan_origins(plan, index, scratch[3], blocks, devices)
+        scan_origins(plan, index, scratch[2], blocks, devices)
     wait_all(loads[5:])
-    step = 16
-    chunks = [slice(i * step, (i + 1) * step) for i in range(LANES // step)]
+    chunks = row_chunks(16)
+    rows_to_pick = [
+        (u, f, e) for u in range(2) for f in range(3) for e in range(elements)
+    ]
+
+    def pick(w, some):
+        for u, f, e in some:
+            row = f * LANES + u * elements + e
+            outer[w, row : row + 1, :] = pool[pl.ds(near[2 * w + u, f * elements + e], 1), :]
 
     def one(i, carry):
-        at = (begin + 2 * i, jnp.minimum(begin + 2 * i + 1, end - 1))
-        both = (order[at[0]], order[at[1]])
+        both = [[order[at(i, 2 * w + u)] for u in range(2)] for w in range(2)]
+        inflow = [None, None]
+
+        def lay_out(w):
+            turn_pair(fields, both[w][0], both[w][1], eye, turned.at[w], halves.at[w], comp)
+            inner = mm(halves[w], own[...])
+            for c in range(3):
+                traces[w, c] = inner[c * LANES : (c + 1) * LANES]
+            spread_pair(coefs, both[w], eye, spread, factors.at[w], elements)
+            inflow[w] = inflow_rows(breach, both[w], t)
+
+        def fluxes(w, rows):
+            volume_rows(rows, turned.at[w], factors.at[w], 4, inflow[w][rows.start // elements], pieces.at[w])
+            flux_rows(rows, traces.at[w], outer.at[w], factors.at[w], pieces.at[w], 4 * LANES, wide)
+
+        def combine(w, c):
+            gains = pair_gains(lift_mm(matrix[...], low, pieces.at[w], c, 4 * LANES), comp, elements)
+            for u in range(2):
+                b = both[w][u]
+                rate = time_step * wet[b].astype(jnp.float32)
+                done = fields[b, c * comp : (c + 1) * comp] + rate * gains[u]
+                if leaving:
+                    staged[at(i, 2 * w + u), c * used : (c + 1) * used] = done[:used]
+                else:
+                    staged[2 * w + u, c * comp : (c + 1) * comp] = done
+
+        def hand_over(w):
+            for u in range(2):
+                if leaving:
+                    p = 4 * i + 2 * w + u
+
+                    @pl.when(p < end)
+                    def _():
+                        @pl.when(p >= RING)
+                        def _():
+                            send(p - RING).wait()
+
+                        send(p).start()
+                else:
+                    write_block(both[w][u], staged.at[2 * w + u], comp, scratch[0], scratch[1], t, blocks)
 
         wait_all(indices(i))
-        for u in range(2):
-            for f in range(3):
-                for e in range(elements):
-                    v = near[u, f * elements + e]
-                    row = f * LANES + u * elements + e
-                    outer[row : row + 1, :] = pool[pl.ds(v, 1), :]
+        pick(0, rows_to_pick)
+        lay_out(0)
+        share = len(rows_to_pick) // len(chunks)
+        for k, rows in enumerate(chunks):
+            fluxes(0, rows)
+            pick(1, rows_to_pick[k * share : (k + 1) * share])
+            if k == 1:
+                lay_out(1)
+        for k, rows in enumerate(chunks):
+            if k < 3:
+                combine(0, k)
+            fluxes(1, rows)
+        for c in range(3):
+            combine(1, c)
 
         @pl.when(i + 1 < steps)
         def _():
             start_all(indices(i + 1))
 
-        turn_pair(fields, both[0], both[1], eye, turned, halves, comp)
-        inner = mm(halves[...], own[...])
-        for c in range(3):
-            traces[c] = inner[c * LANES : (c + 1) * LANES]
-        lower = lax.broadcasted_iota(jnp.int32, (16, LANES), 1) < elements
-        values = jnp.where(lower, coefs[pl.ds(both[0] * 16, 16), :], coefs[pl.ds(both[1] * 16, 16), :])
-        rough = values.astype(jnp.bfloat16).astype(jnp.float32)
-        stacked = jnp.concatenate([rough, values - rough], axis=0).astype(jnp.bfloat16)
-        stacked = mm(eye[:, :LANES], stacked, ((1,), (1,))).astype(jnp.bfloat16)
-        factors[...] = mm(stacked, spread[...])
-
-        lane = lax.broadcasted_iota(jnp.int32, (step, LANES), 1)
-        inflow = []
-        for b in both:
-            row = jnp.zeros((1, LANES), jnp.float32)
-            for s in range(members):
-                level = breach[s, b].astype(jnp.float32)
-                row = jnp.where(lax.broadcasted_iota(jnp.int32, (1, LANES), 1) == 2 * comp + s, level, row)
-            inflow.append(row)
-        for rows in chunks:
-            n_x, n_y, scale, wall, rx, sx, ry, sy = (
-                factors[rows, q * LANES : (q + 1) * LANES] for q in range(8)
-            )
-            height, flow_x, flow_y = (turned[c, rows] for c in range(3))
-            pressure = 0.5 * gravity * height * height
-            inverse = 1.0 / height
-            speed_x = flow_x * inverse
-            speed_y = flow_y * inverse
-            cross = flow_y * speed_x
-            flux_f = (flow_x, flow_x * speed_x + pressure, cross)
-            flux_g = (flow_y, cross, flow_y * speed_y + pressure)
-            add = inflow[rows.start // elements]
-            for c in range(3):
-                along_r = rx * flux_f[c] + ry * flux_g[c]
-                along_s = sx * flux_f[c] + sy * flux_g[c]
-                along_r = jnp.where(lane < 2 * comp, along_r, add if c == 0 else 0.0)
-                pieces[c, rows, 0:LANES], pieces[c, rows, LANES : 2 * LANES] = split(along_r)
-                pieces[c, rows, 2 * LANES : 3 * LANES], pieces[c, rows, 3 * LANES : 4 * LANES] = split(along_s)
-
-            live = lane < 3 * wide
-            theirs = [outer[f * LANES + rows.start : f * LANES + rows.stop] for f in range(3)]
-            height = jnp.where(live, traces[0, rows], 1.0)
-            flow_x, flow_y = traces[1, rows], traces[2, rows]
-            is_wall = wall > 0.5
-            through = flow_x * n_x + flow_y * n_y
-            height_o = jnp.where(live, jnp.where(is_wall, height, place_face(theirs, 0, wide, lane)), 1.0)
-            flow_xo = jnp.where(is_wall, flow_x - 2.0 * through * n_x, place_face(theirs, 1, wide, lane))
-            flow_yo = jnp.where(is_wall, flow_y - 2.0 * through * n_y, place_face(theirs, 2, wide, lane))
-            through_o = flow_xo * n_x + flow_yo * n_y
-            speed = through / height
-            speed_o = through_o / height_o
-            fast = jnp.maximum(
-                jnp.abs(speed) + root(gravity * height), jnp.abs(speed_o) + root(gravity * height_o)
-            )
-            push = 0.5 * gravity * (height * height - height_o * height_o)
-            half = 0.5 * scale
-            jumps = (
-                half * (through - through_o + fast * (height_o - height)),
-                half * (flow_x * speed - flow_xo * speed_o + push * n_x + fast * (flow_xo - flow_x)),
-                half * (flow_y * speed - flow_yo * speed_o + push * n_y + fast * (flow_yo - flow_y)),
-            )
-            for c in range(3):
-                jump = jnp.where(live, jumps[c], 0.0)
-                pieces[c, rows, 4 * LANES : 5 * LANES], pieces[c, rows, 5 * LANES : 6 * LANES] = split(jump)
-
-        rates = [time_step * wet[b].astype(jnp.float32) for b in both]
-        last = ((1,), (1,))
-        narrow = lax.broadcasted_iota(jnp.int32, (comp, LANES), 1) < elements
-        for c in range(3):
-            tall = mm(matrix[...], pieces[c], last) + mm(low[...], pieces[c, :, 4 * LANES : 5 * LANES], last)
-            even, odd = tall[:comp], tall[comp:]
-            gains = (jnp.where(narrow, even, swap_halves(odd)), jnp.where(narrow, swap_halves(even), odd))
-            for u in range(2):
-                done = fields[both[u], c * comp : (c + 1) * comp] + rates[u] * gains[u]
-                if leaving:
-                    staged[at[u], c * used : (c + 1) * used] = done[:used]
-                else:
-                    staged[u, c * comp : (c + 1) * comp] = done
-
-        if leaving:
-            for u in range(2):
-
-                @pl.when(begin + 2 * i + u < end)
-                def _():
-                    pltpu.make_async_copy(
-                        staged.at[at[u]], outs[0].at[place[both[u]]], sems.at[n_loads + at[u]]
-                    ).start()
-        else:
-            for u in range(2):
-                write_block(both[u], staged.at[u], comp, scratch[1], scratch[2], t, blocks)
+        hand_over(0)
+        hand_over(1)
         return carry
 
     lax.fori_loop(0, steps, one, 0)
     if leaving:
 
-        def finish(i, carry):
-            pltpu.make_async_copy(staged.at[i], outs[0].at[place[order[i]]], sems.at[n_loads + i]).wait()
+        def drain(p, carry):
+            send(p).wait()
             return carry
 
-        lax.fori_loop(0, end, finish, 0)
+        lax.fori_loop(jnp.maximum(end - RING, 0), end, drain, 0)
     else:
-        wait_all(
-            start_all(
-                [
-                    pltpu.make_async_copy(a, outs[i], sems.at[n_loads + i])
-                    for i, a in enumerate((scratch[1], scratch[2], scratch[3].at[pl.ds(0, outs[2].shape[0])]))
-                ]
-            )
-        )
+        kept = ((scratch[0], outs[0]), (scratch[1], outs[1]), (scratch[2].at[pl.ds(0, outs[2].shape[0])], outs[2]))
+        wait_all(start_all([pltpu.make_async_copy(a, b, sems.at[n + 4 + i]) for i, (a, b) in enumerate(kept)]))
 
 
 def write_block(b, rows, step, depth, flow, t, blocks):
@@ -506,42 +552,43 @@
 
 
 def merge_kernel(
-    origin_in, got, depth_in, flow_in, depth_out, flow_out, origin, depth, flow, came, sems, *, t, blocks
+    origin_in, got_in, depth_in, flow_in, depth_out, flow_out, origin, depth, flow, got, sems, *, t, blocks
 ):
-    def arrival(b):
-        return pltpu.make_async_copy(got.at[origin[b]], came.at[b], sems.at[b])
-
-    def leave(b):
-        return pltpu.make_async_copy(flow.at[b], flow_out.at[b], sems.at[blocks + b])
-
-    whole = pltpu.make_async_copy(depth_in, depth, sems.at[2 * blocks])
-    first = pltpu.make_async_copy(origin_in, origin, sems.at[2 * blocks + 1])
-    first.start()
-    whole.start()
-    first.wait()
-
-    def each(act):
-        def one(b, carry):
-            @pl.when(origin[b] >= 0)
+    def leave(b, k):
+        return pltpu.make_async_copy(flow.at[b], flow_out.at[b], sems.at[3 + k % RING])
+
+    loads = start_all(
+        [
+            pltpu.make_async_copy(a, b, sems.at[i])
+            for i, (a, b) in enumerate(((origin_in, origin), (got_in, got), (depth_in, depth)))
+        ]
+    )
+    wait_all(loads)
+
+    def put(b, k):
+        came = origin[b] >= 0
+
+        @pl.when(came)
+        def _():
+            write_block(b, got.at[origin[b]], t["used"], depth, flow, t, blocks)
+
+            @pl.when(k >= RING)
             def _():
-                act(b)
-
-            return carry
-
-        lax.fori_loop(0, blocks, one, 0)
-
-    each(lambda b: arrival(b).start())
-    whole.wait()
-
-    def put(b):
-        arrival(b).wait()
-        write_block(b, came.at[b], t["used"], depth, flow, t, blocks)
-        leave(b).start()
-
-    each(put)
-    back = pltpu.make_async_copy(depth, depth_out, sems.at[2 * blocks])
+                leave(b, k).wait()
+
+            leave(b, k).start()
+
+        return k + came.astype(jnp.int32)
+
+    arrivals = lax.fori_loop(0, blocks, put, jnp.int32(0))
+    back = pltpu.make_async_copy(depth, depth_out, sems.at[2])
     back.start()
-    each(lambda b: leave(b).wait())
+
+    def drain(k, carry):
+        leave(0, k).wait()
+        return carry
+
+    lax.fori_loop(jnp.maximum(arrivals - RING, 0), arrivals, drain, 0)
     back.wait()
 
 
@@ -612,26 +659,27 @@
     ]
     packed = round_up(3 * used, 8)
 
-    def finish(leaving, out_shape, extra, n_sems):
+    i32 = jnp.int32
+    rows_of = (3 * comp, LANES)
+
+    def finish(leaving, out_shape, extra):
         return call(
             functools.partial(
-                finish_kernel, t=t, blocks=blocks, elements=elements, leaving=leaving, devices=count
+                finish_kernel, t=t, blocks=blocks, elements=elements, devices=count, leaving=leaving
             ),
             out_shape,
             0, 16,
             [
-                pltpu.SMEM(block_plan.shape, jnp.int32), pltpu.SMEM(wet_blocks.shape, jnp.int32),
-                pltpu.SMEM((members, blocks), jnp.int32), pltpu.VMEM(face_map.shape, jnp.int32),
+                pltpu.SMEM(block_plan.shape, i32), pltpu.SMEM(wet_blocks.shape, i32),
+                pltpu.SMEM((members, blocks), i32), pltpu.VMEM(face_map.shape, i32),
                 pltpu.VMEM(face_angle.shape, f32), pltpu.VMEM(face_scale.shape, f32), pltpu.VMEM(metric.shape, f32),
-                pltpu.VMEM((blocks, 3 * comp, LANES), f32), pltpu.VMEM((faces + 2 * width, LANES), f32),
+                pltpu.VMEM((blocks, *rows_of), f32), pltpu.VMEM((faces + 2 * width, LANES), f32),
                 *[pltpu.VMEM(m.shape, bf16) for m in mats],
-                pltpu.SMEM((blocks,), jnp.int32), pltpu.SMEM((blocks,), jnp.int32),
-                pltpu.VMEM((blocks * 16, LANES), f32),
-                pltpu.VMEM((3, LANES, LANES), f32), pltpu.VMEM((3 * LANES, 2 * LANES), bf16),
-                pltpu.VMEM((3, LANES, LANES), f32), pltpu.VMEM((LANES, 8 * LANES), f32),
-                pltpu.VMEM((3 * LANES, LANES), f32), pltpu.VMEM((3, LANES, 6 * LANES), bf16),
-                pltpu.SMEM((2, face_map.shape[1]), jnp.int32),
-                *extra, dma((18 + n_sems,)),
+                pltpu.SMEM((blocks,), i32), pltpu.SMEM((blocks,), i32), pltpu.VMEM((blocks * 16, LANES), f32),
+                pltpu.VMEM((2, 3, LANES, LANES), f32), pltpu.VMEM((2, 3 * LANES, 2 * LANES), bf16),
+                pltpu.VMEM((2, 3, LANES, LANES), f32), pltpu.VMEM((2, LANES, 8 * LANES), f32),
+                pltpu.VMEM((2, 3 * LANES, LANES), f32), pltpu.VMEM((2, 3, LANES, 6 * LANES), bf16),
+                pltpu.SMEM((4, face_map.shape[1]), i32), dma((20 + RING,)), *extra,
             ],
             jax.tree.map(lambda _: HBM, out_shape),
         )(
@@ -639,22 +687,19 @@
             *mats,
         )
 
-    sent = finish(
-        True, jax.ShapeDtypeStruct((count, packed, LANES), f32), [pltpu.VMEM((blocks, packed, LANES), f32)], blocks
-    )
+    sent = finish(True, jax.ShapeDtypeStruct((count, packed, LANES), f32), [pltpu.VMEM((blocks, packed, LANES), f32)])
     got = lax.all_to_all(sent, "mesh", split_axis=0, concat_axis=0, tiled=True)
     final = (jax.ShapeDtypeStruct(depth_rows.shape, f32), jax.ShapeDtypeStruct(flow_rows.shape, f32))
     whole = [pltpu.VMEM(depth_rows.shape, f32), pltpu.VMEM(flow_rows.shape, f32)]
-    slots = LANES
     depth_kept, flow_kept, origin = finish(
-        False, (*final, jax.ShapeDtypeStruct((slots,), jnp.int32)),
-        [pltpu.VMEM((2, 3 * comp, LANES), f32), *whole, pltpu.SMEM((slots,), jnp.int32)], 3,
+        False, (*final, jax.ShapeDtypeStruct((LANES,), i32)),
+        [pltpu.VMEM((4, *rows_of), f32), *whole, pltpu.SMEM((LANES,), i32)],
     )
     depth_new, flow_new = call(
         functools.partial(merge_kernel, t=t, blocks=blocks),
         final,
         0, 4,
-        [pltpu.SMEM((slots,), jnp.int32), *whole, pltpu.VMEM((blocks, packed, LANES), f32), dma((2 * blocks + 2,))],
+        [pltpu.SMEM((LANES,), i32), *whole, pltpu.VMEM((count, packed, LANES), f32), dma((3 + RING,))],
         (HBM, HBM),
         input_output_aliases={2: 0, 3: 1},
     )(origin, got, depth_kept, flow_kept)

time: 67.5 us -> 63.8 us (0.945)
  Pallas kernels: 41.6 us -> 31.9 us
  waiting for transfers between devices: 14.2 us -> 20.2 us
    pallas_call x2, Pallas kernels: 30.6 us -> 21.4 us  [finish(): call(functools.partial(finish_kernel, t=t, blocks=blocks, elements=elemen...]
    all_to_all x1, waiting for transfers between devices: 9.69 us -> 15.7 us  [body(): got = lax.all_to_all(sent, 'mesh', split_axis=0, concat_axis=0, tiled=True)]
  transfers between devices with their start and end apart: 3 -> 3, of which waited for: 2 -> 2; matrix products, arithmetic and copies ran while one was open for 0% -> 0% of each run, Pallas kernels for 29% -> 21%
where the time goes in v4:
time: 63.8 us; the launch traced here: 63.5 us
  Pallas kernels  31.9 us (50%)
  waiting for transfers between devices  20.2 us (32%)
  starting transfers between devices  10.6 us (17%)
  between operations  0.68 us (1%)
    pallas_call x2, Pallas kernels, finish(): call(functools.partial(finish_kernel, t=t, blocks=blocks, elements=elemen...  21.4 us
    all_to_all x1, waiting for transfers between devices, body(): got = lax.all_to_all(sent, 'mesh', split_axis=0, concat_axis=0, tiled=True)  15.7 us
    pallas_call x1, Pallas kernels, body(): call(functools.partial(prepare_kernel, t=t, blocks=blocks, elements=eleme...  7.5 us
    all_to_all x1, starting transfers between devices, body(): got = lax.all_to_all(sent, 'mesh', split_axis=0, concat_axis=0, tiled=True)  5.01 us
    ppermute x1, waiting for transfers between devices, body(): after = lax.ppermute(head, 'mesh', [(i + 1, i) for i in range(count - 1)])  4.51 us
    ppermute x1, starting transfers between devices, body(): before = lax.ppermute(tail, 'mesh', [(i, i + 1) for i in range(count - 1)])  3.71 us
    pallas_call x1, Pallas kernels, body(): call(functools.partial(merge_kernel, t=t, blocks=blocks), final, 0, 4, [p...  3.02 us
    ppermute x1, starting transfers between devices, body(): after = lax.ppermute(head, 'mesh', [(i + 1, i) for i in range(count - 1)])  1.92 us
  transfers between devices with their start and end apart: 3, of which 2 were waited for; matrix products, arithmetic and copies ran while one was open for 0% of the time, Pallas kernels for 21%

profile of v4, /device:TPU:15, one launch (start us, length us, event | category | flops | bytes accessed | tf_op | source)
XLA Modules:
  0.0 63.5 jit_solution(6963915593100883363)
XLA Ops:
  0.6 7.5 %shard_map.167 = (f32[24,168,128]{2,1,0:T(8,128)}, f32[4608,128]{1,0:T(8,128)}, f32[64,128]{1,0:T(8,128)}, f32[64,128]{1,0:T(8,128)}) custom-call(s32[1,128]{1,0:T(1,128)} %rim_in.1, f32[1200,128]{1,0:T(8,128)} %bitcast.16, f32[24,10,2,640]{3,2,1,0:T(2,128)} %bitcast.14, bf16[256,128]{1,0:T(8,128)(2,1)} %constant.12.clone.back_in, ...), custom_call_target="tpu_custom_call" | custom-call | tf_op jit(solution)/shard_map/pallas_call | solution.py:629
  8.1 3.7 %collective-permute-start = (f32[64,128]{1,0:T(8,128)}, f32[64,128]{1,0:T(8,128)}, u32[]{:S(2)}, u32[]{:S(2)}) collective-permute-start(f32[64,128]{1,0:T(8,128)} %get-tuple-element.13), channel_id=1, source_target_pairs={{0,1},{1,2},{2,3},{3,4},{4,5},{5,6},{6,7},{7,8},{8,9},{9,10},{10,1... | collective-permute-start | bytes 98312 | tf_op jit(solution)/shard_map/ppermute | solution.py:648
  11.9 1.9 %collective-permute-start.1 = (f32[64,128]{1,0:T(8,128)}, f32[64,128]{1,0:T(8,128)}, u32[]{:S(2)}, u32[]{:S(2)}) collective-permute-start(f32[64,128]{1,0:T(8,128)} %get-tuple-element.14), channel_id=1, source_target_pairs={{1,0},{2,1},{3,2},{4,3},{5,4},{6,5},{7,6},{8,7},{9,8},{10,9},{11,1... | collective-permute-start | bytes 98312 | tf_op jit(solution)/shard_map/ppermute | solution.py:649
  13.8 0.0 collective-permute-done.before_in
  13.8 4.5 %collective-permute-done.1.after_in = f32[64,128]{1,0:T(8,128)} collective-permute-done((f32[64,128]{1,0:T(8,128)}, f32[64,128]{1,0:T(8,128)}, u32[]{:S(2)}, u32[]{:S(2)}) %collective-permute-start.1) | collective-permute-done | bytes 32800 | tf_op jit(solution)/shard_map/ppermute | solution.py:649
  18.3 7.9 %shard_map.169 = f32[16,152,128]{2,1,0:T(8,128)} custom-call(s32[384]{0:T(512)} %plan_in.3, s32[24]{0:T(128)} %wet_in.3, s32[10,24]{1,0:T(8,128)} %bitcast.17, s32[24,192]{1,0:T(8,128)} %links_in.3, f32[24,192]{1,0:T(8,128)} %angle_in.3, f32[24,192]{1,0:T(8,128)} %scale_in.3, f32[24,4,64]{2,1,0:T(4,128)} %metric_in.3, ...), custom_call_target="tpu_custom_call" | custom-call | tf_op jit(solution)/shard_map/pallas_call | solution.py:666
  26.2 5.0 %all-to-all-start = ((f32[16,152,128]{2,1,0:T(8,128)}), f32[16,152,128]{2,1,0:T(8,128)}, u32[]{:S(2)}, u32[]{:S(2)}) async-start(f32[16,152,128]{2,1,0:T(8,128)} %shard_map.169), calls=%async_computation | async-start | bytes 2490368 | tf_op jit(solution)/shard_map/all_to_all | solution.py:691
  31.2 13.5 %shard_map.168 = (f32[1200,128]{1,0:T(8,128)}, f32[24,10,2,640]{3,2,1,0:T(2,128)}, s32[128]{0:T(128)}) custom-call(s32[384]{0:T(512)} %plan_in.3, s32[24]{0:T(128)} %wet_in.3, s32[10,24]{1,0:T(8,128)} %bitcast.18, s32[24,192]{1,0:T(8,128)} %links_in.3, f32[24,192]{1,0:T(8,128)} %angle_in.3, f32[24,192]{1,0:T(8,128)} %scale_in.3, f32[24,4,64]{2,1,0:T(4,128)} %metric_in.3, ...), custom_call_target="tpu_custom_call" | custom-call | tf_op jit(solution)/shard_map/pallas_call | solution.py:666
  44.7 15.7 %all-to-all-done.got_in = f32[16,152,128]{2,1,0:T(8,128)} async-done(((f32[16,152,128]{2,1,0:T(8,128)}), f32[16,152,128]{2,1,0:T(8,128)}, u32[]{:S(2)}, u32[]{:S(2)}) %all-to-all-start) | async-done | bytes 1245216 | tf_op jit(solution)/shard_map/all_to_all | solution.py:691
  60.4 3.0 %shard_map.170 = (f32[1200,128]{1,0:T(8,128)}, f32[24,10,2,640]{3,2,1,0:T(2,128)}) custom-call(s32[128]{0:T(128)} %get-tuple-element.15.origin_in, f32[16,152,128]{2,1,0:T(8,128)} %all-to-all-done.got_in, f32[1200,128]{1,0:T(8,128)} %get-tuple-element.16.depth_in, ...), custom_call_target="tpu_custom_call", output_to_operand_aliasing={{0}: (2, {}), {1}: (3, {})} | custom-call | tf_op jit(solution)/shard_map/pallas_call | solution.py:698
Async XLA Ops:
  8.1 5.7 %collective-permute-start = (f32[64,128]{1,0:T(8,128)}, f32[64,128]{1,0:T(8,128)}, u32[]{:S(2)}, u32[]{:S(2)}) collective-permute-start(f32[64,128]{1,0:T(8,128)} %get-tuple-element.13), channel_id=1, source_target_pairs={{0,1},{1,2},{2,3},{3,4},{4,5},{5,6},{6,7},{7,8},{8,9},{9,10},{10,1... | collective-permute-start | bytes 98312 | tf_op jit(solution)/shard_map/ppermute | solution.py:648
  11.9 6.5 %collective-permute-start.1 = (f32[64,128]{1,0:T(8,128)}, f32[64,128]{1,0:T(8,128)}, u32[]{:S(2)}, u32[]{:S(2)}) collective-permute-start(f32[64,128]{1,0:T(8,128)} %get-tuple-element.14), channel_id=1, source_target_pairs={{1,0},{2,1},{3,2},{4,3},{5,4},{6,5},{7,6},{8,7},{9,8},{10,9},{11,1... | collective-permute-start | bytes 98312 | tf_op jit(solution)/shard_map/ppermute | solution.py:649
  26.2 34.3 %all-to-all-start = ((f32[16,152,128]{2,1,0:T(8,128)}), f32[16,152,128]{2,1,0:T(8,128)}, u32[]{:S(2)}, u32[]{:S(2)}) async-start(f32[16,152,128]{2,1,0:T(8,128)} %shard_map.169), calls=%async_computation | async-start | bytes 2490368 | tf_op jit(solution)/shard_map/all_to_all | solution.py:691

commit v5 on v4

--- a/solution.py
+++ b/solution.py
@@ -144,20 +144,31 @@
     return mm(eye[...], jnp.concatenate(split(x), axis=1), ((1,), (1,)))
 
 
-def turn_pair(fields, first, second, eye, turned, halves, comp):
+def turn_rows(first, second, c, eye, turned, halves, comp):
     lower = lax.broadcasted_iota(jnp.int32, (comp, LANES), 1) < LANES // 2
-    for c in range(3):
-        a = fields[first, c * comp : (c + 1) * comp]
-        b = fields[second, c * comp : (c + 1) * comp]
-        even = jnp.where(lower, a, swap_halves(b))
-        odd = jnp.where(lower, swap_halves(a), b)
-        fill = jnp.full((LANES - 2 * comp, LANES), 1.0 if c == 0 else 0.0, jnp.float32)
-        flat = turn(jnp.concatenate([even, odd, fill], axis=0), eye)
-        if turned is not None:
-            turned[c] = flat
-        high, low = split(flat)
-        halves[c * LANES : (c + 1) * LANES, :LANES] = high
-        halves[c * LANES : (c + 1) * LANES, LANES:] = low
+    even = jnp.where(lower, first, swap_halves(second))
+    odd = jnp.where(lower, swap_halves(first), second)
+    fill = jnp.full((LANES - 2 * comp, LANES), 1.0 if c == 0 else 0.0, jnp.float32)
+    flat = turn(jnp.concatenate([even, odd, fill], axis=0), eye)
+    if turned is not None:
+        turned[c] = flat
+    high, low = split(flat)
+    halves[c * LANES : (c + 1) * LANES, :LANES] = high
+    halves[c * LANES : (c + 1) * LANES, LANES:] = low
+
+
+def rows_of(fields, block, c, comp):
+    if c == 0:
+        return fields[block, :comp]
+    return fields[block, pl.ds(comp + c - 1, comp, stride=2), :]
+
+
+def weave(*lists):
+    count = max(len(steps) for steps in lists)
+    for i in range(count):
+        for steps in lists:
+            for step in steps[len(steps) * i // count : len(steps) * (i + 1) // count]:
+                step()
 
 
 def place_face(pieces, c, wide, lane):
@@ -181,102 +192,118 @@
 
 
 def prepare_kernel(
-    rim_in, depth_in, flow_in, back_in, eye_in, fields_out, pool_out, head, tail,
+    rim_in, depth_in, flow_in, back_in, eye_in, fields_out, pool_out, partner, across,
     rim, depth, flow, back, eye, fields, pool, halves, sems, *, t, blocks, elements,
 ):
     comp, pairs, members, wide = t["comp"], t["pairs"], t["members"], t["wide"]
+    odd = lax.axis_index("mesh") % 2
     tiles = blocks // 8
     steps = blocks // 2
-    group = 2 * 3 * elements
+    group = 8 * 3 * elements
     first = start_all(
         [
             pltpu.make_async_copy(depth_in, depth, sems.at[0]), pltpu.make_async_copy(back_in, back, sems.at[1]),
-            pltpu.make_async_copy(eye_in, eye, sems.at[2]),
-            pltpu.make_async_copy(rim_in, rim, sems.at[3 + tiles + 2 * steps]),
+            pltpu.make_async_copy(eye_in, eye, sems.at[2]), pltpu.make_async_copy(rim_in, rim, sems.at[3]),
         ]
     )
 
     def part(tile):
         rows = pl.ds(8 * tile, 8)
-        return pltpu.make_async_copy(flow_in.at[rows], flow.at[rows], sems.at[3 + tile])
-
-    def outward(i):
-        rows, lines = pl.ds(2 * i, 2), pl.ds(group * i, group)
-        return [
-            pltpu.make_async_copy(fields.at[rows], fields_out.at[rows], sems.at[3 + tiles + i]),
-            pltpu.make_async_copy(pool.at[lines], pool_out.at[lines], sems.at[3 + tiles + steps + i]),
-        ]
+        return pltpu.make_async_copy(flow_in.at[rows], flow.at[rows], sems.at[4 + tile])
+
+    def field_part(i, slot):
+        return pltpu.make_async_copy(
+            fields.at[slot], fields_out.at[pl.ds(2 * i, 2)], sems.at[4 + 2 * tiles + slot]
+        )
+
+    def pool_part(tile):
+        lines = pl.ds(group * tile, group)
+        return pltpu.make_async_copy(pool.at[lines], pool_out.at[lines], sems.at[4 + tiles + tile])
 
     start_all([part(tile) for tile in range(tiles)])
+    for slot in range(2):
+        for u in range(2):
+            fields[slot, u, comp - 8 : comp] = jnp.full((8, LANES), 1.0, jnp.float32)
+            fields[slot, u, 3 * comp - 16 : 3 * comp] = jnp.zeros((16, LANES), jnp.float32)
     wait_all(first)
 
-    def build(i):
-        for u in range(2):
+    def build(i, slot):
+        def scenario(u, s):
             b = 2 * i + u
             tile, sub = b // 8, b % 8
-            for c in range(3):
-                end = comp * (c + 1)
-                fields[b, end - 8 : end] = jnp.full((8, LANES), 1.0 if c == 0 else 0.0, jnp.float32)
-            for s in range(members):
-                start = (s * tiles + tile) * pairs * 8 + sub
-                fields[b, s * pairs : (s + 1) * pairs] = depth[pl.ds(start, pairs, stride=8), :]
-                for j in range(pairs):
-                    two = flow[b, s, :, j * LANES : (j + 1) * LANES]
-                    row = s * pairs + j
-                    fields[b, comp + row : comp + row + 1] = two[0:1]
-                    fields[b, 2 * comp + row : 2 * comp + row + 1] = two[1:2]
-
-    def turn_of(i):
-        turn_pair(fields, 2 * i, 2 * i + 1, eye, None, halves, comp)
-
-    def faces_of(i):
-        rows = mm(halves[...], back[...])
+            start = (s * tiles + tile) * pairs * 8 + sub
+            fields[slot, u, s * pairs : (s + 1) * pairs] = depth[pl.ds(start, pairs, stride=8), :]
+            for j in range(pairs):
+                row = comp + 2 * (s * pairs + j)
+                fields[slot, u, row : row + 2] = flow[b, s, :, j * LANES : (j + 1) * LANES]
+
+        return [functools.partial(scenario, u, s) for u in range(2) for s in range(members)]
+
+    def turn_of(slot):
+        def component(c):
+            pair = fields.at[slot]
+            turn_rows(rows_of(pair, 0, c, comp), rows_of(pair, 1, c, comp), c, eye, None, halves.at[slot], comp)
+
+        return [functools.partial(component, c) for c in range(3)]
+
+    def faces_of(i, slot):
         lane = lax.broadcasted_iota(jnp.int32, (LANES, LANES), 1)
-        pieces = [rows[c * LANES : (c + 1) * LANES] for c in range(3)]
-        for f in range(3):
-            face = place_face(pieces, f, wide, lane)
-            for u in range(2):
-                at = ((2 * i + u) * 3 + f) * elements
-                pool[pl.ds(at, elements), :] = face[u * elements : (u + 1) * elements]
+        pieces = []
+
+        def multiply():
+            rows = mm(halves[slot], back[...])
+            pieces.extend(rows[c * LANES : (c + 1) * LANES] for c in range(3))
+
+        def face(f, u):
+            span = slice(u * elements, (u + 1) * elements)
+            at = ((2 * i + u) * 3 + f) * elements
+            pool[pl.ds(at, elements), :] = place_face([p[span] for p in pieces], f, wide, lane[span])
+
+        return [multiply] + [functools.partial(face, f, u) for u in range(2) for f in range(3)]
 
     part(0).wait()
-    build(0)
-    turn_of(0)
-    build(1)
-
-    def one(i, carry):
-        @pl.when(i % 4 == 0)
+    weave(build(0, 0))
+    field_part(0, 0).start()
+    weave(build(1, 1), turn_of(0))
+    field_part(1, 1).start()
+
+    def one(h, carry):
+        i = 2 * h
+
+        @pl.when(h % 2 == 0)
         def _():
-            part(i // 4).wait()
-
-        faces_of(i - 2)
-        turn_of(i - 1)
-        build(i)
-        start_all(outward(i - 2))
+            part(h // 2).wait()
+
+        for slot in range(2):
+            field_part(i - 2 + slot, slot).wait()
+            weave(build(i + slot, slot), turn_of(1 - slot), faces_of(i - 2 + slot, slot))
+            field_part(i + slot, slot).start()
+
+        @pl.when(h % 2 == 0)
+        def _():
+            pool_part(h // 2 - 1).start()
+
         return carry
 
-    lax.fori_loop(2, steps, one, 0)
-    faces_of(steps - 2)
-    turn_of(steps - 1)
-    start_all(outward(steps - 2))
-    faces_of(steps - 1)
-    start_all(outward(steps - 1))
-    width = head.shape[0]
+    lax.fori_loop(1, steps // 2, one, 0)
+    weave(turn_of(1), faces_of(steps - 2, 0))
+    weave(faces_of(steps - 1, 1))
+    pool_part(tiles - 1).start()
+    width = partner.shape[0]
+    near, far = (1 - odd) * width, odd * width
 
     def pick(i, carry):
-        for u in range(16):
-            r = i * 16 + u
-            head[pl.ds(r, 1), :] = pool[pl.ds(rim[0, r], 1), :]
-            tail[pl.ds(r, 1), :] = pool[pl.ds(rim[0, width + r], 1), :]
+        for u in range(32):
+            r = i * 32 + u
+            partner[pl.ds(r, 1), :] = pool[pl.ds(rim[0, near + r], 1), :]
+            across[pl.ds(r, 1), :] = pool[pl.ds(rim[0, far + r], 1), :]
         return carry
 
-    lax.fori_loop(0, width // 16, pick, 0)
-
-    def drain(i, carry):
-        wait_all(outward(i))
-        return carry
-
-    lax.fori_loop(0, steps, drain, 0)
+    lax.fori_loop(0, width // 32, pick, 0)
+    for slot in range(2):
+        field_part(steps - 2 + slot, slot).wait()
+    for tile in range(tiles):
+        pool_part(tile).wait()
 
 
 def scan_moves(plan, base, order, place, blocks):
@@ -385,12 +412,10 @@
         half * (flow_y * ours - flow_yo * others + push * n_y),
     )
     for c in range(3):
-        pieces[c, rows, first : first + LANES], pieces[c, rows, first + LANES : first + 2 * LANES] = split(jumps[c])
-
-
-def lift_mm(lift, low, pieces, c, first):
-    last = ((1,), (1,))
-    return mm(lift, pieces[c, :, : first + 2 * LANES], last) + mm(low[...], pieces[c, :, first : first + LANES], last)
+        high, rest = split(jumps[c])
+        pieces[c, rows, first : first + LANES] = high
+        pieces[c, rows, first + LANES : first + 2 * LANES] = rest
+        pieces[c, rows, first + 2 * LANES : first + 3 * LANES] = high
 
 
 def pair_gains(tall, comp, elements):
@@ -408,20 +433,23 @@
 
 def finish_kernel(
     plan_in, wet_in, breach_in, links_in, angle_in, scale_in, metric_in,
-    fields_in, pool_in, before_in, after_in, own_in, spread_in, matrix_in, low_in, eye_in,
+    fields_in, pool_in, partner_in, across_in, own_in, spread_in, matrix_in, eye_in,
     *rest, t, blocks, elements, devices, leaving,
 ):
     outs, scratch = (rest[:1], rest[1:]) if leaving else (rest[:3], rest[3:])
-    plan, wet, breach, links, angle, scale, metric, fields, pool, own, spread, matrix, low, eye, *scratch = scratch
+    plan, wet, breach, links, angle, scale, metric, fields, pool, own, spread, matrix, eye, *scratch = scratch
     order, place, coefs, turned, halves, traces, factors, outer, pieces, near, sems, staged, *scratch = scratch
     comp, wide, used = t["comp"], t["wide"], t["used"]
     faces = blocks * 3 * elements
-    width = before_in.shape[0]
+    width = partner_in.shape[0]
+    odd = lax.axis_index("mesh") % 2
+    near_rows = pl.multiple_of(faces + (1 - odd) * width, 8)
+    far_rows = pl.multiple_of(faces + odd * width, 8)
     loads = [
         (plan_in, plan), (angle_in, angle), (scale_in, scale), (links_in, links), (metric_in, metric),
         (wet_in, wet), (breach_in, breach), (eye_in, eye), (own_in, own), (fields_in, fields),
-        (pool_in, pool.at[pl.ds(0, faces)]), (before_in, pool.at[pl.ds(faces, width)]),
-        (after_in, pool.at[pl.ds(faces + width, width)]), (spread_in, spread), (matrix_in, matrix), (low_in, low),
+        (pool_in, pool.at[pl.ds(0, faces)]), (partner_in, pool.at[pl.ds(near_rows, width)]),
+        (across_in, pool.at[pl.ds(far_rows, width)]), (spread_in, spread), (matrix_in, matrix),
     ]
     n = len(loads)
     loads = start_all([pltpu.make_async_copy(a, b, sems.at[i]) for i, (a, b) in enumerate(loads)])
@@ -430,16 +458,21 @@
     n_leaving = scan_moves(plan, index * blocks, order, place, blocks)
     begin = 0 if leaving else n_leaving
     end = n_leaving if leaving else blocks
-    steps = (end - begin + 3) // 4
+    n_pairs = near.shape[0] // 2
+    steps = (end - begin + 2 * n_pairs - 1) // (2 * n_pairs)
 
     def at(i, u):
-        return jnp.minimum(begin + 4 * i + u, end - 1)
+        return jnp.minimum(begin + 2 * n_pairs * i + u, end - 1)
 
     def indices(i):
-        return [pltpu.make_async_copy(links_in.at[order[at(i, u)]], near.at[u], sems.at[n + u]) for u in range(4)]
+        return [
+            pltpu.make_async_copy(links_in.at[order[at(i, u)]], near.at[u], sems.at[n + u])
+            for u in range(2 * n_pairs)
+        ]
 
     def send(p):
-        return pltpu.make_async_copy(staged.at[p], outs[0].at[place[order[p]]], sems.at[n + 4 + p % RING])
+        rows = outs[0].shape[1]
+        return pltpu.make_async_copy(staged.at[p, pl.ds(0, rows)], outs[0].at[place[order[p]]], sems.at[n + 2 * n_pairs + p % RING])
 
     @pl.when(steps > 0)
     def _():
@@ -465,7 +498,11 @@
         inflow = [None, None]
 
         def lay_out(w):
-            turn_pair(fields, both[w][0], both[w][1], eye, turned.at[w], halves.at[w], comp)
+            for c in range(3):
+                turn_rows(
+                    rows_of(fields, both[w][0], c, comp), rows_of(fields, both[w][1], c, comp), c, eye,
+                    turned.at[w], halves.at[w], comp,
+                )
             inner = mm(halves[w], own[...])
             for c in range(3):
                 traces[w, c] = inner[c * LANES : (c + 1) * LANES]
@@ -477,15 +514,16 @@
             flux_rows(rows, traces.at[w], outer.at[w], factors.at[w], pieces.at[w], 4 * LANES, wide)
 
         def combine(w, c):
-            gains = pair_gains(lift_mm(matrix[...], low, pieces.at[w], c, 4 * LANES), comp, elements)
+            gains = pair_gains(mm(matrix[...], pieces[w, c], ((1,), (1,))), comp, elements)
             for u in range(2):
                 b = both[w][u]
                 rate = time_step * wet[b].astype(jnp.float32)
-                done = fields[b, c * comp : (c + 1) * comp] + rate * gains[u]
-                if leaving:
-                    staged[at(i, 2 * w + u), c * used : (c + 1) * used] = done[:used]
+                done = rows_of(fields, b, c, comp) + rate * gains[u]
+                row = at(i, 2 * w + u) if leaving else 2 * w + u
+                if c == 0:
+                    staged[row, :comp] = done
                 else:
-                    staged[2 * w + u, c * comp : (c + 1) * comp] = done
+                    staged[row, pl.ds(used + c - 1, comp, stride=2), :] = done
 
         def hand_over(w):
             for u in range(2):
@@ -500,7 +538,7 @@
 
                         send(p).start()
                 else:
-                    write_block(both[w][u], staged.at[2 * w + u], comp, scratch[0], scratch[1], t, blocks)
+                    write_block(both[w][u], staged.at[2 * w + u], scratch[0], scratch[1], t, blocks)
 
         wait_all(indices(i))
         pick(0, rows_to_pick)
@@ -536,19 +574,18 @@
         lax.fori_loop(jnp.maximum(end - RING, 0), end, drain, 0)
     else:
         kept = ((scratch[0], outs[0]), (scratch[1], outs[1]), (scratch[2].at[pl.ds(0, outs[2].shape[0])], outs[2]))
-        wait_all(start_all([pltpu.make_async_copy(a, b, sems.at[n + 4 + i]) for i, (a, b) in enumerate(kept)]))
-
-
-def write_block(b, rows, step, depth, flow, t, blocks):
-    pairs, members = t["pairs"], t["members"]
+        wait_all(start_all([pltpu.make_async_copy(a, b, sems.at[n + 2 * n_pairs + i]) for i, (a, b) in enumerate(kept)]))
+
+
+def write_block(b, rows, depth, flow, t, blocks):
+    pairs, members, used = t["pairs"], t["members"], t["used"]
     tile, sub = b // 8, b % 8
     for s in range(members):
         start = (s * (blocks // 8) + tile) * pairs * 8 + sub
         depth[pl.ds(start, pairs, stride=8), :] = rows[s * pairs : (s + 1) * pairs]
         for j in range(pairs):
-            row = s * pairs + j
-            flow[b, s, 0:1, j * LANES : (j + 1) * LANES] = rows[step + row : step + row + 1]
-            flow[b, s, 1:2, j * LANES : (j + 1) * LANES] = rows[2 * step + row : 2 * step + row + 1]
+            row = used + 2 * (s * pairs + j)
+            flow[b, s, :, j * LANES : (j + 1) * LANES] = rows[row : row + 2]
 
 
 def merge_kernel(
@@ -570,7 +607,7 @@
 
         @pl.when(came)
         def _():
-            write_block(b, got.at[origin[b]], t["used"], depth, flow, t, blocks)
+            write_block(b, got.at[origin[b]], depth, flow, t, blocks)
 
             @pl.when(k >= RING)
             def _():
@@ -626,7 +663,7 @@
 
     back = jnp.asarray(np.tile(t["back"], (2, 1)), bf16)
     eye = jnp.asarray(np.tile(np.eye(LANES), (1, 2)), bf16)
-    fields, pool, head, tail = call(
+    fields, pool, to_partner, to_across = call(
         functools.partial(prepare_kernel, t=t, blocks=blocks, elements=elements),
         (
             jax.ShapeDtypeStruct((blocks, 3 * comp, LANES), f32),
@@ -638,29 +675,32 @@
         [
             pltpu.SMEM(rim_faces.shape, jnp.int32), pltpu.VMEM(depth_rows.shape, f32), pltpu.VMEM(flow_rows.shape, f32), pltpu.VMEM(back.shape, bf16),
             pltpu.VMEM(eye.shape, bf16),
-            pltpu.VMEM((blocks, 3 * comp, LANES), f32), pltpu.VMEM((faces, LANES), f32),
-            pltpu.VMEM((3 * LANES, 2 * LANES), bf16), dma((4 + tiles + blocks,)),
+            pltpu.VMEM((2, 2, 3 * comp, LANES), f32), pltpu.VMEM((faces, LANES), f32),
+            pltpu.VMEM((2, 3 * LANES, 2 * LANES), bf16), dma((6 + 2 * tiles,)),
         ],
         (HBM, HBM, VMEM, VMEM),
     )(rim_faces, depth_rows, flow_rows, back, eye)
 
     count = lax.axis_size("mesh")
-    before = lax.ppermute(tail, "mesh", [(i, i + 1) for i in range(count - 1)])
-    after = lax.ppermute(head, "mesh", [(i + 1, i) for i in range(count - 1)])
+    partners = [(i, i ^ 1) for i in range(count)]
+    neighbours = [(i, i + 1 if i % 2 else i - 1) for i in range(1, count - 1)]
+    across = lax.ppermute(to_across, "mesh", neighbours)
+    partner = lax.ppermute(to_partner, "mesh", partners)
 
     lift_h, lift_l = high_low(t["lift"])
+    along_r, along_s = t["along"]
     matrix = np.concatenate(
-        [t["along"][0], t["along"][0], t["along"][1], t["along"][1], lift_h.astype(np.float32), lift_h.astype(np.float32)],
-        axis=1,
+        [along_r, along_r, along_s, along_s, *(np.asarray(m, np.float32) for m in (lift_h, lift_h, lift_l))], axis=1
     )
     mats = [
         jnp.asarray(np.tile(t["own"], (2, 1)), bf16), jnp.asarray(np.tile(t["spread"], (2, 1)), bf16),
-        jnp.asarray(matrix, bf16), jnp.asarray(lift_l), eye,
+        jnp.asarray(matrix, bf16), eye,
     ]
     packed = round_up(3 * used, 8)
 
     i32 = jnp.int32
-    rows_of = (3 * comp, LANES)
+    block_rows = (3 * comp, LANES)
+    n_pairs = 2
 
     def finish(leaving, out_shape, extra):
         return call(
@@ -668,32 +708,32 @@
                 finish_kernel, t=t, blocks=blocks, elements=elements, devices=count, leaving=leaving
             ),
             out_shape,
-            0, 16,
+            0, 15,
             [
                 pltpu.SMEM(block_plan.shape, i32), pltpu.SMEM(wet_blocks.shape, i32),
                 pltpu.SMEM((members, blocks), i32), pltpu.VMEM(face_map.shape, i32),
                 pltpu.VMEM(face_angle.shape, f32), pltpu.VMEM(face_scale.shape, f32), pltpu.VMEM(metric.shape, f32),
-                pltpu.VMEM((blocks, *rows_of), f32), pltpu.VMEM((faces + 2 * width, LANES), f32),
+                pltpu.VMEM((blocks, *block_rows), f32), pltpu.VMEM((faces + 2 * width, LANES), f32),
                 *[pltpu.VMEM(m.shape, bf16) for m in mats],
                 pltpu.SMEM((blocks,), i32), pltpu.SMEM((blocks,), i32), pltpu.VMEM((blocks * 16, LANES), f32),
                 pltpu.VMEM((2, 3, LANES, LANES), f32), pltpu.VMEM((2, 3 * LANES, 2 * LANES), bf16),
                 pltpu.VMEM((2, 3, LANES, LANES), f32), pltpu.VMEM((2, LANES, 8 * LANES), f32),
-                pltpu.VMEM((2, 3 * LANES, LANES), f32), pltpu.VMEM((2, 3, LANES, 6 * LANES), bf16),
-                pltpu.SMEM((4, face_map.shape[1]), i32), dma((20 + RING,)), *extra,
+                pltpu.VMEM((2, 3 * LANES, LANES), f32), pltpu.VMEM((2, 3, LANES, 7 * LANES), bf16),
+                pltpu.SMEM((2 * n_pairs, face_map.shape[1]), i32), dma((16 + 2 * n_pairs + RING,)), *extra,
             ],
             jax.tree.map(lambda _: HBM, out_shape),
         )(
-            block_plan, wet_blocks, breach.T, face_map, face_angle, face_scale, metric, fields, pool, before, after,
+            block_plan, wet_blocks, breach.T, face_map, face_angle, face_scale, metric, fields, pool, partner, across,
             *mats,
         )
 
-    sent = finish(True, jax.ShapeDtypeStruct((count, packed, LANES), f32), [pltpu.VMEM((blocks, packed, LANES), f32)])
+    sent = finish(True, jax.ShapeDtypeStruct((count, packed, LANES), f32), [pltpu.VMEM((blocks, *block_rows), f32)])
     got = lax.all_to_all(sent, "mesh", split_axis=0, concat_axis=0, tiled=True)
     final = (jax.ShapeDtypeStruct(depth_rows.shape, f32), jax.ShapeDtypeStruct(flow_rows.shape, f32))
     whole = [pltpu.VMEM(depth_rows.shape, f32), pltpu.VMEM(flow_rows.shape, f32)]
     depth_kept, flow_kept, origin = finish(
         False, (*final, jax.ShapeDtypeStruct((LANES,), i32)),
-        [pltpu.VMEM((4, *rows_of), f32), *whole, pltpu.SMEM((LANES,), i32)],
+        [pltpu.VMEM((2 * n_pairs, *block_rows), f32), *whole, pltpu.SMEM((LANES,), i32)],
     )
     depth_new, flow_new = call(
         functools.partial(merge_kernel, t=t, blocks=blocks),

time: 63.8 us -> 61.9 us (0.970)
  starting transfers between devices: 10.6 us -> 8.81 us
  Pallas kernels: 31.9 us -> 33.1 us
  waiting for transfers between devices: 20.2 us -> 19 us
    ppermute x2, starting transfers between devices: 5.63 us -> 3.79 us  [the longest x1 3.04 us: body(): across = lax.ppermute(to_across, 'mesh', neighbours)]
    ppermute x2, waiting for transfers between devices: 4.51 us -> 3.38 us  [the longest x1 3.38 us: body(): across = lax.ppermute(to_across, 'mesh', neighbours)]
    pallas_call x1, Pallas kernels: 7.5 us -> 8.63 us  [body(): call(functools.partial(prepare_kernel, t=t, blocks=blocks, elements=eleme...]
  transfers between devices with their start and end apart: 3 -> 3, of which waited for: 2 -> 2; matrix products, arithmetic and copies ran while one was open for 0% -> 0% of each run, Pallas kernels for 21% -> 22%
where the time goes in v5:
time: 61.9 us; the launch traced here: 61.6 us
  Pallas kernels  33.1 us (53%)
  waiting for transfers between devices  19 us (31%)
  starting transfers between devices  8.81 us (14%)
  between operations  0.67 us (1%)
    pallas_call x2, Pallas kernels, finish(): call(functools.partial(finish_kernel, t=t, blocks=blocks, elements=elemen...  21.7 us
    all_to_all x1, waiting for transfers between devices, body(): got = lax.all_to_all(sent, 'mesh', split_axis=0, concat_axis=0, tiled=True)  15.6 us
    pallas_call x1, Pallas kernels, body(): call(functools.partial(prepare_kernel, t=t, blocks=blocks, elements=eleme...  8.63 us
    all_to_all x1, starting transfers between devices, body(): got = lax.all_to_all(sent, 'mesh', split_axis=0, concat_axis=0, tiled=True)  5.02 us
    ppermute x1, waiting for transfers between devices, body(): across = lax.ppermute(to_across, 'mesh', neighbours)  3.38 us
    ppermute x1, starting transfers between devices, body(): across = lax.ppermute(to_across, 'mesh', neighbours)  3.04 us
    pallas_call x1, Pallas kernels, body(): call(functools.partial(merge_kernel, t=t, blocks=blocks), final, 0, 4, [p...  2.82 us
  transfers between devices with their start and end apart: 3, of which 2 were waited for; matrix products, arithmetic and copies ran while one was open for 0% of the time, Pallas kernels for 22%

profile of v5, /device:TPU:15, one launch (start us, length us, event | category | flops | bytes accessed | tf_op | source)
XLA Modules:
  0.0 61.6 jit_solution(14457476583707803208)
XLA Ops:
  0.6 8.6 %shard_map.158 = (f32[24,168,128]{2,1,0:T(8,128)}, f32[4608,128]{1,0:T(8,128)}, f32[64,128]{1,0:T(8,128)}, f32[64,128]{1,0:T(8,128)}) custom-call(s32[1,128]{1,0:T(1,128)} %rim_in.1, f32[1200,128]{1,0:T(8,128)} %bitcast.16, f32[24,10,2,640]{3,2,1,0:T(2,128)} %bitcast.14, bf16[256,128]{1,0:T(8,128)(2,1)} %constant.10.clone.back_in, ...), custom_call_target="tpu_custom_call" | custom-call | tf_op jit(solution)/shard_map/pallas_call | solution.py:666
  9.3 0.7 %collective-permute-start = (f32[64,128]{1,0:T(8,128)}, f32[64,128]{1,0:T(8,128)}, u32[]{:S(2)}, u32[]{:S(2)}) collective-permute-start(f32[64,128]{1,0:T(8,128)} %get-tuple-element.13), channel_id=1, source_target_pairs={{0,1},{1,0},{2,3},{3,2},{4,5},{5,4},{6,7},{7,6},{8,9},{9,8},{10,11... | collective-permute-start | bytes 98312 | tf_op jit(solution)/shard_map/ppermute | solution.py:688
  10.0 3.0 %collective-permute-start.1 = (f32[64,128]{1,0:T(8,128)}, f32[64,128]{1,0:T(8,128)}, u32[]{:S(2)}, u32[]{:S(2)}) collective-permute-start(f32[64,128]{1,0:T(8,128)} %get-tuple-element.14), channel_id=1, source_target_pairs={{1,2},{2,1},{3,4},{4,3},{5,6},{6,5},{7,8},{8,7},{9,10},{10,9},{11,... | collective-permute-start | bytes 98312 | tf_op jit(solution)/shard_map/ppermute | solution.py:687
  13.1 0.0 collective-permute-done.partner_in
  13.1 3.4 %collective-permute-done.1.across_in = f32[64,128]{1,0:T(8,128)} collective-permute-done((f32[64,128]{1,0:T(8,128)}, f32[64,128]{1,0:T(8,128)}, u32[]{:S(2)}, u32[]{:S(2)}) %collective-permute-start.1) | collective-permute-done | bytes 32800 | tf_op jit(solution)/shard_map/ppermute | solution.py:687
  16.5 8.0 %shard_map.160 = f32[16,152,128]{2,1,0:T(8,128)} custom-call(s32[384]{0:T(512)} %plan_in.3, s32[24]{0:T(128)} %wet_in.3, s32[10,24]{1,0:T(8,128)} %bitcast.17, s32[24,192]{1,0:T(8,128)} %links_in.3, f32[24,192]{1,0:T(8,128)} %angle_in.3, f32[24,192]{1,0:T(8,128)} %scale_in.3, f32[24,4,64]{2,1,0:T(4,128)} %metric_in.3, ...), custom_call_target="tpu_custom_call" | custom-call | tf_op jit(solution)/shard_map/pallas_call | solution.py:706
  24.5 5.0 %all-to-all-start = ((f32[16,152,128]{2,1,0:T(8,128)}), f32[16,152,128]{2,1,0:T(8,128)}, u32[]{:S(2)}, u32[]{:S(2)}) async-start(f32[16,152,128]{2,1,0:T(8,128)} %shard_map.160), calls=%async_computation | async-start | bytes 2490368 | tf_op jit(solution)/shard_map/all_to_all | solution.py:731
  29.5 13.6 %shard_map.159 = (f32[1200,128]{1,0:T(8,128)}, f32[24,10,2,640]{3,2,1,0:T(2,128)}, s32[128]{0:T(128)}) custom-call(s32[384]{0:T(512)} %plan_in.3, s32[24]{0:T(128)} %wet_in.3, s32[10,24]{1,0:T(8,128)} %bitcast.18, s32[24,192]{1,0:T(8,128)} %links_in.3, f32[24,192]{1,0:T(8,128)} %angle_in.3, f32[24,192]{1,0:T(8,128)} %scale_in.3, f32[24,4,64]{2,1,0:T(4,128)} %metric_in.3, ...), custom_call_target="tpu_custom_call" | custom-call | tf_op jit(solution)/shard_map/pallas_call | solution.py:706
  43.1 15.6 %all-to-all-done.got_in = f32[16,152,128]{2,1,0:T(8,128)} async-done(((f32[16,152,128]{2,1,0:T(8,128)}), f32[16,152,128]{2,1,0:T(8,128)}, u32[]{:S(2)}, u32[]{:S(2)}) %all-to-all-start) | async-done | bytes 1245216 | tf_op jit(solution)/shard_map/all_to_all | solution.py:731
  58.8 2.8 %shard_map.161 = (f32[1200,128]{1,0:T(8,128)}, f32[24,10,2,640]{3,2,1,0:T(2,128)}) custom-call(s32[128]{0:T(128)} %get-tuple-element.15.origin_in, f32[16,152,128]{2,1,0:T(8,128)} %all-to-all-done.got_in, f32[1200,128]{1,0:T(8,128)} %get-tuple-element.16.depth_in, ...), custom_call_target="tpu_custom_call", output_to_operand_aliasing={{0}: (2, {}), {1}: (3, {})} | custom-call | tf_op jit(solution)/shard_map/pallas_call | solution.py:738
Async XLA Ops:
  9.3 3.8 %collective-permute-start = (f32[64,128]{1,0:T(8,128)}, f32[64,128]{1,0:T(8,128)}, u32[]{:S(2)}, u32[]{:S(2)}) collective-permute-start(f32[64,128]{1,0:T(8,128)} %get-tuple-element.13), channel_id=1, source_target_pairs={{0,1},{1,0},{2,3},{3,2},{4,5},{5,4},{6,7},{7,6},{8,9},{9,8},{10,11... | collective-permute-start | bytes 98312 | tf_op jit(solution)/shard_map/ppermute | solution.py:688
  10.0 6.4 %collective-permute-start.1 = (f32[64,128]{1,0:T(8,128)}, f32[64,128]{1,0:T(8,128)}, u32[]{:S(2)}, u32[]{:S(2)}) collective-permute-start(f32[64,128]{1,0:T(8,128)} %get-tuple-element.14), channel_id=1, source_target_pairs={{1,2},{2,1},{3,4},{4,3},{5,6},{6,5},{7,8},{8,7},{9,10},{10,9},{11,... | collective-permute-start | bytes 98312 | tf_op jit(solution)/shard_map/ppermute | solution.py:687
  24.5 34.3 %all-to-all-start = ((f32[16,152,128]{2,1,0:T(8,128)}), f32[16,152,128]{2,1,0:T(8,128)}, u32[]{:S(2)}, u32[]{:S(2)}) async-start(f32[16,152,128]{2,1,0:T(8,128)} %shard_map.160), calls=%async_computation | async-start | bytes 2490368 | tf_op jit(solution)/shard_map/all_to_all | solution.py:731

commit v6 on v5

--- a/solution.py
+++ b/solution.py
@@ -163,14 +163,6 @@
     return fields[block, pl.ds(comp + c - 1, comp, stride=2), :]
 
 
-def weave(*lists):
-    count = max(len(steps) for steps in lists)
-    for i in range(count):
-        for steps in lists:
-            for step in steps[len(steps) * i // count : len(steps) * (i + 1) // count]:
-                step()
-
-
 def place_face(pieces, c, wide, lane):
     moved = [pltpu.roll(p, ((i - c) * wide) % LANES, 1) if i != c else p for i, p in enumerate(pieces)]
     return jnp.where(lane < wide, moved[0], jnp.where(lane < 2 * wide, moved[1], moved[2]))
@@ -192,14 +184,14 @@
 
 
 def prepare_kernel(
-    rim_in, depth_in, flow_in, back_in, eye_in, fields_out, pool_out, partner, across,
+    rim_in, depth_in, flow_in, back_in, eye_in, fields_out, pool_out, across, partner,
     rim, depth, flow, back, eye, fields, pool, halves, sems, *, t, blocks, elements,
 ):
     comp, pairs, members, wide = t["comp"], t["pairs"], t["members"], t["wide"]
     odd = lax.axis_index("mesh") % 2
     tiles = blocks // 8
     steps = blocks // 2
-    group = 8 * 3 * elements
+    group = 2 * 3 * elements
     first = start_all(
         [
             pltpu.make_async_copy(depth_in, depth, sems.at[0]), pltpu.make_async_copy(back_in, back, sems.at[1]),
@@ -211,84 +203,73 @@
         rows = pl.ds(8 * tile, 8)
         return pltpu.make_async_copy(flow_in.at[rows], flow.at[rows], sems.at[4 + tile])
 
-    def field_part(i, slot):
-        return pltpu.make_async_copy(
-            fields.at[slot], fields_out.at[pl.ds(2 * i, 2)], sems.at[4 + 2 * tiles + slot]
-        )
-
-    def pool_part(tile):
-        lines = pl.ds(group * tile, group)
-        return pltpu.make_async_copy(pool.at[lines], pool_out.at[lines], sems.at[4 + tiles + tile])
+    def field_part(tile):
+        rows = pl.ds(8 * tile, 8)
+        return pltpu.make_async_copy(fields.at[rows], fields_out.at[rows], sems.at[4 + tiles + tile])
+
+    def pool_part(i):
+        lines = pl.ds(group * i, group)
+        return pltpu.make_async_copy(pool.at[lines], pool_out.at[lines], sems.at[4 + 2 * tiles + i])
 
     start_all([part(tile) for tile in range(tiles)])
-    for slot in range(2):
+    wait_all(first)
+
+    def build(i):
         for u in range(2):
-            fields[slot, u, comp - 8 : comp] = jnp.full((8, LANES), 1.0, jnp.float32)
-            fields[slot, u, 3 * comp - 16 : 3 * comp] = jnp.zeros((16, LANES), jnp.float32)
-    wait_all(first)
-
-    def build(i, slot):
-        def scenario(u, s):
             b = 2 * i + u
             tile, sub = b // 8, b % 8
-            start = (s * tiles + tile) * pairs * 8 + sub
-            fields[slot, u, s * pairs : (s + 1) * pairs] = depth[pl.ds(start, pairs, stride=8), :]
-            for j in range(pairs):
-                row = comp + 2 * (s * pairs + j)
-                fields[slot, u, row : row + 2] = flow[b, s, :, j * LANES : (j + 1) * LANES]
-
-        return [functools.partial(scenario, u, s) for u in range(2) for s in range(members)]
-
-    def turn_of(slot):
-        def component(c):
-            pair = fields.at[slot]
-            turn_rows(rows_of(pair, 0, c, comp), rows_of(pair, 1, c, comp), c, eye, None, halves.at[slot], comp)
-
-        return [functools.partial(component, c) for c in range(3)]
-
-    def faces_of(i, slot):
+            fields[b, comp - 8 : comp] = jnp.full((8, LANES), 1.0, jnp.float32)
+            fields[b, 3 * comp - 16 : 3 * comp] = jnp.zeros((16, LANES), jnp.float32)
+            for s in range(members):
+                start = (s * tiles + tile) * pairs * 8 + sub
+                fields[b, s * pairs : (s + 1) * pairs] = depth[pl.ds(start, pairs, stride=8), :]
+                for j in range(pairs):
+                    row = comp + 2 * (s * pairs + j)
+                    fields[b, row : row + 2] = flow[b, s, :, j * LANES : (j + 1) * LANES]
+
+    def turn_of(i):
+        for c in range(3):
+            turn_rows(
+                rows_of(fields, 2 * i, c, comp), rows_of(fields, 2 * i + 1, c, comp), c, eye, None, halves, comp
+            )
+
+    def faces_of(i):
+        rows = mm(halves[...], back[...])
         lane = lax.broadcasted_iota(jnp.int32, (LANES, LANES), 1)
-        pieces = []
-
-        def multiply():
-            rows = mm(halves[slot], back[...])
-            pieces.extend(rows[c * LANES : (c + 1) * LANES] for c in range(3))
-
-        def face(f, u):
-            span = slice(u * elements, (u + 1) * elements)
-            at = ((2 * i + u) * 3 + f) * elements
-            pool[pl.ds(at, elements), :] = place_face([p[span] for p in pieces], f, wide, lane[span])
-
-        return [multiply] + [functools.partial(face, f, u) for u in range(2) for f in range(3)]
+        pieces = [rows[c * LANES : (c + 1) * LANES] for c in range(3)]
+        for f in range(3):
+            face = place_face(pieces, f, wide, lane)
+            for u in range(2):
+                at = ((2 * i + u) * 3 + f) * elements
+                pool[pl.ds(at, elements), :] = face[u * elements : (u + 1) * elements]
 
     part(0).wait()
-    weave(build(0, 0))
-    field_part(0, 0).start()
-    weave(build(1, 1), turn_of(0))
-    field_part(1, 1).start()
-
-    def one(h, carry):
-        i = 2 * h
-
-        @pl.when(h % 2 == 0)
+    build(0)
+    turn_of(0)
+    build(1)
+
+    def one(i, carry):
+        @pl.when(i % 4 == 0)
         def _():
-            part(h // 2).wait()
-
-        for slot in range(2):
-            field_part(i - 2 + slot, slot).wait()
-            weave(build(i + slot, slot), turn_of(1 - slot), faces_of(i - 2 + slot, slot))
-            field_part(i + slot, slot).start()
-
-        @pl.when(h % 2 == 0)
+            part(i // 4).wait()
+
+        faces_of(i - 2)
+        turn_of(i - 1)
+        build(i)
+        pool_part(i - 2).start()
+
+        @pl.when(i % 4 == 3)
         def _():
-            pool_part(h // 2 - 1).start()
+            field_part(i // 4).start()
 
         return carry
 
-    lax.fori_loop(1, steps // 2, one, 0)
-    weave(turn_of(1), faces_of(steps - 2, 0))
-    weave(faces_of(steps - 1, 1))
-    pool_part(tiles - 1).start()
+    lax.fori_loop(2, steps, one, 0)
+    faces_of(steps - 2)
+    turn_of(steps - 1)
+    pool_part(steps - 2).start()
+    faces_of(steps - 1)
+    pool_part(steps - 1).start()
     width = partner.shape[0]
     near, far = (1 - odd) * width, odd * width
 
@@ -300,10 +281,10 @@
         return carry
 
     lax.fori_loop(0, width // 32, pick, 0)
-    for slot in range(2):
-        field_part(steps - 2 + slot, slot).wait()
     for tile in range(tiles):
-        pool_part(tile).wait()
+        field_part(tile).wait()
+    for i in range(steps):
+        pool_part(i).wait()
 
 
 def scan_moves(plan, base, order, place, blocks):
@@ -447,9 +428,9 @@
     far_rows = pl.multiple_of(faces + odd * width, 8)
     loads = [
         (plan_in, plan), (angle_in, angle), (scale_in, scale), (links_in, links), (metric_in, metric),
-        (wet_in, wet), (breach_in, breach), (eye_in, eye), (own_in, own), (fields_in, fields),
-        (pool_in, pool.at[pl.ds(0, faces)]), (partner_in, pool.at[pl.ds(near_rows, width)]),
-        (across_in, pool.at[pl.ds(far_rows, width)]), (spread_in, spread), (matrix_in, matrix),
+        (fields_in, fields), (wet_in, wet), (breach_in, breach), (eye_in, eye), (own_in, own),
+        (spread_in, spread), (matrix_in, matrix), (pool_in, pool.at[pl.ds(0, faces)]),
+        (partner_in, pool.at[pl.ds(near_rows, width)]), (across_in, pool.at[pl.ds(far_rows, width)]),
     ]
     n = len(loads)
     loads = start_all([pltpu.make_async_copy(a, b, sems.at[i]) for i, (a, b) in enumerate(loads)])
@@ -462,7 +443,7 @@
     steps = (end - begin + 2 * n_pairs - 1) // (2 * n_pairs)
 
     def at(i, u):
-        return jnp.minimum(begin + 2 * n_pairs * i + u, end - 1)
+        return jnp.maximum(jnp.minimum(begin + 2 * n_pairs * i + u, end - 1), 0)
 
     def indices(i):
         return [
@@ -482,32 +463,32 @@
     face_rows(angle, scale, links, metric, coefs, blocks, elements)
     if not leaving:
         scan_origins(plan, index, scratch[2], blocks, devices)
-    wait_all(loads[5:])
+    wait_all(loads[5:-3])
     chunks = row_chunks(16)
-    rows_to_pick = [
-        (u, f, e) for u in range(2) for f in range(3) for e in range(elements)
-    ]
-
-    def pick(w, some):
-        for u, f, e in some:
-            row = f * LANES + u * elements + e
-            outer[w, row : row + 1, :] = pool[pl.ds(near[2 * w + u, f * elements + e], 1), :]
+
+    def pick(w, rows):
+        for f in range(3):
+            for line in range(rows.start, rows.stop):
+                v = near[2 * w + line // elements, f * elements + line % elements]
+                outer[w, f * LANES + line : f * LANES + line + 1, :] = pool[pl.ds(v, 1), :]
+
+    def pair_of(i, w):
+        return [order[at(i, 2 * w + u)] for u in range(2)]
+
+    def lay_out(w, pair):
+        for c in range(3):
+            turn_rows(
+                rows_of(fields, pair[0], c, comp), rows_of(fields, pair[1], c, comp), c, eye,
+                turned.at[w], halves.at[w], comp,
+            )
+        inner = mm(halves[w], own[...])
+        for c in range(3):
+            traces[w, c] = inner[c * LANES : (c + 1) * LANES]
+        spread_pair(coefs, pair, eye, spread, factors.at[w], elements)
 
     def one(i, carry):
-        both = [[order[at(i, 2 * w + u)] for u in range(2)] for w in range(2)]
-        inflow = [None, None]
-
-        def lay_out(w):
-            for c in range(3):
-                turn_rows(
-                    rows_of(fields, both[w][0], c, comp), rows_of(fields, both[w][1], c, comp), c, eye,
-                    turned.at[w], halves.at[w], comp,
-                )
-            inner = mm(halves[w], own[...])
-            for c in range(3):
-                traces[w, c] = inner[c * LANES : (c + 1) * LANES]
-            spread_pair(coefs, both[w], eye, spread, factors.at[w], elements)
-            inflow[w] = inflow_rows(breach, both[w], t)
+        both = [pair_of(i, w) for w in range(2)]
+        inflow = [inflow_rows(breach, pair, t) for pair in both]
 
         def fluxes(w, rows):
             volume_rows(rows, turned.at[w], factors.at[w], 4, inflow[w][rows.start // elements], pieces.at[w])
@@ -538,17 +519,16 @@
 
                         send(p).start()
                 else:
-                    write_block(both[w][u], staged.at[2 * w + u], scratch[0], scratch[1], t, blocks)
+                    write_depth(both[w][u], staged.at[2 * w + u], scratch[0], t, blocks)
+                    write_flow(both[w][u], staged.at[2 * w + u], scratch[1], t)
 
         wait_all(indices(i))
-        pick(0, rows_to_pick)
-        lay_out(0)
-        share = len(rows_to_pick) // len(chunks)
-        for k, rows in enumerate(chunks):
+        for rows in chunks:
+            pick(0, rows)
+        lay_out(1, both[1])
+        for rows in chunks:
             fluxes(0, rows)
-            pick(1, rows_to_pick[k * share : (k + 1) * share])
-            if k == 1:
-                lay_out(1)
+            pick(1, rows)
         for k, rows in enumerate(chunks):
             if k < 3:
                 combine(0, k)
@@ -559,11 +539,14 @@
         @pl.when(i + 1 < steps)
         def _():
             start_all(indices(i + 1))
+            lay_out(0, pair_of(i + 1, 0))
 
         hand_over(0)
         hand_over(1)
         return carry
 
+    lay_out(0, pair_of(0, 0))
+    wait_all(loads[-3:])
     lax.fori_loop(0, steps, one, 0)
     if leaving:
 
@@ -577,12 +560,17 @@
         wait_all(start_all([pltpu.make_async_copy(a, b, sems.at[n + 2 * n_pairs + i]) for i, (a, b) in enumerate(kept)]))
 
 
-def write_block(b, rows, depth, flow, t, blocks):
-    pairs, members, used = t["pairs"], t["members"], t["used"]
+def write_depth(b, rows, depth, t, blocks):
+    pairs, members = t["pairs"], t["members"]
     tile, sub = b // 8, b % 8
     for s in range(members):
         start = (s * (blocks // 8) + tile) * pairs * 8 + sub
         depth[pl.ds(start, pairs, stride=8), :] = rows[s * pairs : (s + 1) * pairs]
+
+
+def write_flow(b, rows, flow, t):
+    pairs, members, used = t["pairs"], t["members"], t["used"]
+    for s in range(members):
         for j in range(pairs):
             row = used + 2 * (s * pairs + j)
             flow[b, s, :, j * LANES : (j + 1) * LANES] = rows[row : row + 2]
@@ -602,12 +590,23 @@
     )
     wait_all(loads)
 
+    def put_depth(b, carry):
+        @pl.when(origin[b] >= 0)
+        def _():
+            write_depth(b, got.at[origin[b]], depth, t, blocks)
+
+        return carry
+
+    lax.fori_loop(0, blocks, put_depth, 0)
+    back = pltpu.make_async_copy(depth, depth_out, sems.at[2])
+    back.start()
+
     def put(b, k):
         came = origin[b] >= 0
 
         @pl.when(came)
         def _():
-            write_block(b, got.at[origin[b]], depth, flow, t, blocks)
+            write_flow(b, got.at[origin[b]], flow, t)
 
             @pl.when(k >= RING)
             def _():
@@ -618,8 +617,6 @@
         return k + came.astype(jnp.int32)
 
     arrivals = lax.fori_loop(0, blocks, put, jnp.int32(0))
-    back = pltpu.make_async_copy(depth, depth_out, sems.at[2])
-    back.start()
 
     def drain(k, carry):
         leave(0, k).wait()
@@ -663,7 +660,7 @@
 
     back = jnp.asarray(np.tile(t["back"], (2, 1)), bf16)
     eye = jnp.asarray(np.tile(np.eye(LANES), (1, 2)), bf16)
-    fields, pool, to_partner, to_across = call(
+    fields, pool, to_across, to_partner = call(
         functools.partial(prepare_kernel, t=t, blocks=blocks, elements=elements),
         (
             jax.ShapeDtypeStruct((blocks, 3 * comp, LANES), f32),
@@ -675,8 +672,8 @@
         [
             pltpu.SMEM(rim_faces.shape, jnp.int32), pltpu.VMEM(depth_rows.shape, f32), pltpu.VMEM(flow_rows.shape, f32), pltpu.VMEM(back.shape, bf16),
             pltpu.VMEM(eye.shape, bf16),
-            pltpu.VMEM((2, 2, 3 * comp, LANES), f32), pltpu.VMEM((faces, LANES), f32),
-            pltpu.VMEM((2, 3 * LANES, 2 * LANES), bf16), dma((6 + 2 * tiles,)),
+            pltpu.VMEM((blocks, 3 * comp, LANES), f32), pltpu.VMEM((faces, LANES), f32),
+            pltpu.VMEM((3 * LANES, 2 * LANES), bf16), dma((4 + 2 * tiles + blocks // 2,)),
         ],
         (HBM, HBM, VMEM, VMEM),
     )(rim_faces, depth_rows, flow_rows, back, eye)
@@ -684,8 +681,8 @@
     count = lax.axis_size("mesh")
     partners = [(i, i ^ 1) for i in range(count)]
     neighbours = [(i, i + 1 if i % 2 else i - 1) for i in range(1, count - 1)]
+    partner = lax.ppermute(to_partner, "mesh", partners)
     across = lax.ppermute(to_across, "mesh", neighbours)
-    partner = lax.ppermute(to_partner, "mesh", partners)
 
     lift_h, lift_l = high_low(t["lift"])
     along_r, along_s = t["along"]

time: 61.9 us -> 60.2 us (0.973)
  Pallas kernels: 33.1 us -> 32 us
    pallas_call x1, Pallas kernels: 8.63 us -> 6.99 us  [body(): call(functools.partial(prepare_kernel, t=t, blocks=blocks, elements=eleme...]
  transfers between devices with their start and end apart: 3 -> 3, of which waited for: 2 -> 2; matrix products, arithmetic and copies ran while one was open for 0% -> 0% of each run, Pallas kernels for 22% -> 24%
where the time goes in v6:
time: 60.2 us; the launch traced here: 60 us
  Pallas kernels  32 us (53%)
  waiting for transfers between devices  18.5 us (31%)
  starting transfers between devices  8.83 us (15%)
  between operations  0.67 us (1%)
    pallas_call x2, Pallas kernels, finish(): call(functools.partial(finish_kernel, t=t, blocks=blocks, elements=elemen...  22.1 us
    all_to_all x1, waiting for transfers between devices, body(): got = lax.all_to_all(sent, 'mesh', split_axis=0, concat_axis=0, tiled=True)  15.1 us
    pallas_call x1, Pallas kernels, body(): call(functools.partial(prepare_kernel, t=t, blocks=blocks, elements=eleme...  6.99 us
    all_to_all x1, starting transfers between devices, body(): got = lax.all_to_all(sent, 'mesh', split_axis=0, concat_axis=0, tiled=True)  5.04 us
    ppermute x1, waiting for transfers between devices, body(): across = lax.ppermute(to_across, 'mesh', neighbours)  3.37 us
    ppermute x1, starting transfers between devices, body(): across = lax.ppermute(to_across, 'mesh', neighbours)  3.05 us
    pallas_call x1, Pallas kernels, body(): call(functools.partial(merge_kernel, t=t, blocks=blocks), final, 0, 4, [p...  2.92 us
  transfers between devices with their start and end apart: 3, of which 2 were waited for; matrix products, arithmetic and copies ran while one was open for 0% of the time, Pallas kernels for 24%

profile of v6, /device:TPU:15, one launch (start us, length us, event | category | flops | bytes accessed | tf_op | source)
XLA Modules:
  0.0 60.0 jit_solution(2744377937248379206)
XLA Ops:
  0.6 7.0 %shard_map.158 = (f32[24,168,128]{2,1,0:T(8,128)}, f32[4608,128]{1,0:T(8,128)}, f32[64,128]{1,0:T(8,128)}, f32[64,128]{1,0:T(8,128)}) custom-call(s32[1,128]{1,0:T(1,128)} %rim_in.1, f32[1200,128]{1,0:T(8,128)} %bitcast.16, f32[24,10,2,640]{3,2,1,0:T(2,128)} %bitcast.14, bf16[256,128]{1,0:T(8,128)(2,1)} %constant.10.clone.back_in, ...), custom_call_target="tpu_custom_call" | custom-call | tf_op jit(solution)/shard_map/pallas_call | solution.py:663
  7.6 0.7 %collective-permute-start = (f32[64,128]{1,0:T(8,128)}, f32[64,128]{1,0:T(8,128)}, u32[]{:S(2)}, u32[]{:S(2)}) collective-permute-start(f32[64,128]{1,0:T(8,128)} %get-tuple-element.13), channel_id=1, source_target_pairs={{0,1},{1,0},{2,3},{3,2},{4,5},{5,4},{6,7},{7,6},{8,9},{9,8},{10,11... | collective-permute-start | bytes 98312 | tf_op jit(solution)/shard_map/ppermute | solution.py:684
  8.4 3.1 %collective-permute-start.1 = (f32[64,128]{1,0:T(8,128)}, f32[64,128]{1,0:T(8,128)}, u32[]{:S(2)}, u32[]{:S(2)}) collective-permute-start(f32[64,128]{1,0:T(8,128)} %get-tuple-element.14), channel_id=1, source_target_pairs={{1,2},{2,1},{3,4},{4,3},{5,6},{6,5},{7,8},{8,7},{9,10},{10,9},{11,... | collective-permute-start | bytes 98312 | tf_op jit(solution)/shard_map/ppermute | solution.py:685
  11.4 0.0 collective-permute-done.partner_in
  11.4 3.4 %collective-permute-done.1.across_in = f32[64,128]{1,0:T(8,128)} collective-permute-done((f32[64,128]{1,0:T(8,128)}, f32[64,128]{1,0:T(8,128)}, u32[]{:S(2)}, u32[]{:S(2)}) %collective-permute-start.1) | collective-permute-done | bytes 32800 | tf_op jit(solution)/shard_map/ppermute | solution.py:685
  14.8 7.9 %shard_map.160 = f32[16,152,128]{2,1,0:T(8,128)} custom-call(s32[384]{0:T(512)} %plan_in.3, s32[24]{0:T(128)} %wet_in.3, s32[10,24]{1,0:T(8,128)} %bitcast.17, s32[24,192]{1,0:T(8,128)} %links_in.3, f32[24,192]{1,0:T(8,128)} %angle_in.3, f32[24,192]{1,0:T(8,128)} %scale_in.3, f32[24,4,64]{2,1,0:T(4,128)} %metric_in.3, ...), custom_call_target="tpu_custom_call" | custom-call | tf_op jit(solution)/shard_map/pallas_call | solution.py:703
  22.7 5.0 %all-to-all-start = ((f32[16,152,128]{2,1,0:T(8,128)}), f32[16,152,128]{2,1,0:T(8,128)}, u32[]{:S(2)}, u32[]{:S(2)}) async-start(f32[16,152,128]{2,1,0:T(8,128)} %shard_map.160), calls=%async_computation | async-start | bytes 2490368 | tf_op jit(solution)/shard_map/all_to_all | solution.py:728
  27.8 14.2 %shard_map.159 = (f32[1200,128]{1,0:T(8,128)}, f32[24,10,2,640]{3,2,1,0:T(2,128)}, s32[128]{0:T(128)}) custom-call(s32[384]{0:T(512)} %plan_in.3, s32[24]{0:T(128)} %wet_in.3, s32[10,24]{1,0:T(8,128)} %bitcast.18, s32[24,192]{1,0:T(8,128)} %links_in.3, f32[24,192]{1,0:T(8,128)} %angle_in.3, f32[24,192]{1,0:T(8,128)} %scale_in.3, f32[24,4,64]{2,1,0:T(4,128)} %metric_in.3, ...), custom_call_target="tpu_custom_call" | custom-call | tf_op jit(solution)/shard_map/pallas_call | solution.py:703
  41.9 15.1 %all-to-all-done.got_in = f32[16,152,128]{2,1,0:T(8,128)} async-done(((f32[16,152,128]{2,1,0:T(8,128)}), f32[16,152,128]{2,1,0:T(8,128)}, u32[]{:S(2)}, u32[]{:S(2)}) %all-to-all-start) | async-done | bytes 1245216 | tf_op jit(solution)/shard_map/all_to_all | solution.py:728
  57.0 2.9 %shard_map.161 = (f32[1200,128]{1,0:T(8,128)}, f32[24,10,2,640]{3,2,1,0:T(2,128)}) custom-call(s32[128]{0:T(128)} %get-tuple-element.15.origin_in, f32[16,152,128]{2,1,0:T(8,128)} %all-to-all-done.got_in, f32[1200,128]{1,0:T(8,128)} %get-tuple-element.16.depth_in, ...), custom_call_target="tpu_custom_call", output_to_operand_aliasing={{0}: (2, {}), {1}: (3, {})} | custom-call | tf_op jit(solution)/shard_map/pallas_call | solution.py:735
Async XLA Ops:
  7.6 3.8 %collective-permute-start = (f32[64,128]{1,0:T(8,128)}, f32[64,128]{1,0:T(8,128)}, u32[]{:S(2)}, u32[]{:S(2)}) collective-permute-start(f32[64,128]{1,0:T(8,128)} %get-tuple-element.13), channel_id=1, source_target_pairs={{0,1},{1,0},{2,3},{3,2},{4,5},{5,4},{6,7},{7,6},{8,9},{9,8},{10,11... | collective-permute-start | bytes 98312 | tf_op jit(solution)/shard_map/ppermute | solution.py:684
  8.4 6.4 %collective-permute-start.1 = (f32[64,128]{1,0:T(8,128)}, f32[64,128]{1,0:T(8,128)}, u32[]{:S(2)}, u32[]{:S(2)}) collective-permute-start(f32[64,128]{1,0:T(8,128)} %get-tuple-element.14), channel_id=1, source_target_pairs={{1,2},{2,1},{3,4},{4,3},{5,6},{6,5},{7,8},{8,7},{9,10},{10,9},{11,... | collective-permute-start | bytes 98312 | tf_op jit(solution)/shard_map/ppermute | solution.py:685
  22.7 34.3 %all-to-all-start = ((f32[16,152,128]{2,1,0:T(8,128)}), f32[16,152,128]{2,1,0:T(8,128)}, u32[]{:S(2)}, u32[]{:S(2)}) async-start(f32[16,152,128]{2,1,0:T(8,128)} %shard_map.160), calls=%async_computation | async-start | bytes 2490368 | tf_op jit(solution)/shard_map/all_to_all | solution.py:728

commit v7 on v6

--- a/solution.py
+++ b/solution.py
@@ -579,51 +579,51 @@
 def merge_kernel(
     origin_in, got_in, depth_in, flow_in, depth_out, flow_out, origin, depth, flow, got, sems, *, t, blocks
 ):
-    def leave(b, k):
-        return pltpu.make_async_copy(flow.at[b], flow_out.at[b], sems.at[3 + k % RING])
-
+    pairs, members = t["pairs"], t["members"]
     loads = start_all(
         [
             pltpu.make_async_copy(a, b, sems.at[i])
-            for i, (a, b) in enumerate(((origin_in, origin), (got_in, got), (depth_in, depth)))
+            for i, (a, b) in enumerate(((origin_in, origin), (got_in, got)))
         ]
     )
     wait_all(loads)
 
-    def put_depth(b, carry):
-        @pl.when(origin[b] >= 0)
-        def _():
-            write_depth(b, got.at[origin[b]], depth, t, blocks)
-
-        return carry
-
-    lax.fori_loop(0, blocks, put_depth, 0)
-    back = pltpu.make_async_copy(depth, depth_out, sems.at[2])
-    back.start()
+    def flow_part(b, k):
+        return pltpu.make_async_copy(flow.at[b], flow_out.at[b], sems.at[2 + k % RING])
+
+    def depth_part(b, k):
+        return pltpu.make_async_copy(
+            depth.at[b], depth_out.at[:, b // 8, :, b % 8], sems.at[2 + RING + k % RING]
+        )
+
+    def settle(k):
+        flow_part(0, k).wait()
+        depth_part(0, k).wait()
 
     def put(b, k):
         came = origin[b] >= 0
 
         @pl.when(came)
         def _():
-            write_flow(b, got.at[origin[b]], flow, t)
-
             @pl.when(k >= RING)
             def _():
-                leave(b, k).wait()
-
-            leave(b, k).start()
+                settle(k)
+
+            for s in range(members):
+                depth[b, s] = got[origin[b], s * pairs : (s + 1) * pairs]
+            depth_part(b, k).start()
+            write_flow(b, got.at[origin[b]], flow, t)
+            flow_part(b, k).start()
 
         return k + came.astype(jnp.int32)
 
     arrivals = lax.fori_loop(0, blocks, put, jnp.int32(0))
 
     def drain(k, carry):
-        leave(0, k).wait()
+        settle(k)
         return carry
 
     lax.fori_loop(jnp.maximum(arrivals - RING, 0), arrivals, drain, 0)
-    back.wait()
 
 
 SMEM = pl.BlockSpec(memory_space=pltpu.SMEM)
@@ -732,14 +732,18 @@
         False, (*final, jax.ShapeDtypeStruct((LANES,), i32)),
         [pltpu.VMEM((2 * n_pairs, *block_rows), f32), *whole, pltpu.SMEM((LANES,), i32)],
     )
+    tall = (members, tiles, pairs, 8, LANES)
     depth_new, flow_new = call(
         functools.partial(merge_kernel, t=t, blocks=blocks),
-        final,
+        (jax.ShapeDtypeStruct(tall, f32), final[1]),
         0, 4,
-        [pltpu.SMEM((LANES,), i32), *whole, pltpu.VMEM((count, packed, LANES), f32), dma((3 + RING,))],
+        [
+            pltpu.SMEM((LANES,), i32), pltpu.VMEM((blocks, members, pairs, LANES), f32), whole[1],
+            pltpu.VMEM((count, packed, LANES), f32), dma((2 + 2 * RING,)),
+        ],
         (HBM, HBM),
         input_output_aliases={2: 0, 3: 1},
-    )(origin, got, depth_kept, flow_kept)
+    )(origin, got, depth_kept.reshape(tall), flow_kept)
     depth_out = depth_new.reshape(members, tiles, pairs, 8, LANES).transpose(1, 3, 0, 2, 4).reshape(water_depth.shape)
     return depth_out, flow_new.transpose(0, 2, 1, 3)
 

time: 60.2 us -> 60 us (level)
  no operation moved by 1% of the time
where the time goes in v7:
time: 60 us; the launch traced here: 59.6 us
  Pallas kernels  31.7 us (53%)
  waiting for transfers between devices  18.5 us (31%)
  starting transfers between devices  8.78 us (15%)
  between operations  0.67 us (1%)
    pallas_call x2, Pallas kernels, finish(): call(functools.partial(finish_kernel, t=t, blocks=blocks, elements=elemen...  22.1 us
    all_to_all x1, waiting for transfers between devices, body(): got = lax.all_to_all(sent, 'mesh', split_axis=0, concat_axis=0, tiled=True)  15.1 us
    pallas_call x1, Pallas kernels, body(): call(functools.partial(prepare_kernel, t=t, blocks=blocks, elements=eleme...  6.99 us
    all_to_all x1, starting transfers between devices, body(): got = lax.all_to_all(sent, 'mesh', split_axis=0, concat_axis=0, tiled=True)  4.99 us
    ppermute x1, waiting for transfers between devices, body(): across = lax.ppermute(to_across, 'mesh', neighbours)  3.37 us
    ppermute x1, starting transfers between devices, body(): across = lax.ppermute(to_across, 'mesh', neighbours)  3.05 us
    pallas_call x1, Pallas kernels, body(): call(functools.partial(merge_kernel, t=t, blocks=blocks), (jax.ShapeDtype...  2.56 us
  transfers between devices with their start and end apart: 3, of which 2 were waited for; matrix products, arithmetic and copies ran while one was open for 0% of the time, Pallas kernels for 24%

profile of v7, /device:TPU:15, one launch (start us, length us, event | category | flops | bytes accessed | tf_op | source)
XLA Modules:
  0.0 59.6 jit_solution(16115788205516478980)
XLA Ops:
  0.6 7.0 %shard_map.158 = (f32[24,168,128]{2,1,0:T(8,128)}, f32[4608,128]{1,0:T(8,128)}, f32[64,128]{1,0:T(8,128)}, f32[64,128]{1,0:T(8,128)}) custom-call(s32[1,128]{1,0:T(1,128)} %rim_in.1, f32[1200,128]{1,0:T(8,128)} %bitcast.16, f32[24,10,2,640]{3,2,1,0:T(2,128)} %bitcast.13, bf16[256,128]{1,0:T(8,128)(2,1)} %constant.10.clone.back_in, ...), custom_call_target="tpu_custom_call" | custom-call | tf_op jit(solution)/shard_map/pallas_call | solution.py:663
  7.6 0.7 %collective-permute-start = (f32[64,128]{1,0:T(8,128)}, f32[64,128]{1,0:T(8,128)}, u32[]{:S(2)}, u32[]{:S(2)}) collective-permute-start(f32[64,128]{1,0:T(8,128)} %get-tuple-element.13), channel_id=1, source_target_pairs={{0,1},{1,0},{2,3},{3,2},{4,5},{5,4},{6,7},{7,6},{8,9},{9,8},{10,11... | collective-permute-start | bytes 98312 | tf_op jit(solution)/shard_map/ppermute | solution.py:684
  8.4 3.1 %collective-permute-start.1 = (f32[64,128]{1,0:T(8,128)}, f32[64,128]{1,0:T(8,128)}, u32[]{:S(2)}, u32[]{:S(2)}) collective-permute-start(f32[64,128]{1,0:T(8,128)} %get-tuple-element.14), channel_id=1, source_target_pairs={{1,2},{2,1},{3,4},{4,3},{5,6},{6,5},{7,8},{8,7},{9,10},{10,9},{11,... | collective-permute-start | bytes 98312 | tf_op jit(solution)/shard_map/ppermute | solution.py:685
  11.4 0.0 collective-permute-done.partner_in
  11.4 3.4 %collective-permute-done.1.across_in = f32[64,128]{1,0:T(8,128)} collective-permute-done((f32[64,128]{1,0:T(8,128)}, f32[64,128]{1,0:T(8,128)}, u32[]{:S(2)}, u32[]{:S(2)}) %collective-permute-start.1) | collective-permute-done | bytes 32800 | tf_op jit(solution)/shard_map/ppermute | solution.py:685
  14.8 8.0 %shard_map.160 = f32[16,152,128]{2,1,0:T(8,128)} custom-call(s32[384]{0:T(512)} %plan_in.3, s32[24]{0:T(128)} %wet_in.3, s32[10,24]{1,0:T(8,128)} %bitcast.17, s32[24,192]{1,0:T(8,128)} %links_in.3, f32[24,192]{1,0:T(8,128)} %angle_in.3, f32[24,192]{1,0:T(8,128)} %scale_in.3, f32[24,4,64]{2,1,0:T(4,128)} %metric_in.3, ...), custom_call_target="tpu_custom_call" | custom-call | tf_op jit(solution)/shard_map/pallas_call | solution.py:703
  22.8 5.0 %all-to-all-start = ((f32[16,152,128]{2,1,0:T(8,128)}), f32[16,152,128]{2,1,0:T(8,128)}, u32[]{:S(2)}, u32[]{:S(2)}) async-start(f32[16,152,128]{2,1,0:T(8,128)} %shard_map.160), calls=%async_computation | async-start | bytes 2490368 | tf_op jit(solution)/shard_map/all_to_all | solution.py:728
  27.8 14.2 %shard_map.159 = (f32[1200,128]{1,0:T(8,128)}, f32[24,10,2,640]{3,2,1,0:T(2,128)}, s32[128]{0:T(128)}) custom-call(s32[384]{0:T(512)} %plan_in.3, s32[24]{0:T(128)} %wet_in.3, s32[10,24]{1,0:T(8,128)} %bitcast.18, s32[24,192]{1,0:T(8,128)} %links_in.3, f32[24,192]{1,0:T(8,128)} %angle_in.3, f32[24,192]{1,0:T(8,128)} %scale_in.3, f32[24,4,64]{2,1,0:T(4,128)} %metric_in.3, ...), custom_call_target="tpu_custom_call" | custom-call | tf_op jit(solution)/shard_map/pallas_call | solution.py:703
  41.9 15.1 %all-to-all-done.got_in = f32[16,152,128]{2,1,0:T(8,128)} async-done(((f32[16,152,128]{2,1,0:T(8,128)}), f32[16,152,128]{2,1,0:T(8,128)}, u32[]{:S(2)}, u32[]{:S(2)}) %all-to-all-start) | async-done | bytes 1245216 | tf_op jit(solution)/shard_map/all_to_all | solution.py:728
  57.0 2.6 %shard_map.161 = (f32[10,3,5,8,128]{4,3,2,1,0:T(8,128)}, f32[24,10,2,640]{3,2,1,0:T(2,128)}) custom-call(s32[128]{0:T(128)} %get-tuple-element.15.origin_in, f32[16,152,128]{2,1,0:T(8,128)} %all-to-all-done.got_in, f32[10,3,5,8,128]{4,3,2,1,0:T(8,128)} %bitcast.14, ...), custom_call_target="tpu_custom_call", output_to_operand_aliasing={{0}: (2, {}), {1}: (3, {})} | custom-call | tf_op jit(solution)/shard_map/pallas_call | solution.py:736
Async XLA Ops:
  7.6 3.8 %collective-permute-start = (f32[64,128]{1,0:T(8,128)}, f32[64,128]{1,0:T(8,128)}, u32[]{:S(2)}, u32[]{:S(2)}) collective-permute-start(f32[64,128]{1,0:T(8,128)} %get-tuple-element.13), channel_id=1, source_target_pairs={{0,1},{1,0},{2,3},{3,2},{4,5},{5,4},{6,7},{7,6},{8,9},{9,8},{10,11... | collective-permute-start | bytes 98312 | tf_op jit(solution)/shard_map/ppermute | solution.py:684
  8.4 6.4 %collective-permute-start.1 = (f32[64,128]{1,0:T(8,128)}, f32[64,128]{1,0:T(8,128)}, u32[]{:S(2)}, u32[]{:S(2)}) collective-permute-start(f32[64,128]{1,0:T(8,128)} %get-tuple-element.14), channel_id=1, source_target_pairs={{1,2},{2,1},{3,4},{4,3},{5,6},{6,5},{7,8},{8,7},{9,10},{10,9},{11,... | collective-permute-start | bytes 98312 | tf_op jit(solution)/shard_map/ppermute | solution.py:685
  22.8 34.3 %all-to-all-start = ((f32[16,152,128]{2,1,0:T(8,128)}), f32[16,152,128]{2,1,0:T(8,128)}, u32[]{:S(2)}, u32[]{:S(2)}) async-start(f32[16,152,128]{2,1,0:T(8,128)} %shard_map.160), calls=%async_computation | async-start | bytes 2490368 | tf_op jit(solution)/shard_map/all_to_all | solution.py:728

commit v8 on v7

--- a/solution.py
+++ b/solution.py
@@ -8,6 +8,7 @@
 from jax.experimental import pallas as pl
 from jax.experimental.pallas import tpu as pltpu
 from jax.sharding import PartitionSpec as P
+
 
 time_step = 0.01
 gravity = 1.0
@@ -79,7 +80,7 @@
     return (value + step - 1) // step * step
 
 
-def static_tables(members, elements):
+def static_tables(members):
     deriv_r, deriv_s, lifting, face_order = node_tables()
     nodes = deriv_r.shape[0]
     pairs = nodes // 2
@@ -646,9 +647,9 @@
 def body(
     water_depth, momentum, metric, face_scale, face_angle, face_map, rim_faces, wet_blocks, breach, block_plan
 ):
-    blocks, members, node_cells = water_depth.shape
+    blocks, members, _ = water_depth.shape
     elements = metric.shape[2]
-    t = static_tables(members, elements)
+    t = static_tables(members)
     comp, pairs, used = t["comp"], t["pairs"], t["used"]
     f32, bf16 = jnp.float32, jnp.bfloat16
     tiles = blocks // 8
@@ -681,8 +682,8 @@
     count = lax.axis_size("mesh")
     partners = [(i, i ^ 1) for i in range(count)]
     neighbours = [(i, i + 1 if i % 2 else i - 1) for i in range(1, count - 1)]
+    across = lax.ppermute(to_across, "mesh", neighbours)
     partner = lax.ppermute(to_partner, "mesh", partners)
-    across = lax.ppermute(to_across, "mesh", neighbours)
 
     lift_h, lift_l = high_low(t["lift"])
     along_r, along_s = t["along"]

time: 60 us -> 60 us (level)
  no operation moved by 1% of the time
where the time goes in v8:
time: 60 us; the launch traced here: 59.6 us
  Pallas kernels  31.7 us (53%)
  waiting for transfers between devices  18.5 us (31%)
  starting transfers between devices  8.82 us (15%)
  between operations  0.67 us (1%)
    pallas_call x2, Pallas kernels, finish(): call(functools.partial(finish_kernel, t=t, blocks=blocks, elements=elemen...  22.1 us
    all_to_all x1, waiting for transfers between devices, body(): got = lax.all_to_all(sent, 'mesh', split_axis=0, concat_axis=0, tiled=True)  15.1 us
    pallas_call x1, Pallas kernels, body(): call(functools.partial(prepare_kernel, t=t, blocks=blocks, elements=eleme...  6.99 us
    all_to_all x1, starting transfers between devices, body(): got = lax.all_to_all(sent, 'mesh', split_axis=0, concat_axis=0, tiled=True)  5.03 us
    ppermute x1, waiting for transfers between devices, body(): across = lax.ppermute(to_across, 'mesh', neighbours)  3.37 us
    ppermute x1, starting transfers between devices, body(): across = lax.ppermute(to_across, 'mesh', neighbours)  3.05 us
    pallas_call x1, Pallas kernels, body(): call(functools.partial(merge_kernel, t=t, blocks=blocks), (jax.ShapeDtype...  2.59 us
  transfers between devices with their start and end apart: 3, of which 2 were waited for; matrix products, arithmetic and copies ran while one was open for 0% of the time, Pallas kernels for 24%

profile of v8, /device:TPU:15, one launch (start us, length us, event | category | flops | bytes accessed | tf_op | source)
XLA Modules:
  0.0 59.6 jit_solution(16115788205516478980)
XLA Ops:
  0.6 7.0 %shard_map.158 = (f32[24,168,128]{2,1,0:T(8,128)}, f32[4608,128]{1,0:T(8,128)}, f32[64,128]{1,0:T(8,128)}, f32[64,128]{1,0:T(8,128)}) custom-call(s32[1,128]{1,0:T(1,128)} %rim_in.1, f32[1200,128]{1,0:T(8,128)} %bitcast.16, f32[24,10,2,640]{3,2,1,0:T(2,128)} %bitcast.13, bf16[256,128]{1,0:T(8,128)(2,1)} %constant.10.clone.back_in, ...), custom_call_target="tpu_custom_call" | custom-call | tf_op jit(solution)/shard_map/pallas_call | solution.py:664
  7.6 0.7 %collective-permute-start = (f32[64,128]{1,0:T(8,128)}, f32[64,128]{1,0:T(8,128)}, u32[]{:S(2)}, u32[]{:S(2)}) collective-permute-start(f32[64,128]{1,0:T(8,128)} %get-tuple-element.13), channel_id=1, source_target_pairs={{0,1},{1,0},{2,3},{3,2},{4,5},{5,4},{6,7},{7,6},{8,9},{9,8},{10,11... | collective-permute-start | bytes 98312 | tf_op jit(solution)/shard_map/ppermute | solution.py:686
  8.4 3.1 %collective-permute-start.1 = (f32[64,128]{1,0:T(8,128)}, f32[64,128]{1,0:T(8,128)}, u32[]{:S(2)}, u32[]{:S(2)}) collective-permute-start(f32[64,128]{1,0:T(8,128)} %get-tuple-element.14), channel_id=1, source_target_pairs={{1,2},{2,1},{3,4},{4,3},{5,6},{6,5},{7,8},{8,7},{9,10},{10,9},{11,... | collective-permute-start | bytes 98312 | tf_op jit(solution)/shard_map/ppermute | solution.py:685
  11.4 0.0 collective-permute-done.partner_in
  11.4 3.4 %collective-permute-done.1.across_in = f32[64,128]{1,0:T(8,128)} collective-permute-done((f32[64,128]{1,0:T(8,128)}, f32[64,128]{1,0:T(8,128)}, u32[]{:S(2)}, u32[]{:S(2)}) %collective-permute-start.1) | collective-permute-done | bytes 32800 | tf_op jit(solution)/shard_map/ppermute | solution.py:685
  14.8 7.9 %shard_map.160 = f32[16,152,128]{2,1,0:T(8,128)} custom-call(s32[384]{0:T(512)} %plan_in.3, s32[24]{0:T(128)} %wet_in.3, s32[10,24]{1,0:T(8,128)} %bitcast.17, s32[24,192]{1,0:T(8,128)} %links_in.3, f32[24,192]{1,0:T(8,128)} %angle_in.3, f32[24,192]{1,0:T(8,128)} %scale_in.3, f32[24,4,64]{2,1,0:T(4,128)} %metric_in.3, ...), custom_call_target="tpu_custom_call" | custom-call | tf_op jit(solution)/shard_map/pallas_call | solution.py:704
  22.7 5.0 %all-to-all-start = ((f32[16,152,128]{2,1,0:T(8,128)}), f32[16,152,128]{2,1,0:T(8,128)}, u32[]{:S(2)}, u32[]{:S(2)}) async-start(f32[16,152,128]{2,1,0:T(8,128)} %shard_map.160), calls=%async_computation | async-start | bytes 2490368 | tf_op jit(solution)/shard_map/all_to_all | solution.py:729
  27.8 14.2 %shard_map.159 = (f32[1200,128]{1,0:T(8,128)}, f32[24,10,2,640]{3,2,1,0:T(2,128)}, s32[128]{0:T(128)}) custom-call(s32[384]{0:T(512)} %plan_in.3, s32[24]{0:T(128)} %wet_in.3, s32[10,24]{1,0:T(8,128)} %bitcast.18, s32[24,192]{1,0:T(8,128)} %links_in.3, f32[24,192]{1,0:T(8,128)} %angle_in.3, f32[24,192]{1,0:T(8,128)} %scale_in.3, f32[24,4,64]{2,1,0:T(4,128)} %metric_in.3, ...), custom_call_target="tpu_custom_call" | custom-call | tf_op jit(solution)/shard_map/pallas_call | solution.py:704
  41.9 15.1 %all-to-all-done.got_in = f32[16,152,128]{2,1,0:T(8,128)} async-done(((f32[16,152,128]{2,1,0:T(8,128)}), f32[16,152,128]{2,1,0:T(8,128)}, u32[]{:S(2)}, u32[]{:S(2)}) %all-to-all-start) | async-done | bytes 1245216 | tf_op jit(solution)/shard_map/all_to_all | solution.py:729
  57.0 2.6 %shard_map.161 = (f32[10,3,5,8,128]{4,3,2,1,0:T(8,128)}, f32[24,10,2,640]{3,2,1,0:T(2,128)}) custom-call(s32[128]{0:T(128)} %get-tuple-element.15.origin_in, f32[16,152,128]{2,1,0:T(8,128)} %all-to-all-done.got_in, f32[10,3,5,8,128]{4,3,2,1,0:T(8,128)} %bitcast.14, ...), custom_call_target="tpu_custom_call", output_to_operand_aliasing={{0}: (2, {}), {1}: (3, {})} | custom-call | tf_op jit(solution)/shard_map/pallas_call | solution.py:737
Async XLA Ops:
  7.6 3.8 %collective-permute-start = (f32[64,128]{1,0:T(8,128)}, f32[64,128]{1,0:T(8,128)}, u32[]{:S(2)}, u32[]{:S(2)}) collective-permute-start(f32[64,128]{1,0:T(8,128)} %get-tuple-element.13), channel_id=1, source_target_pairs={{0,1},{1,0},{2,3},{3,2},{4,5},{5,4},{6,7},{7,6},{8,9},{9,8},{10,11... | collective-permute-start | bytes 98312 | tf_op jit(solution)/shard_map/ppermute | solution.py:686
  8.4 6.4 %collective-permute-start.1 = (f32[64,128]{1,0:T(8,128)}, f32[64,128]{1,0:T(8,128)}, u32[]{:S(2)}, u32[]{:S(2)}) collective-permute-start(f32[64,128]{1,0:T(8,128)} %get-tuple-element.14), channel_id=1, source_target_pairs={{1,2},{2,1},{3,4},{4,3},{5,6},{6,5},{7,8},{8,7},{9,10},{10,9},{11,... | collective-permute-start | bytes 98312 | tf_op jit(solution)/shard_map/ppermute | solution.py:685
  22.7 34.3 %all-to-all-start = ((f32[16,152,128]{2,1,0:T(8,128)}), f32[16,152,128]{2,1,0:T(8,128)}, u32[]{:S(2)}, u32[]{:S(2)}) async-start(f32[16,152,128]{2,1,0:T(8,128)} %shard_map.160), calls=%async_computation | async-start | bytes 2490368 | tf_op jit(solution)/shard_map/all_to_all | solution.py:729

commit v9 on v8

--- a/solution.py
+++ b/solution.py
@@ -471,7 +471,7 @@
         for f in range(3):
             for line in range(rows.start, rows.stop):
                 v = near[2 * w + line // elements, f * elements + line % elements]
-                outer[w, f * LANES + line : f * LANES + line + 1, :] = pool[pl.ds(v, 1), :]
+                outer[w % 2, f * LANES + line : f * LANES + line + 1, :] = pool[pl.ds(v, 1), :]
 
     def pair_of(i, w):
         return [order[at(i, 2 * w + u)] for u in range(2)]
@@ -480,23 +480,24 @@
         for c in range(3):
             turn_rows(
                 rows_of(fields, pair[0], c, comp), rows_of(fields, pair[1], c, comp), c, eye,
-                turned.at[w], halves.at[w], comp,
+                turned.at[w % 2], halves.at[w % 2], comp,
             )
-        inner = mm(halves[w], own[...])
+        inner = mm(halves[w % 2], own[...])
         for c in range(3):
-            traces[w, c] = inner[c * LANES : (c + 1) * LANES]
-        spread_pair(coefs, pair, eye, spread, factors.at[w], elements)
+            traces[w % 2, c] = inner[c * LANES : (c + 1) * LANES]
+        spread_pair(coefs, pair, eye, spread, factors.at[w % 2], elements)
 
     def one(i, carry):
-        both = [pair_of(i, w) for w in range(2)]
+        both = [pair_of(i, w) for w in range(n_pairs)]
         inflow = [inflow_rows(breach, pair, t) for pair in both]
 
         def fluxes(w, rows):
-            volume_rows(rows, turned.at[w], factors.at[w], 4, inflow[w][rows.start // elements], pieces.at[w])
-            flux_rows(rows, traces.at[w], outer.at[w], factors.at[w], pieces.at[w], 4 * LANES, wide)
+            q = w % 2
+            volume_rows(rows, turned.at[q], factors.at[q], 4, inflow[w][rows.start // elements], pieces.at[q])
+            flux_rows(rows, traces.at[q], outer.at[q], factors.at[q], pieces.at[q], 4 * LANES, wide)
 
         def combine(w, c):
-            gains = pair_gains(mm(matrix[...], pieces[w, c], ((1,), (1,))), comp, elements)
+            gains = pair_gains(mm(matrix[...], pieces[w % 2, c], ((1,), (1,))), comp, elements)
             for u in range(2):
                 b = both[w][u]
                 rate = time_step * wet[b].astype(jnp.float32)
@@ -510,7 +511,7 @@
         def hand_over(w):
             for u in range(2):
                 if leaving:
-                    p = 4 * i + 2 * w + u
+                    p = 2 * n_pairs * i + 2 * w + u
 
                     @pl.when(p < end)
                     def _():
@@ -526,24 +527,25 @@
         wait_all(indices(i))
         for rows in chunks:
             pick(0, rows)
-        lay_out(1, both[1])
-        for rows in chunks:
-            fluxes(0, rows)
-            pick(1, rows)
-        for k, rows in enumerate(chunks):
-            if k < 3:
-                combine(0, k)
-            fluxes(1, rows)
+        for w in range(n_pairs):
+            if w + 1 < n_pairs:
+                lay_out(w + 1, both[w + 1])
+            for k, rows in enumerate(chunks):
+                if w > 0 and k < 3:
+                    combine(w - 1, k)
+                fluxes(w, rows)
+                if w + 1 < n_pairs:
+                    pick(w + 1, rows)
         for c in range(3):
-            combine(1, c)
+            combine(n_pairs - 1, c)
 
         @pl.when(i + 1 < steps)
         def _():
             start_all(indices(i + 1))
             lay_out(0, pair_of(i + 1, 0))
 
-        hand_over(0)
-        hand_over(1)
+        for w in range(n_pairs):
+            hand_over(w)
         return carry
 
     lay_out(0, pair_of(0, 0))
@@ -698,9 +700,8 @@
 
     i32 = jnp.int32
     block_rows = (3 * comp, LANES)
-    n_pairs = 2
-
-    def finish(leaving, out_shape, extra):
+
+    def finish(leaving, n_pairs, out_shape, extra):
         return call(
             functools.partial(
                 finish_kernel, t=t, blocks=blocks, elements=elements, devices=count, leaving=leaving
@@ -725,13 +726,13 @@
             *mats,
         )
 
-    sent = finish(True, jax.ShapeDtypeStruct((count, packed, LANES), f32), [pltpu.VMEM((blocks, *block_rows), f32)])
+    sent = finish(True, 4, jax.ShapeDtypeStruct((count, packed, LANES), f32), [pltpu.VMEM((blocks, *block_rows), f32)])
     got = lax.all_to_all(sent, "mesh", split_axis=0, concat_axis=0, tiled=True)
     final = (jax.ShapeDtypeStruct(depth_rows.shape, f32), jax.ShapeDtypeStruct(flow_rows.shape, f32))
     whole = [pltpu.VMEM(depth_rows.shape, f32), pltpu.VMEM(flow_rows.shape, f32)]
     depth_kept, flow_kept, origin = finish(
-        False, (*final, jax.ShapeDtypeStruct((LANES,), i32)),
-        [pltpu.VMEM((2 * n_pairs, *block_rows), f32), *whole, pltpu.SMEM((LANES,), i32)],
+        False, 2, (*final, jax.ShapeDtypeStruct((LANES,), i32)),
+        [pltpu.VMEM((4, *block_rows), f32), *whole, pltpu.SMEM((LANES,), i32)],
     )
     tall = (members, tiles, pairs, 8, LANES)
     depth_new, flow_new = call(

time: 60 us -> 59.2 us (0.987)
  Pallas kernels: 31.7 us -> 30.9 us
    pallas_call x2, Pallas kernels: 22.1 us -> 21.3 us  [finish(): call(functools.partial(finish_kernel, t=t, blocks=blocks, elements=elemen...]
where the time goes in v9:
time: 59.2 us; the launch traced here: 58.9 us
  Pallas kernels  30.9 us (52%)
  waiting for transfers between devices  18.5 us (31%)
  starting transfers between devices  8.83 us (15%)
  between operations  0.67 us (1%)
    pallas_call x2, Pallas kernels, finish(): call(functools.partial(finish_kernel, t=t, blocks=blocks, elements=elemen...  21.3 us
    all_to_all x1, waiting for transfers between devices, body(): got = lax.all_to_all(sent, 'mesh', split_axis=0, concat_axis=0, tiled=True)  15.1 us
    pallas_call x1, Pallas kernels, body(): call(functools.partial(prepare_kernel, t=t, blocks=blocks, elements=eleme...  6.99 us
    all_to_all x1, starting transfers between devices, body(): got = lax.all_to_all(sent, 'mesh', split_axis=0, concat_axis=0, tiled=True)  5.04 us
    ppermute x1, waiting for transfers between devices, body(): across = lax.ppermute(to_across, 'mesh', neighbours)  3.37 us
    ppermute x1, starting transfers between devices, body(): across = lax.ppermute(to_across, 'mesh', neighbours)  3.05 us
    pallas_call x1, Pallas kernels, body(): call(functools.partial(merge_kernel, t=t, blocks=blocks), (jax.ShapeDtype...  2.59 us
  transfers between devices with their start and end apart: 3, of which 2 were waited for; matrix products, arithmetic and copies ran while one was open for 0% of the time, Pallas kernels for 24%

profile of v9, /device:TPU:15, one launch (start us, length us, event | category | flops | bytes accessed | tf_op | source)
XLA Modules:
  0.0 58.9 jit_solution(12812000654832501285)
XLA Ops:
  0.6 7.0 %shard_map.158 = (f32[24,168,128]{2,1,0:T(8,128)}, f32[4608,128]{1,0:T(8,128)}, f32[64,128]{1,0:T(8,128)}, f32[64,128]{1,0:T(8,128)}) custom-call(s32[1,128]{1,0:T(1,128)} %rim_in.1, f32[1200,128]{1,0:T(8,128)} %bitcast.16, f32[24,10,2,640]{3,2,1,0:T(2,128)} %bitcast.13, bf16[256,128]{1,0:T(8,128)(2,1)} %constant.10.clone.back_in, ...), custom_call_target="tpu_custom_call" | custom-call | tf_op jit(solution)/shard_map/pallas_call | solution.py:666
  7.6 0.7 %collective-permute-start = (f32[64,128]{1,0:T(8,128)}, f32[64,128]{1,0:T(8,128)}, u32[]{:S(2)}, u32[]{:S(2)}) collective-permute-start(f32[64,128]{1,0:T(8,128)} %get-tuple-element.13), channel_id=1, source_target_pairs={{0,1},{1,0},{2,3},{3,2},{4,5},{5,4},{6,7},{7,6},{8,9},{9,8},{10,11... | collective-permute-start | bytes 98312 | tf_op jit(solution)/shard_map/ppermute | solution.py:688
  8.4 3.1 %collective-permute-start.1 = (f32[64,128]{1,0:T(8,128)}, f32[64,128]{1,0:T(8,128)}, u32[]{:S(2)}, u32[]{:S(2)}) collective-permute-start(f32[64,128]{1,0:T(8,128)} %get-tuple-element.14), channel_id=1, source_target_pairs={{1,2},{2,1},{3,4},{4,3},{5,6},{6,5},{7,8},{8,7},{9,10},{10,9},{11,... | collective-permute-start | bytes 98312 | tf_op jit(solution)/shard_map/ppermute | solution.py:687
  11.4 0.0 collective-permute-done.partner_in
  11.4 3.4 %collective-permute-done.1.across_in = f32[64,128]{1,0:T(8,128)} collective-permute-done((f32[64,128]{1,0:T(8,128)}, f32[64,128]{1,0:T(8,128)}, u32[]{:S(2)}, u32[]{:S(2)}) %collective-permute-start.1) | collective-permute-done | bytes 32800 | tf_op jit(solution)/shard_map/ppermute | solution.py:687
  14.8 7.2 %shard_map.160 = f32[16,152,128]{2,1,0:T(8,128)} custom-call(s32[384]{0:T(512)} %plan_in.3, s32[24]{0:T(128)} %wet_in.3, s32[10,24]{1,0:T(8,128)} %bitcast.17, s32[24,192]{1,0:T(8,128)} %links_in.3, f32[24,192]{1,0:T(8,128)} %angle_in.3, f32[24,192]{1,0:T(8,128)} %scale_in.3, f32[24,4,64]{2,1,0:T(4,128)} %metric_in.3, ...), custom_call_target="tpu_custom_call" | custom-call | tf_op jit(solution)/shard_map/pallas_call | solution.py:705
  22.0 5.0 %all-to-all-start = ((f32[16,152,128]{2,1,0:T(8,128)}), f32[16,152,128]{2,1,0:T(8,128)}, u32[]{:S(2)}, u32[]{:S(2)}) async-start(f32[16,152,128]{2,1,0:T(8,128)} %shard_map.160), calls=%async_computation | async-start | bytes 2490368 | tf_op jit(solution)/shard_map/all_to_all | solution.py:730
  27.0 14.2 %shard_map.159 = (f32[1200,128]{1,0:T(8,128)}, f32[24,10,2,640]{3,2,1,0:T(2,128)}, s32[128]{0:T(128)}) custom-call(s32[384]{0:T(512)} %plan_in.3, s32[24]{0:T(128)} %wet_in.3, s32[10,24]{1,0:T(8,128)} %bitcast.18, s32[24,192]{1,0:T(8,128)} %links_in.3, f32[24,192]{1,0:T(8,128)} %angle_in.3, f32[24,192]{1,0:T(8,128)} %scale_in.3, f32[24,4,64]{2,1,0:T(4,128)} %metric_in.3, ...), custom_call_target="tpu_custom_call" | custom-call | tf_op jit(solution)/shard_map/pallas_call | solution.py:705
  41.2 15.1 %all-to-all-done.got_in = f32[16,152,128]{2,1,0:T(8,128)} async-done(((f32[16,152,128]{2,1,0:T(8,128)}), f32[16,152,128]{2,1,0:T(8,128)}, u32[]{:S(2)}, u32[]{:S(2)}) %all-to-all-start) | async-done | bytes 1245216 | tf_op jit(solution)/shard_map/all_to_all | solution.py:730
  56.3 2.6 %shard_map.161 = (f32[10,3,5,8,128]{4,3,2,1,0:T(8,128)}, f32[24,10,2,640]{3,2,1,0:T(2,128)}) custom-call(s32[128]{0:T(128)} %get-tuple-element.15.origin_in, f32[16,152,128]{2,1,0:T(8,128)} %all-to-all-done.got_in, f32[10,3,5,8,128]{4,3,2,1,0:T(8,128)} %bitcast.14, ...), custom_call_target="tpu_custom_call", output_to_operand_aliasing={{0}: (2, {}), {1}: (3, {})} | custom-call | tf_op jit(solution)/shard_map/pallas_call | solution.py:738
Async XLA Ops:
  7.6 3.8 %collective-permute-start = (f32[64,128]{1,0:T(8,128)}, f32[64,128]{1,0:T(8,128)}, u32[]{:S(2)}, u32[]{:S(2)}) collective-permute-start(f32[64,128]{1,0:T(8,128)} %get-tuple-element.13), channel_id=1, source_target_pairs={{0,1},{1,0},{2,3},{3,2},{4,5},{5,4},{6,7},{7,6},{8,9},{9,8},{10,11... | collective-permute-start | bytes 98312 | tf_op jit(solution)/shard_map/ppermute | solution.py:688
  8.4 6.4 %collective-permute-start.1 = (f32[64,128]{1,0:T(8,128)}, f32[64,128]{1,0:T(8,128)}, u32[]{:S(2)}, u32[]{:S(2)}) collective-permute-start(f32[64,128]{1,0:T(8,128)} %get-tuple-element.14), channel_id=1, source_target_pairs={{1,2},{2,1},{3,4},{4,3},{5,6},{6,5},{7,8},{8,7},{9,10},{10,9},{11,... | collective-permute-start | bytes 98312 | tf_op jit(solution)/shard_map/ppermute | solution.py:687
  22.0 34.3 %all-to-all-start = ((f32[16,152,128]{2,1,0:T(8,128)}), f32[16,152,128]{2,1,0:T(8,128)}, u32[]{:S(2)}, u32[]{:S(2)}) async-start(f32[16,152,128]{2,1,0:T(8,128)} %shard_map.160), calls=%async_computation | async-start | bytes 2490368 | tf_op jit(solution)/shard_map/all_to_all | solution.py:730

commit v10 on v9

--- a/solution.py
+++ b/solution.py
@@ -228,14 +228,15 @@
                     row = comp + 2 * (s * pairs + j)
                     fields[b, row : row + 2] = flow[b, s, :, j * LANES : (j + 1) * LANES]
 
-    def turn_of(i):
+    def turn_of(i, slot):
         for c in range(3):
             turn_rows(
-                rows_of(fields, 2 * i, c, comp), rows_of(fields, 2 * i + 1, c, comp), c, eye, None, halves, comp
+                rows_of(fields, 2 * i, c, comp), rows_of(fields, 2 * i + 1, c, comp), c, eye, None,
+                halves.at[slot], comp,
             )
 
-    def faces_of(i):
-        rows = mm(halves[...], back[...])
+    def faces_of(i, slot):
+        rows = mm(halves[slot], back[...])
         lane = lax.broadcasted_iota(jnp.int32, (LANES, LANES), 1)
         pieces = [rows[c * LANES : (c + 1) * LANES] for c in range(3)]
         for f in range(3):
@@ -246,31 +247,45 @@
 
     part(0).wait()
     build(0)
-    turn_of(0)
     build(1)
-
-    def one(i, carry):
-        @pl.when(i % 4 == 0)
+    turn_of(0, 0)
+    turn_of(1, 1)
+    build(2)
+    build(3)
+    field_part(0).start()
+
+    def one(h, carry):
+        i = 2 * h
+
+        @pl.when(h % 2 == 0)
         def _():
-            part(i // 4).wait()
-
-        faces_of(i - 2)
-        turn_of(i - 1)
-        build(i)
-        pool_part(i - 2).start()
-
-        @pl.when(i % 4 == 3)
+            part(h // 2).wait()
+
+        for slot in range(2):
+            faces_of(i - 4 + slot, slot)
+        for slot in range(2):
+            turn_of(i - 2 + slot, slot)
+        for slot in range(2):
+            build(i + slot)
+        for slot in range(2):
+            pool_part(i - 4 + slot).start()
+
+        @pl.when(h % 2 == 1)
         def _():
-            field_part(i // 4).start()
+            field_part(h // 2).start()
 
         return carry
 
-    lax.fori_loop(2, steps, one, 0)
-    faces_of(steps - 2)
-    turn_of(steps - 1)
-    pool_part(steps - 2).start()
-    faces_of(steps - 1)
-    pool_part(steps - 1).start()
+    lax.fori_loop(2, steps // 2, one, 0)
+    for slot in range(2):
+        faces_of(steps - 4 + slot, slot)
+    for slot in range(2):
+        turn_of(steps - 2 + slot, slot)
+    for slot in range(2):
+        pool_part(steps - 4 + slot).start()
+    for slot in range(2):
+        faces_of(steps - 2 + slot, slot)
+        pool_part(steps - 2 + slot).start()
     width = partner.shape[0]
     near, far = (1 - odd) * width, odd * width
 
@@ -676,7 +691,7 @@
             pltpu.SMEM(rim_faces.shape, jnp.int32), pltpu.VMEM(depth_rows.shape, f32), pltpu.VMEM(flow_rows.shape, f32), pltpu.VMEM(back.shape, bf16),
             pltpu.VMEM(eye.shape, bf16),
             pltpu.VMEM((blocks, 3 * comp, LANES), f32), pltpu.VMEM((faces, LANES), f32),
-            pltpu.VMEM((3 * LANES, 2 * LANES), bf16), dma((4 + 2 * tiles + blocks // 2,)),
+            pltpu.VMEM((2, 3 * LANES, 2 * LANES), bf16), dma((4 + 2 * tiles + blocks // 2,)),
         ],
         (HBM, HBM, VMEM, VMEM),
     )(rim_faces, depth_rows, flow_rows, back, eye)

time: 59.2 us -> 58 us (0.980)
  Pallas kernels: 30.9 us -> 29.7 us
    pallas_call x1, Pallas kernels: 6.99 us -> 5.78 us  [body(): call(functools.partial(prepare_kernel, t=t, blocks=blocks, elements=eleme...]
  transfers between devices with their start and end apart: 3 -> 3, of which waited for: 2 -> 2; matrix products, arithmetic and copies ran while one was open for 0% -> 0% of each run, Pallas kernels for 24% -> 25%
where the time goes in v10:
time: 58 us; the launch traced here: 57.7 us
  Pallas kernels  29.7 us (51%)
  waiting for transfers between devices  18.5 us (32%)
  starting transfers between devices  8.83 us (15%)
  between operations  0.67 us (1%)
    pallas_call x2, Pallas kernels, finish(): call(functools.partial(finish_kernel, t=t, blocks=blocks, elements=elemen...  21.3 us
    all_to_all x1, waiting for transfers between devices, body(): got = lax.all_to_all(sent, 'mesh', split_axis=0, concat_axis=0, tiled=True)  15.1 us
    pallas_call x1, Pallas kernels, body(): call(functools.partial(prepare_kernel, t=t, blocks=blocks, elements=eleme...  5.78 us
    all_to_all x1, starting transfers between devices, body(): got = lax.all_to_all(sent, 'mesh', split_axis=0, concat_axis=0, tiled=True)  5.04 us
    ppermute x1, waiting for transfers between devices, body(): across = lax.ppermute(to_across, 'mesh', neighbours)  3.36 us
    ppermute x1, starting transfers between devices, body(): across = lax.ppermute(to_across, 'mesh', neighbours)  3.06 us
    pallas_call x1, Pallas kernels, body(): call(functools.partial(merge_kernel, t=t, blocks=blocks), (jax.ShapeDtype...  2.59 us
  transfers between devices with their start and end apart: 3, of which 2 were waited for; matrix products, arithmetic and copies ran while one was open for 0% of the time, Pallas kernels for 25%

profile of v10, /device:TPU:15, one launch (start us, length us, event | category | flops | bytes accessed | tf_op | source)
XLA Modules:
  0.0 57.7 jit_solution(12930301720164460521)
XLA Ops:
  0.6 5.8 %shard_map.158 = (f32[24,168,128]{2,1,0:T(8,128)}, f32[4608,128]{1,0:T(8,128)}, f32[64,128]{1,0:T(8,128)}, f32[64,128]{1,0:T(8,128)}) custom-call(s32[1,128]{1,0:T(1,128)} %rim_in.1, f32[1200,128]{1,0:T(8,128)} %bitcast.16, f32[24,10,2,640]{3,2,1,0:T(2,128)} %bitcast.13, bf16[256,128]{1,0:T(8,128)(2,1)} %constant.10.clone.back_in, ...), custom_call_target="tpu_custom_call" | custom-call | tf_op jit(solution)/shard_map/pallas_call | solution.py:681
  6.4 0.7 %collective-permute-start = (f32[64,128]{1,0:T(8,128)}, f32[64,128]{1,0:T(8,128)}, u32[]{:S(2)}, u32[]{:S(2)}) collective-permute-start(f32[64,128]{1,0:T(8,128)} %get-tuple-element.13), channel_id=1, source_target_pairs={{0,1},{1,0},{2,3},{3,2},{4,5},{5,4},{6,7},{7,6},{8,9},{9,8},{10,11... | collective-permute-start | bytes 98312 | tf_op jit(solution)/shard_map/ppermute | solution.py:703
  7.1 3.1 %collective-permute-start.1 = (f32[64,128]{1,0:T(8,128)}, f32[64,128]{1,0:T(8,128)}, u32[]{:S(2)}, u32[]{:S(2)}) collective-permute-start(f32[64,128]{1,0:T(8,128)} %get-tuple-element.14), channel_id=1, source_target_pairs={{1,2},{2,1},{3,4},{4,3},{5,6},{6,5},{7,8},{8,7},{9,10},{10,9},{11,... | collective-permute-start | bytes 98312 | tf_op jit(solution)/shard_map/ppermute | solution.py:702
  10.2 0.0 collective-permute-done.partner_in
  10.2 3.4 %collective-permute-done.1.across_in = f32[64,128]{1,0:T(8,128)} collective-permute-done((f32[64,128]{1,0:T(8,128)}, f32[64,128]{1,0:T(8,128)}, u32[]{:S(2)}, u32[]{:S(2)}) %collective-permute-start.1) | collective-permute-done | bytes 32800 | tf_op jit(solution)/shard_map/ppermute | solution.py:702
  13.6 7.2 %shard_map.160 = f32[16,152,128]{2,1,0:T(8,128)} custom-call(s32[384]{0:T(512)} %plan_in.3, s32[24]{0:T(128)} %wet_in.3, s32[10,24]{1,0:T(8,128)} %bitcast.17, s32[24,192]{1,0:T(8,128)} %links_in.3, f32[24,192]{1,0:T(8,128)} %angle_in.3, f32[24,192]{1,0:T(8,128)} %scale_in.3, f32[24,4,64]{2,1,0:T(4,128)} %metric_in.3, ...), custom_call_target="tpu_custom_call" | custom-call | tf_op jit(solution)/shard_map/pallas_call | solution.py:720
  20.7 5.0 %all-to-all-start = ((f32[16,152,128]{2,1,0:T(8,128)}), f32[16,152,128]{2,1,0:T(8,128)}, u32[]{:S(2)}, u32[]{:S(2)}) async-start(f32[16,152,128]{2,1,0:T(8,128)} %shard_map.160), calls=%async_computation | async-start | bytes 2490368 | tf_op jit(solution)/shard_map/all_to_all | solution.py:745
  25.8 14.2 %shard_map.159 = (f32[1200,128]{1,0:T(8,128)}, f32[24,10,2,640]{3,2,1,0:T(2,128)}, s32[128]{0:T(128)}) custom-call(s32[384]{0:T(512)} %plan_in.3, s32[24]{0:T(128)} %wet_in.3, s32[10,24]{1,0:T(8,128)} %bitcast.18, s32[24,192]{1,0:T(8,128)} %links_in.3, f32[24,192]{1,0:T(8,128)} %angle_in.3, f32[24,192]{1,0:T(8,128)} %scale_in.3, f32[24,4,64]{2,1,0:T(4,128)} %metric_in.3, ...), custom_call_target="tpu_custom_call" | custom-call | tf_op jit(solution)/shard_map/pallas_call | solution.py:720
  40.0 15.1 %all-to-all-done.got_in = f32[16,152,128]{2,1,0:T(8,128)} async-done(((f32[16,152,128]{2,1,0:T(8,128)}), f32[16,152,128]{2,1,0:T(8,128)}, u32[]{:S(2)}, u32[]{:S(2)}) %all-to-all-start) | async-done | bytes 1245216 | tf_op jit(solution)/shard_map/all_to_all | solution.py:745
  55.1 2.6 %shard_map.161 = (f32[10,3,5,8,128]{4,3,2,1,0:T(8,128)}, f32[24,10,2,640]{3,2,1,0:T(2,128)}) custom-call(s32[128]{0:T(128)} %get-tuple-element.15.origin_in, f32[16,152,128]{2,1,0:T(8,128)} %all-to-all-done.got_in, f32[10,3,5,8,128]{4,3,2,1,0:T(8,128)} %bitcast.14, ...), custom_call_target="tpu_custom_call", output_to_operand_aliasing={{0}: (2, {}), {1}: (3, {})} | custom-call | tf_op jit(solution)/shard_map/pallas_call | solution.py:753
Async XLA Ops:
  6.4 3.8 %collective-permute-start = (f32[64,128]{1,0:T(8,128)}, f32[64,128]{1,0:T(8,128)}, u32[]{:S(2)}, u32[]{:S(2)}) collective-permute-start(f32[64,128]{1,0:T(8,128)} %get-tuple-element.13), channel_id=1, source_target_pairs={{0,1},{1,0},{2,3},{3,2},{4,5},{5,4},{6,7},{7,6},{8,9},{9,8},{10,11... | collective-permute-start | bytes 98312 | tf_op jit(solution)/shard_map/ppermute | solution.py:703
  7.1 6.4 %collective-permute-start.1 = (f32[64,128]{1,0:T(8,128)}, f32[64,128]{1,0:T(8,128)}, u32[]{:S(2)}, u32[]{:S(2)}) collective-permute-start(f32[64,128]{1,0:T(8,128)} %get-tuple-element.14), channel_id=1, source_target_pairs={{1,2},{2,1},{3,4},{4,3},{5,6},{6,5},{7,8},{8,7},{9,10},{10,9},{11,... | collective-permute-start | bytes 98312 | tf_op jit(solution)/shard_map/ppermute | solution.py:702
  20.7 34.3 %all-to-all-start = ((f32[16,152,128]{2,1,0:T(8,128)}), f32[16,152,128]{2,1,0:T(8,128)}, u32[]{:S(2)}, u32[]{:S(2)}) async-start(f32[16,152,128]{2,1,0:T(8,128)} %shard_map.160), calls=%async_computation | async-start | bytes 2490368 | tf_op jit(solution)/shard_map/all_to_all | solution.py:745

commit v11 on v10

--- a/solution.py
+++ b/solution.py
@@ -502,6 +502,8 @@
             traces[w % 2, c] = inner[c * LANES : (c + 1) * LANES]
         spread_pair(coefs, pair, eye, spread, factors.at[w % 2], elements)
 
+    early = n_pairs // 2 if leaving else 0
+
     def one(i, carry):
         both = [pair_of(i, w) for w in range(n_pairs)]
         inflow = [inflow_rows(breach, pair, t) for pair in both]
@@ -551,6 +553,9 @@
                 fluxes(w, rows)
                 if w + 1 < n_pairs:
                     pick(w + 1, rows)
+            if w == early:
+                for v in range(early):
+                    hand_over(v)
         for c in range(3):
             combine(n_pairs - 1, c)
 
@@ -559,7 +564,7 @@
             start_all(indices(i + 1))
             lay_out(0, pair_of(i + 1, 0))
 
-        for w in range(n_pairs):
+        for w in range(early, n_pairs):
             hand_over(w)
         return carry
 

time: 58 us -> 58.2 us (level)
  no operation moved by 1% of the time
where the time goes in v11:
time: 58.2 us; the launch traced here: 57.8 us
  Pallas kernels  29.9 us (51%)
  waiting for transfers between devices  18.5 us (32%)
  starting transfers between devices  8.82 us (15%)
  between operations  0.67 us (1%)
    pallas_call x2, Pallas kernels, finish(): call(functools.partial(finish_kernel, t=t, blocks=blocks, elements=elemen...  21.5 us
    all_to_all x1, waiting for transfers between devices, body(): got = lax.all_to_all(sent, 'mesh', split_axis=0, concat_axis=0, tiled=True)  15.1 us
    pallas_call x1, Pallas kernels, body(): call(functools.partial(prepare_kernel, t=t, blocks=blocks, elements=eleme...  5.78 us
    all_to_all x1, starting transfers between devices, body(): got = lax.all_to_all(sent, 'mesh', split_axis=0, concat_axis=0, tiled=True)  5.03 us
    ppermute x1, waiting for transfers between devices, body(): across = lax.ppermute(to_across, 'mesh', neighbours)  3.36 us
    ppermute x1, starting transfers between devices, body(): across = lax.ppermute(to_across, 'mesh', neighbours)  3.06 us
    pallas_call x1, Pallas kernels, body(): call(functools.partial(merge_kernel, t=t, blocks=blocks), (jax.ShapeDtype...  2.59 us
  transfers between devices with their start and end apart: 3, of which 2 were waited for; matrix products, arithmetic and copies ran while one was open for 0% of the time, Pallas kernels for 25%

profile of v11, /device:TPU:15, one launch (start us, length us, event | category | flops | bytes accessed | tf_op | source)
XLA Modules:
  0.0 57.8 jit_solution(515187518969277122)
XLA Ops:
  0.6 5.8 %shard_map.158 = (f32[24,168,128]{2,1,0:T(8,128)}, f32[4608,128]{1,0:T(8,128)}, f32[64,128]{1,0:T(8,128)}, f32[64,128]{1,0:T(8,128)}) custom-call(s32[1,128]{1,0:T(1,128)} %rim_in.1, f32[1200,128]{1,0:T(8,128)} %bitcast.16, f32[24,10,2,640]{3,2,1,0:T(2,128)} %bitcast.13, bf16[256,128]{1,0:T(8,128)(2,1)} %constant.10.clone.back_in, ...), custom_call_target="tpu_custom_call" | custom-call | tf_op jit(solution)/shard_map/pallas_call | solution.py:686
  6.4 0.7 %collective-permute-start = (f32[64,128]{1,0:T(8,128)}, f32[64,128]{1,0:T(8,128)}, u32[]{:S(2)}, u32[]{:S(2)}) collective-permute-start(f32[64,128]{1,0:T(8,128)} %get-tuple-element.13), channel_id=1, source_target_pairs={{0,1},{1,0},{2,3},{3,2},{4,5},{5,4},{6,7},{7,6},{8,9},{9,8},{10,11... | collective-permute-start | bytes 98312 | tf_op jit(solution)/shard_map/ppermute | solution.py:708
  7.1 3.1 %collective-permute-start.1 = (f32[64,128]{1,0:T(8,128)}, f32[64,128]{1,0:T(8,128)}, u32[]{:S(2)}, u32[]{:S(2)}) collective-permute-start(f32[64,128]{1,0:T(8,128)} %get-tuple-element.14), channel_id=1, source_target_pairs={{1,2},{2,1},{3,4},{4,3},{5,6},{6,5},{7,8},{8,7},{9,10},{10,9},{11,... | collective-permute-start | bytes 98312 | tf_op jit(solution)/shard_map/ppermute | solution.py:707
  10.2 0.0 collective-permute-done.partner_in
  10.2 3.4 %collective-permute-done.1.across_in = f32[64,128]{1,0:T(8,128)} collective-permute-done((f32[64,128]{1,0:T(8,128)}, f32[64,128]{1,0:T(8,128)}, u32[]{:S(2)}, u32[]{:S(2)}) %collective-permute-start.1) | collective-permute-done | bytes 32800 | tf_op jit(solution)/shard_map/ppermute | solution.py:707
  13.6 7.4 %shard_map.160 = f32[16,152,128]{2,1,0:T(8,128)} custom-call(s32[384]{0:T(512)} %plan_in.3, s32[24]{0:T(128)} %wet_in.3, s32[10,24]{1,0:T(8,128)} %bitcast.17, s32[24,192]{1,0:T(8,128)} %links_in.3, f32[24,192]{1,0:T(8,128)} %angle_in.3, f32[24,192]{1,0:T(8,128)} %scale_in.3, f32[24,4,64]{2,1,0:T(4,128)} %metric_in.3, ...), custom_call_target="tpu_custom_call" | custom-call | tf_op jit(solution)/shard_map/pallas_call | solution.py:725
  21.0 5.0 %all-to-all-start = ((f32[16,152,128]{2,1,0:T(8,128)}), f32[16,152,128]{2,1,0:T(8,128)}, u32[]{:S(2)}, u32[]{:S(2)}) async-start(f32[16,152,128]{2,1,0:T(8,128)} %shard_map.160), calls=%async_computation | async-start | bytes 2490368 | tf_op jit(solution)/shard_map/all_to_all | solution.py:750
  26.0 14.2 %shard_map.159 = (f32[1200,128]{1,0:T(8,128)}, f32[24,10,2,640]{3,2,1,0:T(2,128)}, s32[128]{0:T(128)}) custom-call(s32[384]{0:T(512)} %plan_in.3, s32[24]{0:T(128)} %wet_in.3, s32[10,24]{1,0:T(8,128)} %bitcast.18, s32[24,192]{1,0:T(8,128)} %links_in.3, f32[24,192]{1,0:T(8,128)} %angle_in.3, f32[24,192]{1,0:T(8,128)} %scale_in.3, f32[24,4,64]{2,1,0:T(4,128)} %metric_in.3, ...), custom_call_target="tpu_custom_call" | custom-call | tf_op jit(solution)/shard_map/pallas_call | solution.py:725
  40.2 15.1 %all-to-all-done.got_in = f32[16,152,128]{2,1,0:T(8,128)} async-done(((f32[16,152,128]{2,1,0:T(8,128)}), f32[16,152,128]{2,1,0:T(8,128)}, u32[]{:S(2)}, u32[]{:S(2)}) %all-to-all-start) | async-done | bytes 1245216 | tf_op jit(solution)/shard_map/all_to_all | solution.py:750
  55.2 2.6 %shard_map.161 = (f32[10,3,5,8,128]{4,3,2,1,0:T(8,128)}, f32[24,10,2,640]{3,2,1,0:T(2,128)}) custom-call(s32[128]{0:T(128)} %get-tuple-element.15.origin_in, f32[16,152,128]{2,1,0:T(8,128)} %all-to-all-done.got_in, f32[10,3,5,8,128]{4,3,2,1,0:T(8,128)} %bitcast.14, ...), custom_call_target="tpu_custom_call", output_to_operand_aliasing={{0}: (2, {}), {1}: (3, {})} | custom-call | tf_op jit(solution)/shard_map/pallas_call | solution.py:758
Async XLA Ops:
  6.4 3.8 %collective-permute-start = (f32[64,128]{1,0:T(8,128)}, f32[64,128]{1,0:T(8,128)}, u32[]{:S(2)}, u32[]{:S(2)}) collective-permute-start(f32[64,128]{1,0:T(8,128)} %get-tuple-element.13), channel_id=1, source_target_pairs={{0,1},{1,0},{2,3},{3,2},{4,5},{5,4},{6,7},{7,6},{8,9},{9,8},{10,11... | collective-permute-start | bytes 98312 | tf_op jit(solution)/shard_map/ppermute | solution.py:708
  7.1 6.4 %collective-permute-start.1 = (f32[64,128]{1,0:T(8,128)}, f32[64,128]{1,0:T(8,128)}, u32[]{:S(2)}, u32[]{:S(2)}) collective-permute-start(f32[64,128]{1,0:T(8,128)} %get-tuple-element.14), channel_id=1, source_target_pairs={{1,2},{2,1},{3,4},{4,3},{5,6},{6,5},{7,8},{8,7},{9,10},{10,9},{11,... | collective-permute-start | bytes 98312 | tf_op jit(solution)/shard_map/ppermute | solution.py:707
  21.0 34.3 %all-to-all-start = ((f32[16,152,128]{2,1,0:T(8,128)}), f32[16,152,128]{2,1,0:T(8,128)}, u32[]{:S(2)}, u32[]{:S(2)}) async-start(f32[16,152,128]{2,1,0:T(8,128)} %shard_map.160), calls=%async_computation | async-start | bytes 2490368 | tf_op jit(solution)/shard_map/all_to_all | solution.py:750
